TPU v7x, 32 devices: a whole 2x2x4 slice. The times are simulated.
32 devices in a mesh: img: 2 (over y), gx: 4 (over z), gy: 4 (over x, core).
Axes of the slice: x: 2, y: 2, z: 4, core: 2. Of those that a mesh axis runs over, the one named last changes fastest.
Arguments:
- conc_old: float32 [128, 64, 128], P(('img', 'gx'), 'gy'), parts along dimension 0, may hold values from -1 to 1
- chem_old: float32 [128, 64, 128], P(('img', 'gx'), 'gy'), parts along dimension 0, may hold values from -4 to 4
Outputs:
- conc_new: float32 [128, 64, 128], P(('img', 'gx'), 'gy'), parts along dimension 0
- chem_new: float32 [128, 64, 128], P(('img', 'gx'), 'gy'), parts along dimension 0
There are 2 independent parts, one for each index of `img`. A program takes and returns all parts, laid end to end along the dimension named above; each array names one. Nothing has to cross between parts.
All inputs are finite; a program needn't handle non-finite values.
Results may differ from a plain program's by a relative error of at most 0.0001.
Values sent between devices are 32-bit elements; how exact they have to be, the bound alone decides.
No kernel may reach another device: no remote copies, remote signals or barrier semaphores. Data moves between devices by JAX's collectives and lax.ppermute only.
A program may use at most 128 MiB of HBM per device.

v0:
```python
import jax
import jax.numpy as jnp
from jax import lax
from jax.sharding import PartitionSpec as P

LEVELS = 4
SWEEPS = 2
COARSE = 6


TIME_STEP = 32.0
GRADIENT_ENERGY = 0.5
STABILIZER = 2.0
DAMPING = 0.7


def extended(cells, sides, width):
    for axis, dim in sides:
        count = lax.axis_size(axis)
        head = lax.slice_in_dim(cells, 0, width, axis=dim)
        tail = lax.slice_in_dim(cells, cells.shape[dim] - width, cells.shape[dim], axis=dim)
        cells = jnp.concatenate(
            [
                lax.ppermute(tail, axis, [(i, (i + 1) % count) for i in range(count)]),
                cells,
                lax.ppermute(head, axis, [((i + 1) % count, i) for i in range(count)]),
            ],
            axis=dim,
        )
    return cells


def mobility_of(concentration):
    return 0.1 + jnp.square(1.0 - concentration * concentration)


def right_of(concentration):
    return jnp.stack(
        [
            concentration,
            concentration * concentration * concentration - (1.0 + STABILIZER) * concentration,
        ]
    )


def face_weights(mob_padded, level_scale):
    middle = mob_padded[1:-1, 1:-1, :]
    half_scale = 0.5 * level_scale
    weights = (
        half_scale * (middle + mob_padded[2:, 1:-1, :]),
        half_scale * (middle + mob_padded[:-2, 1:-1, :]),
        half_scale * (middle + mob_padded[1:-1, 2:, :]),
        half_scale * (middle + mob_padded[1:-1, :-2, :]),
        half_scale * (middle + jnp.roll(middle, -1, axis=2)),
        half_scale * (middle + jnp.roll(middle, 1, axis=2)),
    )
    total_weight = weights[0] + weights[1] + weights[2] + weights[3] + weights[4] + weights[5]
    return (weights, total_weight)


def neighbour_list(padded, middle):
    return (
        padded[2:, 1:-1, :],
        padded[:-2, 1:-1, :],
        padded[1:-1, 2:, :],
        padded[1:-1, :-2, :],
        jnp.roll(middle, -1, axis=2),
        jnp.roll(middle, 1, axis=2),
    )


def apply_operator(padded, weights, level_scale):
    middle = padded[:, 1:-1, 1:-1, :]
    conc_near = neighbour_list(padded[0], middle[0])
    chem_near = neighbour_list(padded[1], middle[1])
    flux = weights[0] * (chem_near[0] - middle[1])
    for position in range(1, 6):
        flux = flux + weights[position] * (chem_near[position] - middle[1])
    laplace = (
        conc_near[0]
        + conc_near[1]
        + conc_near[2]
        + conc_near[3]
        + conc_near[4]
        + conc_near[5]
        - 6.0 * middle[0]
    )
    first_eq = middle[0] - TIME_STEP * flux
    second_eq = middle[1] - STABILIZER * middle[0] + GRADIENT_ENERGY * level_scale * laplace
    return jnp.stack([first_eq, second_eq])


def update(residual, total_weight, level_scale):
    diagonal = STABILIZER + 6.0 * GRADIENT_ENERGY * level_scale
    coupling = TIME_STEP * total_weight
    determinant = 1.0 + coupling * diagonal
    conc_step = (residual[0] - coupling * residual[1]) / determinant
    chem_step = (residual[1] + diagonal * residual[0]) / determinant
    return DAMPING * jnp.stack([conc_step, chem_step])


def sweep_once(padded, right_side, mob_padded, level_scale):
    weights, total_weight = face_weights(mob_padded, level_scale)
    residual = right_side - apply_operator(padded, weights, level_scale)
    return padded[:, 1:-1, 1:-1, :] + update(residual, total_weight, level_scale)


def defect(padded, right_side, mob_padded, level_scale):
    weights = face_weights(mob_padded, level_scale)[0]
    return right_side - apply_operator(padded, weights, level_scale)


def coarsen(values):
    dims_now = values.shape
    grouped = values.reshape(
        dims_now[:-3] + (dims_now[-3] // 2, 2, dims_now[-2] // 2, 2, dims_now[-1] // 2, 2)
    )
    return jnp.sum(grouped, axis=(-5, -3, -1)) * 0.125


def refine(values):
    for axis_pos in (-3, -2, -1):
        values = jnp.repeat(values, 2, axis=axis_pos)
    return values


def trim_rim(values, width):
    return values[..., width:-width, width:-width, :]


def field_rim(fields):
    return extended(fields, (("gx", 1), ("gy", 2)), 1)


def coarsest_solve(right_side, mobility, level_scale):
    mob_padded = extended(mobility, (("gx", 0), ("gy", 1)), 1)
    fields = update(right_side, face_weights(mob_padded, level_scale)[1], level_scale)
    for sweep_index in range(COARSE - 1):
        padded = extended(fields, (("gx", 1), ("gy", 2)), 1)
        fields = sweep_once(padded, right_side, mob_padded, level_scale)
    return fields


def plain_solve(start_fields):
    outer_fields = field_rim(start_fields)
    mob_outer = mobility_of(outer_fields[0])
    mobility = trim_rim(mob_outer, 1)
    level_data = []
    for level_index in range(LEVELS - 1):
        if level_index == 0:
            mob_padded = mob_outer
        else:
            mob_padded = extended(mobility, (("gx", 0), ("gy", 1)), 1)
        level_data.append((mob_padded, 0.25**level_index))
        mobility = coarsen(mobility)
    coarsest_scale = 0.25 ** (LEVELS - 1)

    def cycle_level(level_index, right_side):
        if level_index == LEVELS - 1:
            return coarsest_solve(right_side, mobility, coarsest_scale)
        mob_padded, level_scale = level_data[level_index]
        if level_index == 0:
            fields = sweep_once(outer_fields, right_side, mob_padded, level_scale)
        else:
            fields = update(right_side, face_weights(mob_padded, level_scale)[1], level_scale)
        fields = sweep_once(field_rim(fields), right_side, mob_padded, level_scale)
        residual = defect(field_rim(fields), right_side, mob_padded, level_scale)
        fields = fields + refine(cycle_level(level_index + 1, coarsen(residual)))
        for sweep_index in range(SWEEPS):
            fields = sweep_once(field_rim(fields), right_side, mob_padded, level_scale)
        return fields

    return cycle_level(0, right_of(start_fields[0]))


def body(conc_old, chem_old):
    start_fields = jnp.stack([conc_old, chem_old])
    result = plain_solve(start_fields)
    return (result[0], result[1])


def solution(mesh):
    in_specs = (P(("img", "gx"), "gy", None), P(("img", "gx"), "gy", None))
    out_specs = (P(("img", "gx"), "gy", None), P(("img", "gx"), "gy", None))
    return jax.shard_map(body, mesh=mesh, in_specs=in_specs, out_specs=out_specs, check_vma=False)
```

profile of v0, /device:TPU:0, one launch (start us, length us, event | category | flops | bytes accessed | tf_op | source)
XLA Modules:
  0.0 302.8 jit_solution(2621444720984587918)
XLA Ops:
  1.4 3.0 collective-permute-start
  4.5 2.1 collective-permute-start.1
  10.8 1.8 collective-permute-start.3
  12.7 9.8 %stack.362 = f32[1,8,2,8,2,64,2]{6,5,4,3,2,1,0:T(8,128)} reshape(f32[16,16,128]{2,1,0:T(8,128)S(1)} %copy-done) | data formatting | bytes 262144 | tf_op jit(solution)/shard_map/stack | solution.py:38
  22.5 6.1 %copy.413 = f32[1,8,2,8,2,64,2]{5,3,6,4,2,1,0:T(8,128)} copy(f32[1,8,2,8,2,64,2]{6,5,4,3,2,1,0:T(8,128)} %stack.362) | data formatting | bytes 262144 | tf_op jit(solution)/shard_map/stack | solution.py:38
  31.5 9.8 %reshape.67 = f32[8,2,8,2,64,2]{5,4,3,2,1,0:T(8,128)} reshape(f32[16,16,128]{2,1,0:T(8,128)S(1)} %slice.2437) | data formatting | bytes 262144 | tf_op jit(solution)/shard_map/reshape | solution.py:115
  41.3 4.0 %reduce_sum.55 = f32[8,8,64]{2,1,0:T(8,128)S(1)} reduce(f32[8,2,8,2,64,2]{5,4,3,2,1,0:T(8,128)} %reshape.67, f32[]{:T(128)} %constant.30.clone.1), dimensions={1,3,5}, to_apply=%region_1.0 | reduce | flops 28672 | bytes 147460 | tf_op jit(solution)/shard_map/reduce_sum | solution.py:118
  51.0 3.8 %collective-permute-start.5 = (f32[2,1,16,128]{3,2,1,0:T(8,128)S(1)}, f32[2,1,16,128]{3,2,1,0:T(8,128)S(1)}, u32[]{:S(2)}, u32[]{:S(2)}) collective-permute-start(f32[2,1,16,128]{3,2,1,0:T(8,128)S(1)} %get-tuple-element.80), channel_id=1, source_target_pairs={{4,0},{8,4},{12,8},{0,12},{5,1},{9,5},{13,9},{1,13},{6,2},{10,6},{... | collective-permute-start | bytes 49160 | tf_op jit(solution)/shard_map/ppermute | solution.py:26
  54.8 9.8 %stack.363 = f32[1,8,2,8,2,64,2]{6,5,4,3,2,1,0:T(8,128)} reshape(f32[16,16,128]{2,1,0:T(8,128)S(1)} %get-tuple-element.119) | data formatting | bytes 262144 | tf_op jit(solution)/shard_map/stack | solution.py:38
  64.6 6.0 %copy.414 = f32[1,8,2,8,2,64,2]{5,3,6,4,2,1,0:T(8,128)} copy(f32[1,8,2,8,2,64,2]{6,5,4,3,2,1,0:T(8,128)} %stack.363) | data formatting | bytes 262144 | tf_op jit(solution)/shard_map/stack | solution.py:38
  71.4 1.8 collective-permute-start.37
  74.7 2.0 collective-permute-start.24
  79.9 2.2 collective-permute-done.25
  84.7 1.7 collective-permute-start.7
  89.0 3.8 %collective-permute-start.9 = (f32[2,1,16,128]{3,2,1,0:T(8,128)S(1)}, f32[2,1,16,128]{3,2,1,0:T(8,128)S(1)}, u32[]{:S(2)}, u32[]{:S(2)}) collective-permute-start(f32[2,1,16,128]{3,2,1,0:T(8,128)S(1)} %get-tuple-element.76), channel_id=1, source_target_pairs={{4,0},{8,4},{12,8},{0,12},{5,1},{9,5},{13,9},{1,13},{6,2},{10,6},{... | collective-permute-start | bytes 49160 | tf_op jit(solution)/shard_map/ppermute | solution.py:26
  97.9 1.7 collective-permute-start.15
  99.9 9.8 %stack.365 = f32[1,8,2,8,2,64,2]{6,5,4,3,2,1,0:T(8,128)} reshape(f32[16,16,128]{2,1,0:T(8,128)S(1)} %fusion.54) | data formatting | bytes 262144 | tf_op jit(solution)/shard_map/stack | solution.py:90
  109.7 5.5 %copy.419 = f32[1,8,2,8,2,64,2]{5,3,6,4,2,1,0:T(8,128)S(1)} copy(f32[1,8,2,8,2,64,2]{6,5,4,3,2,1,0:T(8,128)} %stack.365) | data formatting | bytes 262144 | tf_op jit(solution)/shard_map/stack | solution.py:90
  115.3 9.8 %stack.366 = f32[1,8,2,8,2,64,2]{6,5,4,3,2,1,0:T(8,128)} reshape(f32[16,16,128]{2,1,0:T(8,128)S(1)} %fusion.48) | data formatting | bytes 262144 | tf_op jit(solution)/shard_map/stack | solution.py:90
  125.2 5.5 %copy.420 = f32[1,8,2,8,2,64,2]{5,3,6,4,2,1,0:T(8,128)S(1)} copy(f32[1,8,2,8,2,64,2]{6,5,4,3,2,1,0:T(8,128)} %stack.366) | data formatting | bytes 262144 | tf_op jit(solution)/shard_map/stack | solution.py:90
  133.7 3.8 %collective-permute-start.17 = (f32[2,1,8,64]{3,2,1,0:T(8,128)S(1)}, f32[2,1,8,64]{3,2,1,0:T(8,128)S(1)}, u32[]{:S(2)}, u32[]{:S(2)}) collective-permute-start(f32[2,1,8,64]{3,2,1,0:T(8,128)S(1)} %get-tuple-element.173), channel_id=1, source_target_pairs={{4,0},{8,4},{12,8},{0,12},{5,1},{9,5},{13,9},{1,13},{6,2},{10,6},{... | collective-permute-start | bytes 12296 | tf_op jit(solution)/shard_map/ppermute | solution.py:26
  140.4 1.7 collective-permute-start.19
  142.8 3.0 mul.1078
  153.0 2.8 collective-permute-start.21
  157.5 1.7 collective-permute-start.23
  162.0 2.8 stack.377
  164.8 1.7 fusion.155
  166.5 2.8 stack.378
  169.4 2.0 fusion
  173.9 2.6 collective-permute-start.29
  183.5 2.6 collective-permute-start.33
  194.4 2.6 collective-permute-start.41
  203.4 2.6 collective-permute-start.45
  207.7 1.6 collective-permute-start.47
  212.4 2.6 collective-permute-start.49
  221.6 2.6 collective-permute-start.53
  230.6 2.6 collective-permute-start.57
  239.9 2.6 collective-permute-start.61
  249.0 2.6 collective-permute-start.65
  259.4 2.6 collective-permute-start.69
  268.7 2.6 collective-permute-start.73
  273.1 1.7 collective-permute-start.75
  283.7 2.6 collective-permute-start.77
  286.4 1.7 collective-permute-done.76
  288.4 1.7 collective-permute-start.79
  293.5 2.7 collective-permute-start.81
  296.4 1.7 collective-permute-done.80
  298.2 1.8 collective-permute-start.83
  (624 shorter events, 133.1 us)
Async XLA Ops:
  1.4 8.3 %collective-permute-start = (f32[2,1,16,128]{3,2,1,0:T(8,128)S(1)}, f32[2,1,16,128]{3,2,1,0:T(8,128)S(1)}, u32[]{:S(2)}, u32[]{:S(2)}) collective-permute-start(f32[2,1,16,128]{3,2,1,0:T(8,128)S(1)} %get-tuple-element.81), channel_id=1, source_target_pairs={{0,4},{4,8},{8,12},{12,0},{1,5},{5,9},{9,13},{13,1},{2,6},{6,10},{... | collective-permute-start | bytes 49160 | tf_op jit(solution)/shard_map/ppermute | solution.py:24
  4.5 5.3 %collective-permute-start.1 = (f32[2,1,16,128]{3,2,1,0:T(8,128)S(1)}, f32[2,1,16,128]{3,2,1,0:T(8,128)S(1)}, u32[]{:S(2)}, u32[]{:S(2)}) collective-permute-start(f32[2,1,16,128]{3,2,1,0:T(8,128)S(1)} %get-tuple-element.82), channel_id=1, source_target_pairs={{4,0},{8,4},{12,8},{0,12},{5,1},{9,5},{13,9},{1,13},{6,2},{10,6},{... | collective-permute-start | bytes 49160 | tf_op jit(solution)/shard_map/ppermute | solution.py:26
  10.8 17.8 %collective-permute-start.2 = (f32[2,18,1,128]{3,0,2,1:T(2,128)S(1)}, f32[2,18,1,128]{3,0,2,1:T(2,128)S(1)}, u32[]{:S(2)}, u32[]{:S(2)}) collective-permute-start(f32[2,18,1,128]{3,0,2,1:T(2,128)S(1)} %copy.455), channel_id=1, source_target_pairs={{0,1},{1,2},{2,3},{3,0},{4,5},{5,6},{6,7},{7,4},{8,9},{9,10},{10,1... | collective-permute-start | bytes 55304 | tf_op jit(solution)/shard_map/ppermute | solution.py:24
  10.8 17.8 %collective-permute-start.3 = (f32[2,18,1,128]{3,0,2,1:T(2,128)S(1)}, f32[2,18,1,128]{3,0,2,1:T(2,128)S(1)}, u32[]{:S(2)}, u32[]{:S(2)}) collective-permute-start(f32[2,18,1,128]{3,0,2,1:T(2,128)S(1)} %copy.456), channel_id=1, source_target_pairs={{1,0},{2,1},{3,2},{0,3},{5,4},{6,5},{7,6},{4,7},{9,8},{10,9},{11,1... | collective-permute-start | bytes 55304 | tf_op jit(solution)/shard_map/ppermute | solution.py:26
  51.0 31.8 %collective-permute-start.4 = (f32[2,1,16,128]{3,2,1,0:T(8,128)S(1)}, f32[2,1,16,128]{3,2,1,0:T(8,128)S(1)}, u32[]{:S(2)}, u32[]{:S(2)}) collective-permute-start(f32[2,1,16,128]{3,2,1,0:T(8,128)S(1)} %get-tuple-element.79), channel_id=1, source_target_pairs={{0,4},{4,8},{8,12},{12,0},{1,5},{5,9},{9,13},{13,1},{2,6},{6,10},{... | collective-permute-start | bytes 49160 | tf_op jit(solution)/shard_map/ppermute | solution.py:24
  51.0 32.3 %collective-permute-start.5 = (f32[2,1,16,128]{3,2,1,0:T(8,128)S(1)}, f32[2,1,16,128]{3,2,1,0:T(8,128)S(1)}, u32[]{:S(2)}, u32[]{:S(2)}) collective-permute-start(f32[2,1,16,128]{3,2,1,0:T(8,128)S(1)} %get-tuple-element.80), channel_id=1, source_target_pairs={{4,0},{8,4},{12,8},{0,12},{5,1},{9,5},{13,9},{1,13},{6,2},{10,6},{... | collective-permute-start | bytes 49160 | tf_op jit(solution)/shard_map/ppermute | solution.py:26
  70.6 14.0 %collective-permute-start.12 = (f32[1,8,64]{2,1,0:T(8,128)S(1)}, f32[1,8,64]{2,1,0:T(8,128)S(1)}, u32[]{:S(2)}, u32[]{:S(2)}) collective-permute-start(f32[1,8,64]{2,1,0:T(8,128)S(1)} %get-tuple-element.221), channel_id=1, source_target_pairs={{4,0},{8,4},{12,8},{0,12},{5,1},{9,5},{13,9},{1,13},{6,2},{10,6},{... | collective-permute-start | bytes 6152 | tf_op jit(solution)/shard_map/ppermute | solution.py:26
  71.4 5.4 %collective-permute-start.37 = (f32[1,2,16]{2,1,0:T(2,128)S(1)}, f32[1,2,16]{2,1,0:T(2,128)S(1)}, u32[]{:S(2)}, u32[]{:S(2)}) collective-permute-start(f32[1,2,16]{2,1,0:T(2,128)S(1)} %get-tuple-element.389), channel_id=1, source_target_pairs={{0,4},{4,8},{8,12},{12,0},{1,5},{5,9},{9,13},{13,1},{2,6},{6,10},{... | collective-permute-start | bytes 392 | tf_op jit(solution)/shard_map/ppermute | solution.py:24
  76.7 5.4 %collective-permute-start.25 = (f32[1,4,32]{2,1,0:T(4,128)S(1)}, f32[1,4,32]{2,1,0:T(4,128)S(1)}, u32[]{:S(2)}, u32[]{:S(2)}) collective-permute-start(f32[1,4,32]{2,1,0:T(4,128)S(1)} %get-tuple-element.311), channel_id=1, source_target_pairs={{0,4},{4,8},{8,12},{12,0},{1,5},{5,9},{9,13},{13,1},{2,6},{6,10},{... | collective-permute-start | bytes 1544 | tf_op jit(solution)/shard_map/ppermute | solution.py:24
  78.3 6.4 %collective-permute-start.13 = (f32[1,8,64]{2,1,0:T(8,128)S(1)}, f32[1,8,64]{2,1,0:T(8,128)S(1)}, u32[]{:S(2)}, u32[]{:S(2)}) collective-permute-start(f32[1,8,64]{2,1,0:T(8,128)S(1)} %get-tuple-element.220), channel_id=1, source_target_pairs={{0,4},{4,8},{8,12},{12,0},{1,5},{5,9},{9,13},{13,1},{2,6},{6,10},{... | collective-permute-start | bytes 6152 | tf_op jit(solution)/shard_map/ppermute | solution.py:24
  82.1 110.0 %collective-permute-start.38 = (f32[4,1,16]{2,1,0:T(1,128)}, f32[4,1,16]{2,1,0:T(1,128)}, u32[]{:S(2)}, u32[]{:S(2)}) collective-permute-start(f32[4,1,16]{2,1,0:T(1,128)} %get-tuple-element.343), channel_id=1, source_target_pairs={{1,0},{2,1},{3,2},{0,3},{5,4},{6,5},{7,6},{4,7},{9,8},{10,9},{11,1... | collective-permute-start | bytes 776 | tf_op jit(solution)/shard_map/ppermute | solution.py:26
  82.7 109.4 %collective-permute-start.39 = (f32[4,1,16]{2,1,0:T(1,128)}, f32[4,1,16]{2,1,0:T(1,128)}, u32[]{:S(2)}, u32[]{:S(2)}) collective-permute-start(f32[4,1,16]{2,1,0:T(1,128)} %get-tuple-element.342), channel_id=1, source_target_pairs={{0,1},{1,2},{2,3},{3,0},{4,5},{5,6},{6,7},{7,4},{8,9},{9,10},{10,1... | collective-permute-start | bytes 776 | tf_op jit(solution)/shard_map/ppermute | solution.py:24
  83.2 88.2 %collective-permute-start.26 = (f32[6,1,32]{2,1,0:T(1,128)}, f32[6,1,32]{2,1,0:T(1,128)}, u32[]{:S(2)}, u32[]{:S(2)}) collective-permute-start(f32[6,1,32]{2,1,0:T(1,128)} %get-tuple-element.263), channel_id=1, source_target_pairs={{1,0},{2,1},{3,2},{0,3},{5,4},{6,5},{7,6},{4,7},{9,8},{10,9},{11,1... | collective-permute-start | bytes 2312 | tf_op jit(solution)/shard_map/ppermute | solution.py:26
  88.9 5.6 %collective-permute-start.8 = (f32[2,1,16,128]{3,2,1,0:T(8,128)S(1)}, f32[2,1,16,128]{3,2,1,0:T(8,128)S(1)}, u32[]{:S(2)}, u32[]{:S(2)}) collective-permute-start(f32[2,1,16,128]{3,2,1,0:T(8,128)S(1)} %get-tuple-element.75), channel_id=1, source_target_pairs={{0,4},{4,8},{8,12},{12,0},{1,5},{5,9},{9,13},{13,1},{2,6},{6,10},{... | collective-permute-start | bytes 49160 | tf_op jit(solution)/shard_map/ppermute | solution.py:24
  89.0 5.5 %collective-permute-start.9 = (f32[2,1,16,128]{3,2,1,0:T(8,128)S(1)}, f32[2,1,16,128]{3,2,1,0:T(8,128)S(1)}, u32[]{:S(2)}, u32[]{:S(2)}) collective-permute-start(f32[2,1,16,128]{3,2,1,0:T(8,128)S(1)} %get-tuple-element.76), channel_id=1, source_target_pairs={{4,0},{8,4},{12,8},{0,12},{5,1},{9,5},{13,9},{1,13},{6,2},{10,6},{... | collective-permute-start | bytes 49160 | tf_op jit(solution)/shard_map/ppermute | solution.py:26
  97.8 33.0 %collective-permute-start.14 = (f32[10,1,64]{2,1,0:T(1,128)}, f32[10,1,64]{2,1,0:T(1,128)S(1)}, u32[]{:S(2)}, u32[]{:S(2)}) collective-permute-start(f32[10,1,64]{2,1,0:T(1,128)} %get-tuple-element.182), channel_id=1, source_target_pairs={{1,0},{2,1},{3,2},{0,3},{5,4},{6,5},{7,6},{4,7},{9,8},{10,9},{11,1... | collective-permute-start | bytes 7688 | tf_op jit(solution)/shard_map/ppermute | solution.py:26
  97.9 32.9 %collective-permute-start.15 = (f32[10,1,64]{2,1,0:T(1,128)}, f32[10,1,64]{2,1,0:T(1,128)S(1)}, u32[]{:S(2)}, u32[]{:S(2)}) collective-permute-start(f32[10,1,64]{2,1,0:T(1,128)} %get-tuple-element.183), channel_id=1, source_target_pairs={{0,1},{1,2},{2,3},{3,0},{4,5},{5,6},{6,7},{7,4},{8,9},{9,10},{10,1... | collective-permute-start | bytes 7688 | tf_op jit(solution)/shard_map/ppermute | solution.py:24
  133.7 5.5 %collective-permute-start.16 = (f32[2,1,8,64]{3,2,1,0:T(8,128)S(1)}, f32[2,1,8,64]{3,2,1,0:T(8,128)S(1)}, u32[]{:S(2)}, u32[]{:S(2)}) collective-permute-start(f32[2,1,8,64]{3,2,1,0:T(8,128)S(1)} %get-tuple-element.172), channel_id=1, source_target_pairs={{0,4},{4,8},{8,12},{12,0},{1,5},{5,9},{9,13},{13,1},{2,6},{6,10},{... | collective-permute-start | bytes 12296 | tf_op jit(solution)/shard_map/ppermute | solution.py:24
  133.7 5.5 %collective-permute-start.17 = (f32[2,1,8,64]{3,2,1,0:T(8,128)S(1)}, f32[2,1,8,64]{3,2,1,0:T(8,128)S(1)}, u32[]{:S(2)}, u32[]{:S(2)}) collective-permute-start(f32[2,1,8,64]{3,2,1,0:T(8,128)S(1)} %get-tuple-element.173), channel_id=1, source_target_pairs={{4,0},{8,4},{12,8},{0,12},{5,1},{9,5},{13,9},{1,13},{6,2},{10,6},{... | collective-permute-start | bytes 12296 | tf_op jit(solution)/shard_map/ppermute | solution.py:26
  139.8 6.1 %collective-permute-start.18 = (f32[2,10,1,64]{3,0,2,1:T(2,128)}, f32[2,10,1,64]{3,0,2,1:T(2,128)}, u32[]{:S(2)}, u32[]{:S(2)}) collective-permute-start(f32[2,10,1,64]{3,0,2,1:T(2,128)} %copy.457), channel_id=1, source_target_pairs={{0,1},{1,2},{2,3},{3,0},{4,5},{5,6},{6,7},{7,4},{8,9},{9,10},{10,1... | collective-permute-start | bytes 15368 | tf_op jit(solution)/shard_map/ppermute | solution.py:24
  140.4 6.2 %collective-permute-start.19 = (f32[2,10,1,64]{3,0,2,1:T(2,128)}, f32[2,10,1,64]{3,0,2,1:T(2,128)}, u32[]{:S(2)}, u32[]{:S(2)}) collective-permute-start(f32[2,10,1,64]{3,0,2,1:T(2,128)} %copy.458), channel_id=1, source_target_pairs={{1,0},{2,1},{3,2},{0,3},{5,4},{6,5},{7,6},{4,7},{9,8},{10,9},{11,1... | collective-permute-start | bytes 15368 | tf_op jit(solution)/shard_map/ppermute | solution.py:26
  151.9 5.5 %collective-permute-start.20 = (f32[2,1,8,64]{3,2,1,0:T(8,128)S(1)}, f32[2,1,8,64]{3,2,1,0:T(8,128)S(1)}, u32[]{:S(2)}, u32[]{:S(2)}) collective-permute-start(f32[2,1,8,64]{3,2,1,0:T(8,128)S(1)} %get-tuple-element.168), channel_id=1, source_target_pairs={{0,4},{4,8},{8,12},{12,0},{1,5},{5,9},{9,13},{13,1},{2,6},{6,10},{... | collective-permute-start | bytes 12296 | tf_op jit(solution)/shard_map/ppermute | solution.py:24
  153.0 4.3 %collective-permute-start.21 = (f32[2,1,8,64]{3,2,1,0:T(8,128)S(1)}, f32[2,1,8,64]{3,2,1,0:T(8,128)S(1)}, u32[]{:S(2)}, u32[]{:S(2)}) collective-permute-start(f32[2,1,8,64]{3,2,1,0:T(8,128)S(1)} %get-tuple-element.169), channel_id=1, source_target_pairs={{4,0},{8,4},{12,8},{0,12},{5,1},{9,5},{13,9},{1,13},{6,2},{10,6},{... | collective-permute-start | bytes 12296 | tf_op jit(solution)/shard_map/ppermute | solution.py:26
  160.5 10.9 %collective-permute-start.27 = (f32[6,1,32]{2,1,0:T(1,128)}, f32[6,1,32]{2,1,0:T(1,128)}, u32[]{:S(2)}, u32[]{:S(2)}) collective-permute-start(f32[6,1,32]{2,1,0:T(1,128)} %get-tuple-element.262), channel_id=1, source_target_pairs={{0,1},{1,2},{2,3},{3,0},{4,5},{5,6},{6,7},{7,4},{8,9},{9,10},{10,1... | collective-permute-start | bytes 2312 | tf_op jit(solution)/shard_map/ppermute | solution.py:24
  172.5 5.5 %collective-permute-start.28 = (f32[2,1,4,32]{3,2,1,0:T(4,128)S(1)}, f32[2,1,4,32]{3,2,1,0:T(4,128)S(1)}, u32[]{:S(2)}, u32[]{:S(2)}) collective-permute-start(f32[2,1,4,32]{3,2,1,0:T(4,128)S(1)} %get-tuple-element.260), channel_id=1, source_target_pairs={{0,4},{4,8},{8,12},{12,0},{1,5},{5,9},{9,13},{13,1},{2,6},{6,10},{... | collective-permute-start | bytes 3080 | tf_op jit(solution)/shard_map/ppermute | solution.py:24
  173.9 4.1 %collective-permute-start.29 = (f32[2,1,4,32]{3,2,1,0:T(4,128)S(1)}, f32[2,1,4,32]{3,2,1,0:T(4,128)S(1)}, u32[]{:S(2)}, u32[]{:S(2)}) collective-permute-start(f32[2,1,4,32]{3,2,1,0:T(4,128)S(1)} %get-tuple-element.261), channel_id=1, source_target_pairs={{4,0},{8,4},{12,8},{0,12},{5,1},{9,5},{13,9},{1,13},{6,2},{10,6},{... | collective-permute-start | bytes 3080 | tf_op jit(solution)/shard_map/ppermute | solution.py:26
  182.2 5.5 %collective-permute-start.32 = (f32[2,1,4,32]{3,2,1,0:T(4,128)S(1)}, f32[2,1,4,32]{3,2,1,0:T(4,128)S(1)}, u32[]{:S(2)}, u32[]{:S(2)}) collective-permute-start(f32[2,1,4,32]{3,2,1,0:T(4,128)S(1)} %get-tuple-element.256), channel_id=1, source_target_pairs={{0,4},{4,8},{8,12},{12,0},{1,5},{5,9},{9,13},{13,1},{2,6},{6,10},{... | collective-permute-start | bytes 3080 | tf_op jit(solution)/shard_map/ppermute | solution.py:24
  183.5 4.2 %collective-permute-start.33 = (f32[2,1,4,32]{3,2,1,0:T(4,128)S(1)}, f32[2,1,4,32]{3,2,1,0:T(4,128)S(1)}, u32[]{:S(2)}, u32[]{:S(2)}) collective-permute-start(f32[2,1,4,32]{3,2,1,0:T(4,128)S(1)} %get-tuple-element.257), channel_id=1, source_target_pairs={{4,0},{8,4},{12,8},{0,12},{5,1},{9,5},{13,9},{1,13},{6,2},{10,6},{... | collective-permute-start | bytes 3080 | tf_op jit(solution)/shard_map/ppermute | solution.py:26
  193.1 5.4 %collective-permute-start.40 = (f32[2,1,2,16]{3,2,1,0:T(2,128)S(1)}, f32[2,1,2,16]{3,2,1,0:T(2,128)S(1)}, u32[]{:S(2)}, u32[]{:S(2)}) collective-permute-start(f32[2,1,2,16]{3,2,1,0:T(2,128)S(1)} %get-tuple-element.340), channel_id=1, source_target_pairs={{0,4},{4,8},{8,12},{12,0},{1,5},{5,9},{9,13},{13,1},{2,6},{6,10},{... | collective-permute-start | bytes 776 | tf_op jit(solution)/shard_map/ppermute | solution.py:24
  194.4 4.1 %collective-permute-start.41 = (f32[2,1,2,16]{3,2,1,0:T(2,128)S(1)}, f32[2,1,2,16]{3,2,1,0:T(2,128)S(1)}, u32[]{:S(2)}, u32[]{:S(2)}) collective-permute-start(f32[2,1,2,16]{3,2,1,0:T(2,128)S(1)} %get-tuple-element.341), channel_id=1, source_target_pairs={{4,0},{8,4},{12,8},{0,12},{5,1},{9,5},{13,9},{1,13},{6,2},{10,6},{... | collective-permute-start | bytes 776 | tf_op jit(solution)/shard_map/ppermute | solution.py:26
  202.1 5.4 %collective-permute-start.44 = (f32[2,1,2,16]{3,2,1,0:T(2,128)S(1)}, f32[2,1,2,16]{3,2,1,0:T(2,128)S(1)}, u32[]{:S(2)}, u32[]{:S(2)}) collective-permute-start(f32[2,1,2,16]{3,2,1,0:T(2,128)S(1)} %get-tuple-element.336), channel_id=1, source_target_pairs={{0,4},{4,8},{8,12},{12,0},{1,5},{5,9},{9,13},{13,1},{2,6},{6,10},{... | collective-permute-start | bytes 776 | tf_op jit(solution)/shard_map/ppermute | solution.py:24
  203.4 4.1 %collective-permute-start.45 = (f32[2,1,2,16]{3,2,1,0:T(2,128)S(1)}, f32[2,1,2,16]{3,2,1,0:T(2,128)S(1)}, u32[]{:S(2)}, u32[]{:S(2)}) collective-permute-start(f32[2,1,2,16]{3,2,1,0:T(2,128)S(1)} %get-tuple-element.337), channel_id=1, source_target_pairs={{4,0},{8,4},{12,8},{0,12},{5,1},{9,5},{13,9},{1,13},{6,2},{10,6},{... | collective-permute-start | bytes 776 | tf_op jit(solution)/shard_map/ppermute | solution.py:26
  211.1 5.4 %collective-permute-start.48 = (f32[2,1,2,16]{3,2,1,0:T(2,128)S(1)}, f32[2,1,2,16]{3,2,1,0:T(2,128)S(1)}, u32[]{:S(2)}, u32[]{:S(2)}) collective-permute-start(f32[2,1,2,16]{3,2,1,0:T(2,128)S(1)} %get-tuple-element.332), channel_id=1, source_target_pairs={{0,4},{4,8},{8,12},{12,0},{1,5},{5,9},{9,13},{13,1},{2,6},{6,10},{... | collective-permute-start | bytes 776 | tf_op jit(solution)/shard_map/ppermute | solution.py:24
  212.4 4.1 %collective-permute-start.49 = (f32[2,1,2,16]{3,2,1,0:T(2,128)S(1)}, f32[2,1,2,16]{3,2,1,0:T(2,128)S(1)}, u32[]{:S(2)}, u32[]{:S(2)}) collective-permute-start(f32[2,1,2,16]{3,2,1,0:T(2,128)S(1)} %get-tuple-element.333), channel_id=1, source_target_pairs={{4,0},{8,4},{12,8},{0,12},{5,1},{9,5},{13,9},{1,13},{6,2},{10,6},{... | collective-permute-start | bytes 776 | tf_op jit(solution)/shard_map/ppermute | solution.py:26
  220.3 5.4 %collective-permute-start.52 = (f32[2,1,2,16]{3,2,1,0:T(2,128)S(1)}, f32[2,1,2,16]{3,2,1,0:T(2,128)S(1)}, u32[]{:S(2)}, u32[]{:S(2)}) collective-permute-start(f32[2,1,2,16]{3,2,1,0:T(2,128)S(1)} %get-tuple-element.328), channel_id=1, source_target_pairs={{0,4},{4,8},{8,12},{12,0},{1,5},{5,9},{9,13},{13,1},{2,6},{6,10},{... | collective-permute-start | bytes 776 | tf_op jit(solution)/shard_map/ppermute | solution.py:24
  229.3 5.4 %collective-permute-start.56 = (f32[2,1,2,16]{3,2,1,0:T(2,128)S(1)}, f32[2,1,2,16]{3,2,1,0:T(2,128)S(1)}, u32[]{:S(2)}, u32[]{:S(2)}) collective-permute-start(f32[2,1,2,16]{3,2,1,0:T(2,128)S(1)} %get-tuple-element.324), channel_id=1, source_target_pairs={{0,4},{4,8},{8,12},{12,0},{1,5},{5,9},{9,13},{13,1},{2,6},{6,10},{... | collective-permute-start | bytes 776 | tf_op jit(solution)/shard_map/ppermute | solution.py:24
  238.6 5.5 %collective-permute-start.60 = (f32[2,1,4,32]{3,2,1,0:T(4,128)S(1)}, f32[2,1,4,32]{3,2,1,0:T(4,128)S(1)}, u32[]{:S(2)}, u32[]{:S(2)}) collective-permute-start(f32[2,1,4,32]{3,2,1,0:T(4,128)S(1)} %get-tuple-element.242), channel_id=1, source_target_pairs={{0,4},{4,8},{8,12},{12,0},{1,5},{5,9},{9,13},{13,1},{2,6},{6,10},{... | collective-permute-start | bytes 3080 | tf_op jit(solution)/shard_map/ppermute | solution.py:24
  239.9 4.2 %collective-permute-start.61 = (f32[2,1,4,32]{3,2,1,0:T(4,128)S(1)}, f32[2,1,4,32]{3,2,1,0:T(4,128)S(1)}, u32[]{:S(2)}, u32[]{:S(2)}) collective-permute-start(f32[2,1,4,32]{3,2,1,0:T(4,128)S(1)} %get-tuple-element.243), channel_id=1, source_target_pairs={{4,0},{8,4},{12,8},{0,12},{5,1},{9,5},{13,9},{1,13},{6,2},{10,6},{... | collective-permute-start | bytes 3080 | tf_op jit(solution)/shard_map/ppermute | solution.py:26
  247.7 5.4 %collective-permute-start.64 = (f32[2,1,4,32]{3,2,1,0:T(4,128)S(1)}, f32[2,1,4,32]{3,2,1,0:T(4,128)S(1)}, u32[]{:S(2)}, u32[]{:S(2)}) collective-permute-start(f32[2,1,4,32]{3,2,1,0:T(4,128)S(1)} %get-tuple-element.238), channel_id=1, source_target_pairs={{0,4},{4,8},{8,12},{12,0},{1,5},{5,9},{9,13},{13,1},{2,6},{6,10},{... | collective-permute-start | bytes 3080 | tf_op jit(solution)/shard_map/ppermute | solution.py:24
  249.0 4.2 %collective-permute-start.65 = (f32[2,1,4,32]{3,2,1,0:T(4,128)S(1)}, f32[2,1,4,32]{3,2,1,0:T(4,128)S(1)}, u32[]{:S(2)}, u32[]{:S(2)}) collective-permute-start(f32[2,1,4,32]{3,2,1,0:T(4,128)S(1)} %get-tuple-element.239), channel_id=1, source_target_pairs={{4,0},{8,4},{12,8},{0,12},{5,1},{9,5},{13,9},{1,13},{6,2},{10,6},{... | collective-permute-start | bytes 3080 | tf_op jit(solution)/shard_map/ppermute | solution.py:26
  258.1 5.5 %collective-permute-start.68 = (f32[2,1,8,64]{3,2,1,0:T(8,128)S(1)}, f32[2,1,8,64]{3,2,1,0:T(8,128)S(1)}, u32[]{:S(2)}, u32[]{:S(2)}) collective-permute-start(f32[2,1,8,64]{3,2,1,0:T(8,128)S(1)} %get-tuple-element.164), channel_id=1, source_target_pairs={{0,4},{4,8},{8,12},{12,0},{1,5},{5,9},{9,13},{13,1},{2,6},{6,10},{... | collective-permute-start | bytes 12296 | tf_op jit(solution)/shard_map/ppermute | solution.py:24
  259.4 4.3 %collective-permute-start.69 = (f32[2,1,8,64]{3,2,1,0:T(8,128)S(1)}, f32[2,1,8,64]{3,2,1,0:T(8,128)S(1)}, u32[]{:S(2)}, u32[]{:S(2)}) collective-permute-start(f32[2,1,8,64]{3,2,1,0:T(8,128)S(1)} %get-tuple-element.165), channel_id=1, source_target_pairs={{4,0},{8,4},{12,8},{0,12},{5,1},{9,5},{13,9},{1,13},{6,2},{10,6},{... | collective-permute-start | bytes 12296 | tf_op jit(solution)/shard_map/ppermute | solution.py:26
  267.4 5.5 %collective-permute-start.72 = (f32[2,1,8,64]{3,2,1,0:T(8,128)S(1)}, f32[2,1,8,64]{3,2,1,0:T(8,128)S(1)}, u32[]{:S(2)}, u32[]{:S(2)}) collective-permute-start(f32[2,1,8,64]{3,2,1,0:T(8,128)S(1)} %get-tuple-element.160), channel_id=1, source_target_pairs={{0,4},{4,8},{8,12},{12,0},{1,5},{5,9},{9,13},{13,1},{2,6},{6,10},{... | collective-permute-start | bytes 12296 | tf_op jit(solution)/shard_map/ppermute | solution.py:24
  268.7 4.3 %collective-permute-start.73 = (f32[2,1,8,64]{3,2,1,0:T(8,128)S(1)}, f32[2,1,8,64]{3,2,1,0:T(8,128)S(1)}, u32[]{:S(2)}, u32[]{:S(2)}) collective-permute-start(f32[2,1,8,64]{3,2,1,0:T(8,128)S(1)} %get-tuple-element.161), channel_id=1, source_target_pairs={{4,0},{8,4},{12,8},{0,12},{5,1},{9,5},{13,9},{1,13},{6,2},{10,6},{... | collective-permute-start | bytes 12296 | tf_op jit(solution)/shard_map/ppermute | solution.py:26
  282.4 5.7 %collective-permute-start.76 = (f32[2,1,16,128]{3,2,1,0:T(8,128)S(1)}, f32[2,1,16,128]{3,2,1,0:T(8,128)S(1)}, u32[]{:S(2)}, u32[]{:S(2)}) collective-permute-start(f32[2,1,16,128]{3,2,1,0:T(8,128)S(1)} %get-tuple-element.71), channel_id=1, source_target_pairs={{0,4},{4,8},{8,12},{12,0},{1,5},{5,9},{9,13},{13,1},{2,6},{6,10},{... | collective-permute-start | bytes 49160 | tf_op jit(solution)/shard_map/ppermute | solution.py:24
  283.7 4.5 %collective-permute-start.77 = (f32[2,1,16,128]{3,2,1,0:T(8,128)S(1)}, f32[2,1,16,128]{3,2,1,0:T(8,128)S(1)}, u32[]{:S(2)}, u32[]{:S(2)}) collective-permute-start(f32[2,1,16,128]{3,2,1,0:T(8,128)S(1)} %get-tuple-element.72), channel_id=1, source_target_pairs={{4,0},{8,4},{12,8},{0,12},{5,1},{9,5},{13,9},{1,13},{6,2},{10,6},{... | collective-permute-start | bytes 49160 | tf_op jit(solution)/shard_map/ppermute | solution.py:26
  292.4 5.7 %collective-permute-start.80 = (f32[2,1,16,128]{3,2,1,0:T(8,128)S(1)}, f32[2,1,16,128]{3,2,1,0:T(8,128)S(1)}, u32[]{:S(2)}, u32[]{:S(2)}) collective-permute-start(f32[2,1,16,128]{3,2,1,0:T(8,128)S(1)} %get-tuple-element.67), channel_id=1, source_target_pairs={{0,4},{4,8},{8,12},{12,0},{1,5},{5,9},{9,13},{13,1},{2,6},{6,10},{... | collective-permute-start | bytes 49160 | tf_op jit(solution)/shard_map/ppermute | solution.py:24
  293.5 4.5 %collective-permute-start.81 = (f32[2,1,16,128]{3,2,1,0:T(8,128)S(1)}, f32[2,1,16,128]{3,2,1,0:T(8,128)S(1)}, u32[]{:S(2)}, u32[]{:S(2)}) collective-permute-start(f32[2,1,16,128]{3,2,1,0:T(8,128)S(1)} %get-tuple-element.68), channel_id=1, source_target_pairs={{4,0},{8,4},{12,8},{0,12},{5,1},{9,5},{13,9},{1,13},{6,2},{10,6},{... | collective-permute-start | bytes 49160 | tf_op jit(solution)/shard_map/ppermute | solution.py:26
  (109 other events, 1128.2 us)
where the time goes:
time: 304 us; the launch traced here: 303 us
  local copies, waits for them, and re-layouts  113 us (37%)
  starting transfers between devices  113 us (37%)
  waiting for transfers between devices  46.3 us (15%)
  other arithmetic  27.2 us (9%)
  between operations  3.25 us (1%)
    ppermute x42, starting transfers between devices, extended(): lax.ppermute(head, axis, [((i + 1) % count, i) for i in range(count)])  83.9 us
    ppermute x42, waiting for transfers between devices, extended(): lax.ppermute(tail, axis, [(i, (i + 1) % count) for i in range(count)])  43.1 us
    another operation x8, local copies, waits for them, and re-layouts, apply_operator(): return jnp.stack([first_eq, second_eq])  36.4 us
    another operation x4, local copies, waits for them, and re-layouts, right_of(): jnp.stack([concentration, concentration * concentration * concentration -...  31.7 us
    ppermute x42, starting transfers between devices, extended(): lax.ppermute(tail, axis, [(i, (i + 1) % count) for i in range(count)])  29.3 us
    slice x50, local copies, waits for them, and re-layouts, neighbour_list(): jnp.roll(middle, 1, axis=2)  13.5 us
    reshape x1, local copies, waits for them, and re-layouts, coarsen(): values.reshape(dims_now[:-3] + (dims_now[-3] // 2, 2, dims_now[-2] // 2,...  9.81 us
    reduce_sum x6, other arithmetic, coarsen(): return jnp.sum(grouped, axis=(-5, -3, -1)) * 0.125  6.47 us
  transfers between devices with their start and end apart: 84, of which 37 were waited for; matrix products, arithmetic and copies ran while one was open for 33% of the time, Pallas kernels for 0%

commit v1 on v0

--- a/solution.py
+++ b/solution.py
@@ -1,6 +1,8 @@
 import jax
 import jax.numpy as jnp
 from jax import lax
+from jax.experimental import pallas as pl
+from jax.experimental.pallas import tpu as pltpu
 from jax.sharding import PartitionSpec as P
 
 LEVELS = 4
@@ -173,7 +175,466 @@
     return cycle_level(0, right_of(start_fields[0]))
 
 
+HALO = 4
+GRID_BYTES_MAX = 2 * 1024 * 1024
+
+
+def whole_block():
+    return pl.BlockSpec(memory_space=pltpu.VMEM)
+
+
+def lane_roll(values, shift):
+    return pltpu.roll(values, shift % values.shape[1], axis=1)
+
+
+def row_roll(values, shift):
+    return pltpu.roll(values, shift % values.shape[0], axis=0)
+
+
+def lane_bit(shape, dup):
+    return (lax.broadcasted_iota(jnp.int32, shape, 1) // dup) % 2 == 0
+
+
+def low_rows(shape):
+    return lax.broadcasted_iota(jnp.int32, shape, 0) < HALO
+
+
+def loop_rows(count, unroll, row_group):
+    steps, rest = divmod(count, unroll)
+    if steps == 1:
+        row_group(0, unroll)
+    elif steps > 1:
+
+        def step(index, carry):
+            row_group(index * unroll, unroll)
+            return carry
+
+        lax.fori_loop(0, steps, step, 0)
+    if rest:
+        row_group(steps * unroll, rest)
+
+
+def wrapped(row, count):
+    if isinstance(row, int):
+        return row % count
+    return lax.rem(row + count, count)
+
+
+class Level:
+    def __init__(self, level_index, weights):
+        self.scale = 0.25**level_index
+        self.dup = 2**level_index
+        self.diagonal = STABILIZER + 6.0 * GRADIENT_ENERGY * self.scale
+        self.face_x, self.face_y, self.face_z, self.coupling, self.gain = weights
+
+    def set_weights(self, mobility, start, count, unroll):
+        total = mobility.shape[0]
+        half = 0.5 * self.scale * TIME_STEP
+
+        def group(first, size):
+            rows = [mobility[wrapped(start + first + i - 1, total)] for i in range(size + 2)]
+            before = half * (rows[0] + rows[1])
+            for i in range(size):
+                at = wrapped(start + first + i, total)
+                here = rows[i + 1]
+                after = half * (here + rows[i + 2])
+                along_y = half * (here + row_roll(here, -1))
+                along_z = half * (here + lane_roll(here, -self.dup))
+                coupling = (
+                    before
+                    + after
+                    + along_y
+                    + row_roll(along_y, 1)
+                    + along_z
+                    + lane_roll(along_z, self.dup)
+                )
+                self.face_x[at] = after
+                self.face_y[at] = along_y
+                self.face_z[at] = along_z
+                self.coupling[at] = coupling
+                self.gain[at] = DAMPING / (1.0 + coupling * self.diagonal)
+                before = after
+
+        loop_rows(count, unroll, group)
+
+    def residuals(self, fields, right, start, first, size):
+        conc, chem = fields
+        total = conc.shape[0]
+        at = [wrapped(start + first + i - 1, total) for i in range(size + 2)]
+        u = [chem[r] for r in at]
+        c = [conc[r] for r in at]
+        before = self.face_x[at[0]] * (u[1] - u[0])
+        for i in range(1, size + 1):
+            r = at[i]
+            after = self.face_x[r] * (u[i + 1] - u[i])
+            along_y = self.face_y[r] * (row_roll(u[i], -1) - u[i])
+            along_z = self.face_z[r] * (lane_roll(u[i], -self.dup) - u[i])
+            flux = (after - before) + (along_y - row_roll(along_y, 1))
+            flux = flux + (along_z - lane_roll(along_z, self.dup))
+            near = (c[i - 1] + c[i + 1]) + (row_roll(c[i], 1) + row_roll(c[i], -1))
+            near = near + (lane_roll(c[i], self.dup) + lane_roll(c[i], -self.dup))
+            conc_left = right[0][r] - c[i] + flux
+            chem_left = (
+                right[1][r] - u[i] + self.diagonal * c[i] - (GRADIENT_ENERGY * self.scale) * near
+            )
+            before = after
+            yield r, c[i], u[i], conc_left, chem_left
+
+    def steps(self, row, conc_left, chem_left):
+        gain = self.gain[row]
+        return (
+            gain * (conc_left - self.coupling[row] * chem_left),
+            gain * (chem_left + self.diagonal * conc_left),
+        )
+
+    def first_sweep(self, right, out, unroll):
+        def group(first, size):
+            for i in range(size):
+                r = first + i
+                conc_step, chem_step = self.steps(r, right[0][r], right[1][r])
+                out[0][r] = conc_step
+                out[1][r] = chem_step
+
+        loop_rows(right[0].shape[0], unroll, group)
+
+    def sweep(self, fields, right, start, count, unroll, put):
+        def group(first, size):
+            for r, c, u, conc_left, chem_left in self.residuals(fields, right, start, first, size):
+                conc_step, chem_step = self.steps(r, conc_left, chem_left)
+                put(r, c + conc_step, u + chem_step)
+
+        loop_rows(count, unroll, group)
+
+    def coarse_right(self, fields, right, start, count, unroll, put):
+        def group(first, size):
+            lefts = [(a, b) for _, _, _, a, b in self.residuals(fields, right, start, first, size)]
+            for i in range(0, size, 2):
+                put(
+                    (first + i) // 2,
+                    lefts[i][0] + lefts[i + 1][0],
+                    lefts[i][1] + lefts[i + 1][1],
+                )
+
+        loop_rows(count, unroll, group)
+
+
+def put_in(conc, chem):
+    def put(row, conc_value, chem_value):
+        conc[row] = conc_value
+        chem[row] = chem_value
+
+    return put
+
+
+def pair_rows(ref, row, count):
+    return ref[row, pl.ds(0, count, stride=2), :] + ref[row, pl.ds(1, count, stride=2), :]
+
+
+def pair_lanes(values, dup):
+    swapped = jnp.where(
+        lane_bit(values.shape, dup), lane_roll(values, -dup), lane_roll(values, dup)
+    )
+    return values + swapped
+
+
+def edge_rows_kernel(conc, chem, low, high):
+    rows = conc.shape[0]
+    low[0] = conc[:HALO]
+    low[1] = chem[:HALO]
+    high[0] = conc[rows - HALO :]
+    high[1] = chem[rows - HALO :]
+
+
+def frame_row(row, rows, own, before, after):
+    if row < HALO:
+        return before[row]
+    if row < HALO + rows:
+        return own[row - HALO]
+    return after[row - HALO - rows]
+
+
+def edge_columns_kernel(conc, chem, before, after, to_left, to_right):
+    rows, columns = conc.shape[0], conc.shape[1]
+    for row in range(rows + 2 * HALO):
+        c = frame_row(row, rows, conc, before.at[0], after.at[0])
+        u = frame_row(row, rows, chem, before.at[1], after.at[1])
+        low = low_rows((8, c.shape[1]))
+        to_left[row] = jnp.where(low, c[:8], row_roll(u[:8], HALO))
+        to_right[row] = jnp.where(low, row_roll(u[columns - 8 :], HALO), c[columns - 8 :])
+
+
+def fine_down_kernel(
+    conc, chem, before, after, from_left, from_right,
+    packed, conc_out, chem_out, right_conc, right_chem,
+    face_x, face_y, face_z, coupling, gain,
+    chem_start, mobility, conc_mid, chem_mid, sums,
+):
+    rows, columns, lanes = conc.shape
+    frame = rows + 2 * HALO
+    low = low_rows((8, lanes))
+    for row in range(frame):
+        c = frame_row(row, rows, conc, before.at[0], after.at[0])
+        u = frame_row(row, rows, chem, before.at[1], after.at[1])
+        left, right = from_left[row], from_right[row]
+        c = jnp.concatenate([c, jnp.where(low, right, left)], axis=0)
+        u = jnp.concatenate([u, row_roll(jnp.where(low, left, right), HALO)], axis=0)
+        right_conc[row] = c
+        chem_start[row] = u
+        right_chem[row] = c * (c * c - (1.0 + STABILIZER))
+        gap = 1.0 - c * c
+        mobility[row] = 0.1 + gap * gap
+    level = Level(0, (face_x, face_y, face_z, coupling, gain))
+    level.set_weights(mobility, 0, frame, 2)
+    right_side = (right_conc, right_chem)
+    level.sweep(
+        (right_conc, chem_start), right_side, 1, frame - 2, 2, put_in(conc_mid, chem_mid)
+    )
+    level.sweep(
+        (conc_mid, chem_mid), right_side, 2, frame - 4, 2, put_in(conc_out, chem_out)
+    )
+
+    def keep(index, conc_sum, chem_sum):
+        sums[0, index] = conc_sum
+        sums[1, index] = chem_sum
+
+    level.coarse_right((conc_out, chem_out), right_side, HALO, rows, 2, keep)
+    for index in range(rows // 2):
+        sums[2, index] = mobility[HALO + 2 * index] + mobility[HALO + 2 * index + 1]
+    even = lane_bit((columns // 2, lanes), 1)
+    for field in range(3):
+        for index in range(rows // 4):
+            a = pair_rows(sums.at[field], 2 * index, columns // 2)
+            b = pair_rows(sums.at[field], 2 * index + 1, columns // 2)
+            packed[field, index] = 0.125 * jnp.where(
+                even, a + lane_roll(a, -1), b + lane_roll(b, 1)
+            )
+
+
+def spread_rows(ref, row, values):
+    count = values.shape[0]
+    ref[row, pl.ds(0, count, stride=2), :] = values
+    ref[row, pl.ds(1, count, stride=2), :] = values
+
+
+def coarse_kernel(
+    place, packed, conc_in, chem_in, right_conc, right_chem,
+    face_x, face_y, face_z, coupling, gain,
+    conc_new, chem_new,
+    *scratch,
+):
+    at_x, at_y = place[0], place[1]
+    scratch = list(scratch)
+    levels = []
+    for level_index in (1, 2, 3):
+        mobility, right0, right1, a0, a1, b0, b1 = scratch[:7]
+        level = Level(level_index, scratch[7:12])
+        levels.append((level, mobility, (right0, right1), (a0, a1), (b0, b1)))
+        del scratch[:12]
+    sums1, sums2, spread2, spread3, spread_fine, fine_a0, fine_a1, fine_b0, fine_b1 = scratch
+    one, mob1, right1, a1, b1 = levels[0]
+    two, mob2, right2, a2, b2 = levels[1]
+    three, mob3, right3, a3, b3 = levels[2]
+    rows1, columns1, lanes = mob1.shape
+    rows2, columns2 = mob2.shape[:2]
+    rows3, columns3 = mob3.shape[:2]
+    slots_x, slots_y = packed.shape[1], packed.shape[0]
+    own_rows, own_columns = rows1 // slots_x, columns1 // slots_y
+    even = lane_bit((own_columns, lanes), 1)
+    targets = (right1[0], right1[1], mob1)
+
+    bits = slots_y.bit_length() - 1
+
+    def unpack(slot, carry):
+        slot_y, slot_x = slot // slots_x, slot % slots_x
+        from_y = at_y
+        for bit in range(bits):
+            from_y = from_y ^ (((slot_y >> bit) & 1) << (bits - 1 - bit))
+        row0 = (at_x ^ slot_x) * own_rows
+        column = pl.ds(pl.multiple_of(from_y * own_columns, 8), own_columns)
+        for field in range(3):
+            for index in range(own_rows // 2):
+                pair = packed[slot_y, slot_x, field, index]
+                targets[field][row0 + 2 * index, column, :] = jnp.where(
+                    even, pair, lane_roll(pair, 1)
+                )
+                targets[field][row0 + 2 * index + 1, column, :] = jnp.where(
+                    even, lane_roll(pair, -1), pair
+                )
+        return carry
+
+    lax.fori_loop(0, slots_x * slots_y, unpack, 0)
+
+    def coarsen_into(sums, out, count, columns, dup):
+        for field in range(len(out)):
+            for index in range(count):
+                half = pair_rows(sums.at[field], index, columns)
+                out[field][index] = 0.125 * pair_lanes(half, dup)
+
+    def mobility_sums(mobility, sums):
+        for index in range(mobility.shape[0] // 2):
+            sums[2, index] = mobility[2 * index] + mobility[2 * index + 1]
+
+    def keep_in(sums):
+        def keep(index, conc_sum, chem_sum):
+            sums[0, index] = conc_sum
+            sums[1, index] = chem_sum
+
+        return keep
+
+    one.set_weights(mob1, 0, rows1, 2)
+    one.first_sweep(right1, a1, 2)
+    one.sweep(a1, right1, 0, rows1, 2, put_in(*b1))
+    one.coarse_right(b1, right1, 0, rows1, 2, keep_in(sums1))
+    mobility_sums(mob1, sums1)
+    coarsen_into(sums1, (right2[0], right2[1], mob2), rows2, columns2, 2)
+
+    two.set_weights(mob2, 0, rows2, 4)
+    two.first_sweep(right2, a2, 4)
+    two.sweep(a2, right2, 0, rows2, 4, put_in(*b2))
+    two.coarse_right(b2, right2, 0, rows2, 4, keep_in(sums2))
+    mobility_sums(mob2, sums2)
+    coarsen_into(sums2, (right3[0], right3[1], mob3), rows3, columns3, 4)
+
+    three.set_weights(mob3, 0, rows3, rows3)
+    three.first_sweep(right3, a3, rows3)
+    now, other = a3, b3
+    for sweep_index in range(COARSE - 1):
+        three.sweep(now, right3, 0, rows3, rows3, put_in(*other))
+        now, other = other, now
+
+    for field in range(2):
+        for row in range(rows3):
+            spread_rows(spread3.at[field], row, now[field][row])
+            both = spread3[field, row]
+            a2[field][2 * row] = b2[field][2 * row] + both
+            a2[field][2 * row + 1] = b2[field][2 * row + 1] + both
+    two.sweep(a2, right2, 0, rows2, 4, put_in(*b2))
+    two.sweep(b2, right2, 0, rows2, 4, put_in(*a2))
+
+    first2 = at_x * (own_rows // 2) - 2
+    for field in range(2):
+        for index in range(own_rows // 2 + 4):
+            row = wrapped(first2 + index, rows2)
+            spread_rows(spread2.at[field], index, a2[field][row])
+            both = spread2[field, index]
+            a1[field][2 * row] = b1[field][2 * row] + both
+            a1[field][2 * row + 1] = b1[field][2 * row + 1] + both
+    own_first = at_x * own_rows
+    one.sweep(a1, right1, own_first - 2, own_rows + 4, 2, put_in(*b1))
+    one.sweep(b1, right1, own_first - 1, own_rows + 2, 2, put_in(*a1))
+
+    low = low_rows((8, lanes))
+    fine_columns = 2 * own_columns
+    for field, (source, target) in enumerate(((conc_in, fine_a0), (chem_in, fine_a1))):
+        for index in range(own_rows + 2):
+            row = wrapped(own_first - 1 + index, rows1)
+            for side in range(3):
+                column = lax.rem(at_y + slots_y + side - 1, slots_y) * own_columns
+                tile = a1[field][row, pl.ds(pl.multiple_of(column, 8), own_columns), :]
+                spread_rows(spread_fine.at[field, side], index, tile)
+            rim = jnp.where(
+                low,
+                spread_fine[field, 2, index, :8],
+                spread_fine[field, 0, index, fine_columns - 8 :],
+            )
+            both = jnp.concatenate([spread_fine[field, 1, index], rim], axis=0)
+            for fine in (HALO - 2 + 2 * index, HALO - 1 + 2 * index):
+                target[fine] = source[fine] + both
+    fine = Level(0, (face_x, face_y, face_z, coupling, gain))
+    right_side = (right_conc, right_chem)
+    rows = conc_new.shape[0]
+    fine.sweep(
+        (fine_a0, fine_a1), right_side, HALO - 1, rows + 2, 2, put_in(fine_b0, fine_b1)
+    )
+
+    def put_new(row, conc_value, chem_value):
+        conc_new[row - HALO] = conc_value[:fine_columns]
+        chem_new[row - HALO] = chem_value[:fine_columns]
+
+    fine.sweep((fine_b0, fine_b1), right_side, HALO, rows, 2, put_new)
+
+
+def call_kernel(kernel, outs, scratch, *args, scalars=0):
+    shapes = tuple(jax.ShapeDtypeStruct(shape, jnp.float32) for shape in outs)
+    specs = [pl.BlockSpec(memory_space=pltpu.SMEM)] * scalars
+    specs += [whole_block()] * (len(args) - scalars)
+    return pl.pallas_call(
+        kernel,
+        out_shape=shapes,
+        in_specs=specs,
+        out_specs=tuple(whole_block() for _ in outs),
+        scratch_shapes=[pltpu.VMEM(shape, jnp.float32) for shape in scratch],
+        compiler_params=pltpu.CompilerParams(vmem_limit_bytes=40 * 1024 * 1024),
+    )(*args)
+
+
+def shifted(values, axis, by):
+    count = lax.axis_size(axis)
+    return lax.ppermute(values, axis, [(i, (i + by) % count) for i in range(count)])
+
+
+def swapped(values, axis, mask):
+    count = lax.axis_size(axis)
+    return lax.ppermute(values, axis, [(i, i ^ mask) for i in range(count)])
+
+
+def gathered(values):
+    count_x, count_y = lax.axis_size("gx"), lax.axis_size("gy")
+    stack = jnp.stack([values] + [swapped(values, "gx", mask) for mask in range(1, count_x)])
+    stack = stack[None]
+    for bit in reversed(range(count_y.bit_length() - 1)):
+        stack = jnp.concatenate([stack, swapped(stack, "gy", 1 << bit)], axis=0)
+    return stack
+
+
+def two_phase_solve(conc, chem):
+    rows, columns, lanes = conc.shape
+    frame = (rows + 2 * HALO, columns + 8, lanes)
+    edge = (2, HALO, columns, lanes)
+    low, high = call_kernel(edge_rows_kernel, (edge, edge), (), conc, chem)
+    before, after = shifted(high, "gx", 1), shifted(low, "gx", -1)
+    side = (frame[0], 8, lanes)
+    to_left, to_right = call_kernel(
+        edge_columns_kernel, (side, side), (), conc, chem, before, after
+    )
+    from_left, from_right = shifted(to_right, "gy", 1), shifted(to_left, "gy", -1)
+    packed_shape = (3, rows // 4, columns // 2, lanes)
+    packed, *kept = call_kernel(
+        fine_down_kernel,
+        (packed_shape,) + (frame,) * 9,
+        (frame,) * 4 + ((3, rows // 2, columns + 8, lanes),),
+        conc, chem, before, after, from_left, from_right,
+    )
+    place = jnp.stack([lax.axis_index("gx"), lax.axis_index("gy")])
+    count_x, count_y = lax.axis_size("gx"), lax.axis_size("gy")
+    grids = [
+        (count_x * rows >> level, count_y * columns >> level, lanes) for level in range(4)
+    ]
+    own_rows = rows // 2
+    scratch = [grids[level] for level in (1, 2, 3) for _ in range(12)]
+    scratch += [(3, grids[2][0], grids[1][1], lanes), (3, grids[3][0], grids[2][1], lanes)]
+    scratch += [(2, own_rows // 2 + 4, grids[1][1], lanes), (2, grids[3][0], grids[2][1], lanes)]
+    scratch += [(2, 3, own_rows + 2, columns, lanes)] + [frame] * 4
+    block = (rows, columns, lanes)
+    return call_kernel(
+        coarse_kernel, (block, block), scratch, place, gathered(packed), *kept, scalars=1
+    )
+
+
 def body(conc_old, chem_old):
+    rows, columns, lanes = conc_old.shape
+    count_x, count_y = lax.axis_size("gx"), lax.axis_size("gy")
+    grid_bytes = count_x * rows * count_y * columns * lanes
+    if (
+        grid_bytes <= GRID_BYTES_MAX
+        and rows % 16 == 0
+        and columns % 16 == 0
+        and lanes % 128 == 0
+        and count_x * rows >= 32
+        and count_x & (count_x - 1) == 0
+        and count_y & (count_y - 1) == 0
+    ):
+        return two_phase_solve(conc_old, chem_old)
     start_fields = jnp.stack([conc_old, chem_old])
     result = plain_solve(start_fields)
     return (result[0], result[1])

time: 304 us -> 61.3 us (0.20)
  local copies, waits for them, and re-layouts: 113 us -> 1.8 us
  starting transfers between devices: 113 us -> 12.9 us
  waiting for transfers between devices: 46.3 us -> 18.5 us
  other arithmetic: 27.2 us -> 1.17 us
  Pallas kernels: 0 us -> 26 us
    ppermute x84 -> x9, starting transfers between devices: 113 us -> 12.9 us  [the longest x4 6.96 us: shifted(): lax.ppermute(values, axis, [(i, (i + by) % count) for i in range(count)])]
    another operation x12 -> x0, local copies, waits for them, and re-layouts: 68.1 us -> none  [the longest x8 36.4 us: apply_operator(): return jnp.stack([first_eq, second_eq])]
    ppermute x84 -> x9, waiting for transfers between devices: 46.3 us -> 18.5 us  [the longest x5 13.2 us: swapped(): return lax.ppermute(values, axis, [(i, i ^ mask) for i in range(count)])]
    pallas_call x0 -> x4, Pallas kernels: none -> 26 us  [call_kernel(): pl.pallas_call(kernel, out_shape=shapes, in_specs=specs, out_specs=tuple(...]
    slice x113 -> x0, local copies, waits for them, and re-layouts: 20 us -> none  [the longest x50 13.5 us: neighbour_list(): jnp.roll(middle, 1, axis=2)]
    reshape x7 -> x0, local copies, waits for them, and re-layouts: 13.3 us -> none  [the longest x1 9.81 us: coarsen(): values.reshape(dims_now[:-3] + (dims_now[-3] // 2, 2, dims_now[-2] // 2,...]
    another operation x52 -> x1, other arithmetic: 8.69 us -> 0.08 us  [two_phase_solve(): place = jnp.stack([lax.axis_index('gx'), lax.axis_index('gy')])]
    reduce_sum x6 -> x0, other arithmetic: 6.47 us -> none  [coarsen(): return jnp.sum(grouped, axis=(-5, -3, -1)) * 0.125]
  transfers between devices with their start and end apart: 84 -> 9, of which waited for: 37 -> 8; matrix products, arithmetic and copies ran while one was open for 33% -> 0% of each run, Pallas kernels for 0% -> 0%
where the time goes in v1:
time: 61.3 us; the launch traced here: 61.1 us
  Pallas kernels  26 us (42%)
  waiting for transfers between devices  18.5 us (30%)
  starting transfers between devices  12.9 us (21%)
  local copies, waits for them, and re-layouts  1.8 us (3%)
  other arithmetic  1.17 us (2%)
  between operations  0.7 us (1%)
    pallas_call x4, Pallas kernels, call_kernel(): pl.pallas_call(kernel, out_shape=shapes, in_specs=specs, out_specs=tuple(...  26 us
    ppermute x5, waiting for transfers between devices, swapped(): return lax.ppermute(values, axis, [(i, i ^ mask) for i in range(count)])  13.2 us
    ppermute x4, starting transfers between devices, shifted(): lax.ppermute(values, axis, [(i, (i + by) % count) for i in range(count)])  6.96 us
    ppermute x5, starting transfers between devices, swapped(): return lax.ppermute(values, axis, [(i, i ^ mask) for i in range(count)])  5.94 us
    ppermute x4, waiting for transfers between devices, shifted(): lax.ppermute(values, axis, [(i, (i + by) % count) for i in range(count)])  5.23 us
    unnamed x4, local copies, waits for them, and re-layouts  1.8 us
  transfers between devices with their start and end apart: 9, of which 8 were waited for; matrix products, arithmetic and copies ran while one was open for 0% of the time, Pallas kernels for 0%

profile of v1, /device:TPU:0, one launch (start us, length us, event | category | flops | bytes accessed | tf_op | source)
XLA Modules:
  0.0 61.1 jit_solution(14991707772466993266)
XLA Ops:
  0.6 0.0 copy-start
  0.6 0.9 %copy-done = f32[16,16,128]{2,1,0:T(8,128)S(1)} copy-done((f32[16,16,128]{2,1,0:T(8,128)S(1)}, f32[16,16,128]{2,1,0:T(8,128)}, u32[]{:S(2)}) %copy-start) | copy-done | bytes 131096
  1.5 0.0 copy-start.1
  1.5 0.9 %copy-done.1 = f32[16,16,128]{2,1,0:T(8,128)S(1)} copy-done((f32[16,16,128]{2,1,0:T(8,128)S(1)}, f32[16,16,128]{2,1,0:T(8,128)}, u32[]{:S(2)}) %copy-start.1) | copy-done | bytes 131096
  2.5 3.1 %collective-permute-start = (f32[2,4,16,128]{3,2,1,0:T(8,128)S(1)}, f32[2,4,16,128]{3,2,1,0:T(8,128)S(1)}, u32[]{:S(2)}, u32[]{:S(2)}) collective-permute-start(f32[2,4,16,128]{3,2,1,0:T(8,128)S(1)} %get-tuple-element.16), channel_id=1, source_target_pairs={{0,4},{4,8},{8,12},{12,0},{1,5},{5,9},{9,13},{13,1},{2,6},{6,10},{... | collective-permute-start | bytes 196616 | tf_op jit(solution)/shard_map/ppermute | solution.py:573
  5.5 2.1 %collective-permute-start.1 = (f32[2,4,16,128]{3,2,1,0:T(8,128)S(1)}, f32[2,4,16,128]{3,2,1,0:T(8,128)S(1)}, u32[]{:S(2)}, u32[]{:S(2)}) collective-permute-start(f32[2,4,16,128]{3,2,1,0:T(8,128)S(1)} %get-tuple-element.17), channel_id=1, source_target_pairs={{0,12},{4,0},{8,4},{12,8},{1,13},{5,1},{9,5},{13,9},{2,14},{6,2},{... | collective-permute-start | bytes 196616 | tf_op jit(solution)/shard_map/ppermute | solution.py:573
  7.6 2.3 %collective-permute-done.before = f32[2,4,16,128]{3,2,1,0:T(8,128)S(1)} collective-permute-done((f32[2,4,16,128]{3,2,1,0:T(8,128)S(1)}, f32[2,4,16,128]{3,2,1,0:T(8,128)S(1)}, u32[]{:S(2)}, u32[]{:S(2)}) %collective-permute-start) | collective-permute-done | bytes 65568 | tf_op jit(solution)/shard_map/ppermute | solution.py:573
  9.9 0.5 collective-permute-done.1.after
  10.5 0.1 collective-permute-start.2
  10.6 1.7 %collective-permute-start.3 = (f32[24,8,128]{2,1,0:T(8,128)S(1)}, f32[24,8,128]{2,1,0:T(8,128)S(1)}, u32[]{:S(2)}, u32[]{:S(2)}) collective-permute-start(f32[24,8,128]{2,1,0:T(8,128)S(1)} %get-tuple-element.19), channel_id=1, source_target_pairs={{0,3},{1,0},{2,1},{3,2},{4,7},{5,4},{6,5},{7,6},{8,11},{9,8},{10,9... | collective-permute-start | bytes 294920 | tf_op jit(solution)/shard_map/ppermute | solution.py:573
  12.3 2.3 %collective-permute-done.2.from_left = f32[24,8,128]{2,1,0:T(8,128)S(1)} collective-permute-done((f32[24,8,128]{2,1,0:T(8,128)S(1)}, f32[24,8,128]{2,1,0:T(8,128)S(1)}, u32[]{:S(2)}, u32[]{:S(2)}) %collective-permute-start.2) | collective-permute-done | bytes 98336 | tf_op jit(solution)/shard_map/ppermute | solution.py:573
  14.6 0.1 collective-permute-done.3.from_right
  14.7 6.6 %shard_map.43 = (f32[3,4,8,128]{3,2,1,0:T(8,128)S(1)}, f32[24,24,128]{2,1,0:T(8,128)S(1)}, f32[24,24,128]{2,1,0:T(8,128)S(1)}, f32[24,24,128]{2,1,0:T(8,128)S(1)...) custom-call(f32[16,16,128]{2,1,0:T(8,128)S(1)} %copy-done, ...), custom_call_target="tpu_custom_call" | custom-call | tf_op jit(solution)/shard_map/pallas_call | solution.py:561
  21.3 1.2 %collective-permute-start.4 = (f32[3,4,8,128]{3,2,1,0:T(8,128)S(1)}, f32[3,4,8,128]{3,2,1,0:T(8,128)S(1)}, u32[]{:S(2)}, u32[]{:S(2)}) collective-permute-start(f32[3,4,8,128]{3,2,1,0:T(8,128)S(1)} %get-tuple-element.20), channel_id=1, source_target_pairs={{0,4},{4,0},{8,12},{12,8},{1,5},{5,1},{9,13},{13,9},{2,6},{6,2},{1... | collective-permute-start | bytes 147464 | tf_op jit(solution)/shard_map/ppermute | solution.py:578
  22.5 2.8 %collective-permute-start.5 = (f32[3,4,8,128]{3,2,1,0:T(8,128)S(1)}, f32[3,4,8,128]{3,2,1,0:T(8,128)S(1)}, u32[]{:S(2)}, u32[]{:S(2)}) collective-permute-start(f32[3,4,8,128]{3,2,1,0:T(8,128)S(1)} %get-tuple-element.20), channel_id=1, source_target_pairs={{0,8},{4,12},{8,0},{12,4},{1,9},{5,13},{9,1},{13,5},{2,10},{6,14},... | collective-permute-start | bytes 147464 | tf_op jit(solution)/shard_map/ppermute | solution.py:578
  25.3 0.5 collective-permute-start.6
  25.8 0.0 collective-permute-done.4
  25.8 2.3 %collective-permute-done.5 = f32[3,4,8,128]{3,2,1,0:T(8,128)S(1)} collective-permute-done((f32[3,4,8,128]{3,2,1,0:T(8,128)S(1)}, f32[3,4,8,128]{3,2,1,0:T(8,128)S(1)}, u32[]{:S(2)}, u32[]{:S(2)}) %collective-permute-start.5) | collective-permute-done | bytes 49184 | tf_op jit(solution)/shard_map/ppermute | solution.py:578
  28.1 3.6 %collective-permute-done.6 = f32[3,4,8,128]{3,2,1,0:T(8,128)S(1)} collective-permute-done((f32[3,4,8,128]{3,2,1,0:T(8,128)S(1)}, f32[3,4,8,128]{3,2,1,0:T(8,128)S(1)}, u32[]{:S(2)}, u32[]{:S(2)}) %collective-permute-start.6) | collective-permute-done | bytes 49184 | tf_op jit(solution)/shard_map/ppermute | solution.py:578
  31.7 1.4 %collective-permute-start.7 = (f32[1,4,3,4,8,128]{5,4,3,2,1,0:T(8,128)S(1)}, f32[1,4,3,4,8,128]{5,4,3,2,1,0:T(8,128)S(1)}, u32[]{:S(2)}, u32[]{:S(2)}) collective-permute-start(f32[1,4,3,4,8,128]{5,4,3,2,1,0:T(8,128)S(1)} %maximum_bitcast_fusion), channel_id=1, source_target_pairs={{0,2},{1,3},{2,0},{3,1},{4,6},{5,7},{6,4},{7,5},{8,10},{9,11},{10,... | collective-permute-start | bytes 589832 | tf_op jit(solution)/shard_map/ppermute | solution.py:578
  33.1 5.6 %collective-permute-done.7 = f32[1,4,3,4,8,128]{5,4,3,2,1,0:T(8,128)S(1)} collective-permute-done((f32[1,4,3,4,8,128]{5,4,3,2,1,0:T(8,128)S(1)}, f32[1,4,3,4,8,128]{5,4,3,2,1,0:T(8,128)S(1)}, u32[]{:S(2)}, u32[]{:S(2)}) %collective-permute-start.7) | collective-permute-done | bytes 196640 | tf_op jit(solution)/shard_map/ppermute | solution.py:578
  38.7 0.1 collective-permute-start.8
  38.8 0.1 pad_add_fusion.place
  38.9 1.8 %collective-permute-done.8 = f32[2,4,3,4,8,128]{5,4,3,2,1,0:T(8,128)} collective-permute-done((f32[2,4,3,4,8,128]{5,4,3,2,1,0:T(8,128)S(1)}, f32[2,4,3,4,8,128]{5,4,3,2,1,0:T(8,128)}, u32[]{:S(2)}, u32[]{:S(2)}) %collective-permute-start.8) | collective-permute-done | bytes 393248 | tf_op jit(solution)/shard_map/ppermute | solution.py:578
  40.7 1.1 %pad_maximum_fusion.packed = f32[4,4,3,4,8,128]{5,4,3,2,1,0:T(8,128)S(1)} fusion(f32[2,4,3,4,8,128]{5,4,3,2,1,0:T(8,128)} %collective-permute-done.8, f32[1,4,3,4,8,128]{5,4,3,2,1,0:T(8,128)S(1)} %collective-permute-done.7, f32[1,4,3,4,8,128]{5,4,3,2,1,0:T(8,128)S(1)} %maximum_bitcast_fusion), kind=kLoop, calls=%fused_computation | loop fusion | flops 393216 | bytes 1572864 | tf_op jit(solution)/shard_map/concatenate | solution.py:586
  41.7 19.4 %shard_map.44 = (f32[16,16,128]{2,1,0:T(8,128)}, f32[16,16,128]{2,1,0:T(8,128)}) custom-call(s32[2]{0:T(128)S(1)} %pad_add_fusion.place, f32[4,4,3,4,8,128]{5,4,3,2,1,0:T(8,128)S(1)} %pad_maximum_fusion.packed, f32[24,24,128]{2,1,0:T(8,128)S(1)} %get-tuple-element.21.conc_in, f32[24,24,128]{2,1,0:T(8,128)S(1)} %get-tuple-element.22.chem_in, ...), custom_call_target="tpu_custom_call" | custom-call | tf_op jit(solution)/shard_map/pallas_call | solution.py:561
  (4 shorter events, 0.1 us)
Async XLA Ops:
  0.6 0.9 %copy-start = (f32[16,16,128]{2,1,0:T(8,128)S(1)}, f32[16,16,128]{2,1,0:T(8,128)}, u32[]{:S(2)}) copy-start(f32[16,16,128]{2,1,0:T(8,128)} %conc.5) | copy-start | bytes 393220
  1.5 0.9 %copy-start.1 = (f32[16,16,128]{2,1,0:T(8,128)S(1)}, f32[16,16,128]{2,1,0:T(8,128)}, u32[]{:S(2)}) copy-start(f32[16,16,128]{2,1,0:T(8,128)} %chem.5) | copy-start | bytes 393220
  2.5 7.5 %collective-permute-start = (f32[2,4,16,128]{3,2,1,0:T(8,128)S(1)}, f32[2,4,16,128]{3,2,1,0:T(8,128)S(1)}, u32[]{:S(2)}, u32[]{:S(2)}) collective-permute-start(f32[2,4,16,128]{3,2,1,0:T(8,128)S(1)} %get-tuple-element.16), channel_id=1, source_target_pairs={{0,4},{4,8},{8,12},{12,0},{1,5},{5,9},{9,13},{13,1},{2,6},{6,10},{... | collective-permute-start | bytes 196616 | tf_op jit(solution)/shard_map/ppermute | solution.py:573
  5.5 5.0 %collective-permute-start.1 = (f32[2,4,16,128]{3,2,1,0:T(8,128)S(1)}, f32[2,4,16,128]{3,2,1,0:T(8,128)S(1)}, u32[]{:S(2)}, u32[]{:S(2)}) collective-permute-start(f32[2,4,16,128]{3,2,1,0:T(8,128)S(1)} %get-tuple-element.17), channel_id=1, source_target_pairs={{0,12},{4,0},{8,4},{12,8},{1,13},{5,1},{9,5},{13,9},{2,14},{6,2},{... | collective-permute-start | bytes 196616 | tf_op jit(solution)/shard_map/ppermute | solution.py:573
  10.5 4.1 %collective-permute-start.2 = (f32[24,8,128]{2,1,0:T(8,128)S(1)}, f32[24,8,128]{2,1,0:T(8,128)S(1)}, u32[]{:S(2)}, u32[]{:S(2)}) collective-permute-start(f32[24,8,128]{2,1,0:T(8,128)S(1)} %get-tuple-element.18), channel_id=1, source_target_pairs={{0,1},{1,2},{2,3},{3,0},{4,5},{5,6},{6,7},{7,4},{8,9},{9,10},{10,1... | collective-permute-start | bytes 294920 | tf_op jit(solution)/shard_map/ppermute | solution.py:573
  10.6 4.1 %collective-permute-start.3 = (f32[24,8,128]{2,1,0:T(8,128)S(1)}, f32[24,8,128]{2,1,0:T(8,128)S(1)}, u32[]{:S(2)}, u32[]{:S(2)}) collective-permute-start(f32[24,8,128]{2,1,0:T(8,128)S(1)} %get-tuple-element.19), channel_id=1, source_target_pairs={{0,3},{1,0},{2,1},{3,2},{4,7},{5,4},{6,5},{7,6},{8,11},{9,8},{10,9... | collective-permute-start | bytes 294920 | tf_op jit(solution)/shard_map/ppermute | solution.py:573
  21.3 4.5 %collective-permute-start.4 = (f32[3,4,8,128]{3,2,1,0:T(8,128)S(1)}, f32[3,4,8,128]{3,2,1,0:T(8,128)S(1)}, u32[]{:S(2)}, u32[]{:S(2)}) collective-permute-start(f32[3,4,8,128]{3,2,1,0:T(8,128)S(1)} %get-tuple-element.20), channel_id=1, source_target_pairs={{0,4},{4,0},{8,12},{12,8},{1,5},{5,1},{9,13},{13,9},{2,6},{6,2},{1... | collective-permute-start | bytes 147464 | tf_op jit(solution)/shard_map/ppermute | solution.py:578
  22.5 5.6 %collective-permute-start.5 = (f32[3,4,8,128]{3,2,1,0:T(8,128)S(1)}, f32[3,4,8,128]{3,2,1,0:T(8,128)S(1)}, u32[]{:S(2)}, u32[]{:S(2)}) collective-permute-start(f32[3,4,8,128]{3,2,1,0:T(8,128)S(1)} %get-tuple-element.20), channel_id=1, source_target_pairs={{0,8},{4,12},{8,0},{12,4},{1,9},{5,13},{9,1},{13,5},{2,10},{6,14},... | collective-permute-start | bytes 147464 | tf_op jit(solution)/shard_map/ppermute | solution.py:578
  25.3 6.4 %collective-permute-start.6 = (f32[3,4,8,128]{3,2,1,0:T(8,128)S(1)}, f32[3,4,8,128]{3,2,1,0:T(8,128)S(1)}, u32[]{:S(2)}, u32[]{:S(2)}) collective-permute-start(f32[3,4,8,128]{3,2,1,0:T(8,128)S(1)} %get-tuple-element.20), channel_id=1, source_target_pairs={{0,12},{4,8},{8,4},{12,0},{1,13},{5,9},{9,5},{13,1},{2,14},{6,10},... | collective-permute-start | bytes 147464 | tf_op jit(solution)/shard_map/ppermute | solution.py:578
  31.7 7.0 %collective-permute-start.7 = (f32[1,4,3,4,8,128]{5,4,3,2,1,0:T(8,128)S(1)}, f32[1,4,3,4,8,128]{5,4,3,2,1,0:T(8,128)S(1)}, u32[]{:S(2)}, u32[]{:S(2)}) collective-permute-start(f32[1,4,3,4,8,128]{5,4,3,2,1,0:T(8,128)S(1)} %maximum_bitcast_fusion), channel_id=1, source_target_pairs={{0,2},{1,3},{2,0},{3,1},{4,6},{5,7},{6,4},{7,5},{8,10},{9,11},{10,... | collective-permute-start | bytes 589832 | tf_op jit(solution)/shard_map/ppermute | solution.py:578
  38.7 1.9 %collective-permute-start.8 = (f32[2,4,3,4,8,128]{5,4,3,2,1,0:T(8,128)S(1)}, f32[2,4,3,4,8,128]{5,4,3,2,1,0:T(8,128)}, u32[]{:S(2)}, u32[]{:S(2)}) collective-permute-start(f32[2,4,3,4,8,128]{5,4,3,2,1,0:T(8,128)S(1)} %pad_maximum_fusion.1), channel_id=1, source_target_pairs={{0,1},{1,0},{2,3},{3,2},{4,5},{5,4},{6,7},{7,6},{8,9},{9,8},{10,11... | collective-permute-start | bytes 1179656 | tf_op jit(solution)/shard_map/ppermute | solution.py:578

commit v2 on v0

--- a/solution.py
+++ b/solution.py
@@ -1,6 +1,8 @@
 import jax
 import jax.numpy as jnp
 from jax import lax
+from jax.experimental import pallas as pl
+from jax.experimental.pallas import tpu as pltpu
 from jax.sharding import PartitionSpec as P
 
 LEVELS = 4
@@ -173,7 +175,496 @@
     return cycle_level(0, right_of(start_fields[0]))
 
 
+HALO = 4
+PAD = 8
+GRID_BYTES_MAX = 2 * 1024 * 1024
+
+
+def whole_block():
+    return pl.BlockSpec(memory_space=pltpu.VMEM)
+
+
+def lane_roll(values, shift):
+    return pltpu.roll(values, shift % values.shape[1], axis=1)
+
+
+def lane_even(shape, dup):
+    return (lax.broadcasted_iota(jnp.int32, shape, 1) // dup) % 2 == 0
+
+
+def loop_rows(count, unroll, row_group):
+    steps, rest = divmod(count, unroll)
+    if steps == 1:
+        row_group(0, unroll)
+    elif steps > 1:
+
+        def step(index, carry):
+            row_group(index * unroll, unroll)
+            return carry
+
+        lax.fori_loop(0, steps, step, 0)
+    if rest:
+        row_group(steps * unroll, rest)
+
+
+def wrapped(row, count):
+    if isinstance(row, int):
+        return row % count
+    return row & (count - 1) if count & (count - 1) == 0 else row
+
+
+def chem_right(conc):
+    return conc * (conc * conc - (1.0 + STABILIZER))
+
+
+class Level:
+    def __init__(self, level_index, weights, weights_from=PAD, right_from=PAD):
+        self.scale = 0.25**level_index
+        self.dup = 2**level_index
+        self.diagonal = STABILIZER + 6.0 * GRADIENT_ENERGY * self.scale
+        self.weights = weights
+        self.weights_from, self.right_from = weights_from, right_from
+
+    def set_weights(self, mobility, unroll):
+        total, width = mobility.shape[0], self.weights[0].shape[1]
+        half = 0.5 * self.scale * TIME_STEP
+        face_x, up_y, down_y, up_z, down_z, coupling, gain = self.weights
+
+        def at(row, shift=0):
+            return mobility[row, pl.ds(self.weights_from + shift, width), :]
+
+        def group(first, size):
+            rows = [at(wrapped(first + i - 1, total)) for i in range(size + 2)]
+            before = half * (rows[0] + rows[1])
+            for i in range(size):
+                r = first + i
+                here = rows[i + 1]
+                after = half * (here + rows[i + 2])
+                to_up_y = half * (here + at(r, 1))
+                to_down_y = half * (here + at(r, -1))
+                to_up_z = half * (here + lane_roll(here, -self.dup))
+                to_down_z = half * (here + lane_roll(here, self.dup))
+                total_weight = (before + after) + (to_up_y + to_down_y) + (to_up_z + to_down_z)
+                face_x[r] = after
+                up_y[r] = to_up_y
+                down_y[r] = to_down_y
+                up_z[r] = to_up_z
+                down_z[r] = to_down_z
+                coupling[r] = total_weight
+                gain[r] = DAMPING / (1.0 + total_weight * self.diagonal)
+                before = after
+
+        loop_rows(total, unroll, group)
+
+    def residuals(self, fields, right, rows, window, fields_from=0):
+        conc, chem = fields
+        first, width = window
+        face_x, up_y, down_y, up_z, down_z, coupling, gain = self.weights
+
+        def at(ref, row, shift=0):
+            return ref[row, pl.ds(first - fields_from + shift, width), :]
+
+        def weight(ref, row):
+            return ref[row, pl.ds(first - self.weights_from, width), :]
+
+        def right_at(row):
+            values = [ref[row, pl.ds(first - self.right_from, width), :] for ref in right]
+            return values if len(values) == 2 else values + [chem_right(values[0])]
+
+        u = [at(chem, row) for row in rows]
+        c = [at(conc, row) for row in rows]
+        for i in range(1, len(rows) - 1):
+            r = rows[i]
+            here = weight(coupling, r)
+            flux = weight(face_x, r) * u[i + 1] + weight(face_x, rows[i - 1]) * u[i - 1]
+            flux = flux + weight(up_y, r) * at(chem, r, 1) + weight(down_y, r) * at(chem, r, -1)
+            flux = flux + weight(up_z, r) * lane_roll(u[i], -self.dup)
+            flux = flux + weight(down_z, r) * lane_roll(u[i], self.dup)
+            near = (c[i - 1] + c[i + 1]) + (at(conc, r, 1) + at(conc, r, -1))
+            near = near + (lane_roll(c[i], self.dup) + lane_roll(c[i], -self.dup))
+            conc_right, chem_right_here = right_at(r)
+            conc_left = conc_right - c[i] + (flux - here * u[i])
+            chem_left = chem_right_here - u[i] + self.diagonal * c[i]
+            chem_left = chem_left - (GRADIENT_ENERGY * self.scale) * near
+            yield r, c[i], u[i], conc_left, chem_left, here, weight(gain, r)
+
+    def steps(self, conc_left, chem_left, coupling, gain):
+        return (
+            gain * (conc_left - coupling * chem_left),
+            gain * (chem_left + self.diagonal * conc_left),
+        )
+
+    def first_sweep(self, right, unroll, put):
+        coupling, gain = self.weights[5:]
+
+        def group(first, size):
+            for i in range(size):
+                r = first + i
+                put(r, *self.steps(right[0][r], right[1][r], coupling[r], gain[r]))
+
+        loop_rows(right[0].shape[0], unroll, group)
+
+    def row_window(self, total, start, first, size):
+        return [wrapped(start + first + i - 1, total) for i in range(size + 2)]
+
+    def sweep(self, fields, right, start, count, unroll, window, put):
+        def group(first, size):
+            rows = self.row_window(fields[0].shape[0], start, first, size)
+            for r, c, u, *left in self.residuals(fields, right, rows, window):
+                conc_step, chem_step = self.steps(*left)
+                put(r, c + conc_step, u + chem_step)
+
+        loop_rows(count, unroll, group)
+
+    def coarse_right(self, fields, right, start, count, unroll, window, put, fields_from=0):
+        def group(first, size):
+            rows = self.row_window(fields[0].shape[0], start, first, size)
+            items = self.residuals(fields, right, rows, window, fields_from)
+            lefts = [item[3:5] for item in items]
+            for i in range(0, size, 2):
+                half = first // 2 if isinstance(first, int) else lax.shift_right_logical(first, 1)
+                put(half + i // 2, *(a + b for a, b in zip(lefts[i], lefts[i + 1])))
+
+        loop_rows(count, unroll, group)
+
+
+def put_padded(refs):
+    def put(row, *values):
+        for ref, value in zip(refs, values):
+            width = value.shape[0]
+            ref[row, PAD : PAD + width, :] = value
+            ref[row, :PAD, :] = value[width - PAD :]
+            ref[row, PAD + width :, :] = value[:PAD]
+
+    return put
+
+
+def put_window(refs, window):
+    def put(row, *values):
+        for ref, value in zip(refs, values):
+            ref[row, window[0] : window[0] + window[1], :] = value
+
+    return put
+
+
+def put_sums(sums):
+    def put(row, *values):
+        for field, value in enumerate(values):
+            sums[field, row] = value
+
+    return put
+
+
+def pair_rows(ref, row, count):
+    return ref[row, pl.ds(0, count, stride=2), :] + ref[row, pl.ds(1, count, stride=2), :]
+
+
+def spread_rows(ref, row, values):
+    count = values.shape[0]
+    ref[row, pl.ds(0, count, stride=2), :] = values
+    ref[row, pl.ds(1, count, stride=2), :] = values
+
+
+def pair_lanes(values, dup):
+    other = jnp.where(
+        lane_even(values.shape, dup), lane_roll(values, -dup), lane_roll(values, dup)
+    )
+    return values + other
+
+
+def edge_rows_kernel(fields, low, high):
+    rows = fields.shape[1]
+    low[...] = fields[:, :HALO]
+    high[...] = fields[:, rows - HALO :]
+
+
+def frame_row(row, rows, own, before, after):
+    if row < HALO:
+        return before[row]
+    if row < HALO + rows:
+        return own[row - HALO]
+    return after[row - HALO - rows]
+
+
+def half_turn(values):
+    return pltpu.roll(values, HALO, axis=0)
+
+
+def edge_columns_kernel(fields, before, after, to_left, to_right):
+    conc, chem = fields.at[0], fields.at[1]
+    rows, columns, lanes = conc.shape
+    low = lax.broadcasted_iota(jnp.int32, (PAD, lanes), 0) < HALO
+    for row in range(rows + 2 * HALO):
+        c = frame_row(row, rows, conc, before.at[0], after.at[0])
+        u = frame_row(row, rows, chem, before.at[1], after.at[1])
+        to_left[row] = jnp.where(low, c[:PAD], half_turn(u[:PAD]))
+        to_right[row] = jnp.where(low, half_turn(u[columns - PAD :]), c[columns - PAD :])
+
+
+def fine_level(weights):
+    return Level(0, weights, HALO, 0)
+
+
+def fine_down_kernel(
+    fields, before, after, from_left, from_right,
+    packed, kept, right_conc, all_weights,
+    chem_start, mobility, conc_mid, chem_mid, sums,
+):
+    conc, chem = fields.at[0], fields.at[1]
+    conc_out, chem_out = kept.at[0], kept.at[1]
+    weights = [all_weights.at[i] for i in range(7)]
+    rows, columns, lanes = conc.shape
+    frame = rows + 2 * HALO
+    for row in range(frame):
+        left, right = from_left[row], from_right[row]
+        c = jnp.concatenate([left, frame_row(row, rows, conc, before.at[0], after.at[0]), right])
+        own = frame_row(row, rows, chem, before.at[1], after.at[1])
+        right_conc[row] = c
+        chem_start[row] = jnp.concatenate([half_turn(left), own, half_turn(right)])
+        gap = 1.0 - c * c
+        mobility[row] = 0.1 + gap * gap
+    level = fine_level(weights)
+    level.set_weights(mobility, frame)
+    right_side = (right_conc,)
+    wide = (PAD - HALO, columns + 2 * HALO)
+    level.sweep(
+        (right_conc, chem_start), right_side, 1, frame - 2, 11, wide,
+        put_window((conc_mid, chem_mid), wide),
+    )
+    level.sweep(
+        (conc_mid, chem_mid), right_side, 2, frame - 4, 10, wide,
+        put_window((conc_out, chem_out), (0, wide[1])),
+    )
+    level.coarse_right(
+        (conc_out, chem_out), right_side, HALO, rows, 8, (PAD, columns), put_sums(sums), wide[0]
+    )
+    for index in range(rows // 2):
+        row = HALO + 2 * index
+        own = slice(PAD, PAD + columns)
+        sums[2, index] = mobility[row, own, :] + mobility[row + 1, own, :]
+    even = lane_even((columns // 2, lanes), 1)
+    for field in range(3):
+        for index in range(rows // 4):
+            a = pair_rows(sums.at[field], 2 * index, columns // 2)
+            b = pair_rows(sums.at[field], 2 * index + 1, columns // 2)
+            packed[field, index] = 0.125 * jnp.where(
+                even, a + lane_roll(a, -1), b + lane_roll(b, 1)
+            )
+
+
+def coarse_kernel(
+    place, near, far, kept, right_conc, all_weights, conc_new, chem_new, *scratch
+):
+    conc_in, chem_in = kept.at[0], kept.at[1]
+    weights = [all_weights.at[i] for i in range(7)]
+    scratch = list(scratch)
+    at_x, at_y = place[0], place[1]
+    levels = []
+    for level_index in (1, 2, 3):
+        level = Level(level_index, scratch[5:14][2:])
+        mobility, a, b, right = scratch[0], scratch[1:3], scratch[3:5], scratch[5:7]
+        levels.append((level, mobility, right, a, b))
+        del scratch[:14]
+    sums1, sums2, spread2, spread3, spread_fine, fine_a0, fine_a1, fine_b0, fine_b1 = scratch
+    one, mob1, right1, a1, b1 = levels[0]
+    two, mob2, right2, a2, b2 = levels[1]
+    three, mob3, right3, a3, b3 = levels[2]
+    rows1, columns1, lanes = right1[0].shape
+    rows2, columns2 = right2[0].shape[:2]
+    rows3, columns3 = right3[0].shape[:2]
+    window1, window2, window3 = (PAD, columns1), (PAD, columns2), (PAD, columns3)
+    slots_x, slots_y = near.shape[1], 2 * near.shape[0]
+    own_rows, own_columns = rows1 // slots_x, columns1 // slots_y
+    even = lane_even((own_columns, lanes), 1)
+    bits = slots_y.bit_length() - 1
+
+    def unpack(source, slot_y, from_y):
+        offset = from_y * own_columns
+        plain = pl.ds(pl.multiple_of(offset, PAD), own_columns)
+        padded = pl.ds(pl.multiple_of(offset + PAD, PAD), own_columns)
+        for slot_x in range(slots_x):
+            row = (at_x ^ slot_x) * own_rows
+            for field, (ref, at) in enumerate(
+                ((right1[0], plain), (right1[1], plain), (mob1, padded))
+            ):
+                for index in range(own_rows // 2):
+                    pair = source[slot_y, slot_x, field, index]
+                    ref[row + 2 * index, at, :] = jnp.where(even, pair, lane_roll(pair, 1))
+                    ref[row + 2 * index + 1, at, :] = jnp.where(even, lane_roll(pair, -1), pair)
+
+    for last, source in enumerate((near, far)):
+        for slot_y in range(slots_y // 2):
+            mask = last
+            for bit in range(bits - 1):
+                mask |= (slot_y >> bit & 1) << (bits - 1 - bit)
+            unpack(source, slot_y, at_y ^ mask)
+    for row in range(rows1):
+        mob1[row, :PAD, :] = mob1[row, columns1 : columns1 + PAD, :]
+        mob1[row, PAD + columns1 :, :] = mob1[row, PAD : 2 * PAD, :]
+
+    def coarsen(mobility, sums, out, out_mobility, dup):
+        count, columns = out[0].shape[:2]
+        fine = pl.ds(PAD, 2 * columns)
+        for index in range(count):
+            sums[2, index] = mobility[2 * index, fine, :] + mobility[2 * index + 1, fine, :]
+        for index in range(count):
+            for field in range(2):
+                half = pair_rows(sums.at[field], index, columns)
+                out[field][index] = 0.125 * pair_lanes(half, dup)
+            half = pair_rows(sums.at[2], index, columns)
+            put_padded((out_mobility,))(index, 0.125 * pair_lanes(half, dup))
+
+    one.set_weights(mob1, 16)
+    one.first_sweep(right1, 16, put_padded(a1))
+    one.sweep(a1, right1, 0, rows1, 16, window1, put_padded(b1))
+    one.coarse_right(b1, right1, 0, rows1, 16, window1, put_sums(sums1))
+    coarsen(mob1, sums1, right2, mob2, 2)
+
+    two.set_weights(mob2, 16)
+    two.first_sweep(right2, 16, put_padded(a2))
+    two.sweep(a2, right2, 0, rows2, 16, window2, put_padded(b2))
+    two.coarse_right(b2, right2, 0, rows2, 16, window2, put_sums(sums2))
+    coarsen(mob2, sums2, right3, mob3, 4)
+
+    three.set_weights(mob3, rows3)
+    three.first_sweep(right3, rows3, put_padded(a3))
+    now, other = a3, b3
+    for sweep_index in range(COARSE - 1):
+        three.sweep(now, right3, 0, rows3, rows3, window3, put_padded(other))
+        now, other = other, now
+
+    def correct(coarse, coarse_row, fine_in, fine_out, spread, index):
+        for field in range(2):
+            columns = fine_in[field].shape[1] - 2 * PAD
+            spread_rows(
+                spread.at[field], index, coarse[field][coarse_row, pl.ds(PAD, columns // 2), :]
+            )
+            both = spread[field, index]
+            for row in (2 * coarse_row, 2 * coarse_row + 1):
+                put_padded((fine_out[field],))(
+                    row, fine_in[field][row, pl.ds(PAD, columns), :] + both
+                )
+
+    for row in range(rows3):
+        correct(now, row, b2, a2, spread3, row)
+    two.sweep(a2, right2, 0, rows2, 16, window2, put_padded(b2))
+    two.sweep(b2, right2, 0, rows2, 16, window2, put_padded(a2))
+    for index in range(own_rows // 2 + 4):
+        row = wrapped(at_x * (own_rows // 2) - 2 + index, rows2)
+        correct(a2, row, b1, a1, spread2, index)
+    own_first = at_x * own_rows
+    one.sweep(a1, right1, own_first - 2, own_rows + 4, 12, window1, put_padded(b1))
+    one.sweep(b1, right1, own_first - 1, own_rows + 2, 10, window1, put_padded(a1))
+
+    rows, columns = conc_new.shape[:2]
+    wide = (PAD - HALO, columns + 2 * HALO)
+    near_own = pl.ds(pl.multiple_of(at_y * own_columns, PAD), own_columns + 2 * PAD)
+    for index in range(own_rows + 2):
+        row = wrapped(own_first - 1 + index, rows1)
+        for field, (source, target) in enumerate(((conc_in, fine_a0), (chem_in, fine_a1))):
+            spread_rows(spread_fine.at[field], index, a1[field][row, near_own, :])
+            both = spread_fine[field, index, pl.ds(wide[0] + PAD, wide[1]), :]
+            for fine in (HALO - 2 + 2 * index, HALO - 1 + 2 * index):
+                put_window((target,), wide)(fine, source[fine] + both)
+    fine = fine_level(weights)
+    right_side = (right_conc,)
+    fine.sweep(
+        (fine_a0, fine_a1), right_side, HALO - 1, rows + 2, 9, wide,
+        put_window((fine_b0, fine_b1), wide),
+    )
+
+    def put_new(row, conc_value, chem_value):
+        conc_new[row - HALO] = conc_value
+        chem_new[row - HALO] = chem_value
+
+    fine.sweep((fine_b0, fine_b1), right_side, HALO, rows, 8, (PAD, columns), put_new)
+
+
+def call_kernel(kernel, outs, scratch, *args, specs=None, vmem_mib=8):
+    shapes = tuple(jax.ShapeDtypeStruct(shape, jnp.float32) for shape in outs)
+    scratch = [pltpu.VMEM(shape, jnp.float32) if isinstance(shape, tuple) else shape for shape in scratch]
+    return pl.pallas_call(
+        kernel,
+        out_shape=shapes,
+        in_specs=specs or [whole_block()] * len(args),
+        out_specs=tuple(whole_block() for _ in outs),
+        scratch_shapes=scratch,
+        compiler_params=pltpu.CompilerParams(vmem_limit_bytes=vmem_mib * 1024 * 1024),
+    )(*args)
+
+
+def shifted(values, axis, by):
+    count = lax.axis_size(axis)
+    return lax.ppermute(values, axis, [(i, (i + by) % count) for i in range(count)])
+
+
+def swapped(values, axis, mask):
+    count = lax.axis_size(axis)
+    return lax.ppermute(values, axis, [(i, i ^ mask) for i in range(count)])
+
+
+def gathered(values):
+    count_x, count_y = lax.axis_size("gx"), lax.axis_size("gy")
+    stack = jnp.stack([values] + [swapped(values, "gx", mask) for mask in range(1, count_x)])
+    stack = stack[None]
+    for bit in reversed(range(1, count_y.bit_length() - 1)):
+        stack = jnp.concatenate([stack, swapped(stack, "gy", 1 << bit)], axis=0)
+    return stack, swapped(stack, "gy", 1)
+
+
+def two_phase_solve(conc, chem):
+    rows, columns, lanes = conc.shape
+    frame = (rows + 2 * HALO, columns + 2 * PAD, lanes)
+    inner = (frame[0], columns + 2 * HALO, lanes)
+    edge = (2, HALO, columns, lanes)
+    block = (rows, columns, lanes)
+    fields = jnp.concatenate([conc, chem], axis=0).reshape((2,) + block)
+    low, high = call_kernel(edge_rows_kernel, (edge, edge), (), fields)
+    before, after = shifted(high, "gx", 1), shifted(low, "gx", -1)
+    side = (frame[0], PAD, lanes)
+    to_left, to_right = call_kernel(
+        edge_columns_kernel, (side, side), (), fields, before, after
+    )
+    from_left, from_right = shifted(to_right, "gy", 1), shifted(to_left, "gy", -1)
+    packed, *kept = call_kernel(
+        fine_down_kernel,
+        ((3, rows // 4, columns // 2, lanes), (2,) + inner, frame, (7,) + inner),
+        (frame,) * 4 + ((3, rows // 2, columns, lanes),),
+        fields, before, after, from_left, from_right,
+    )
+    place = jnp.stack([lax.axis_index("gx"), lax.axis_index("gy")])
+    count_x, count_y = lax.axis_size("gx"), lax.axis_size("gy")
+    grids = [(count_x * rows >> level, count_y * columns >> level) for level in range(4)]
+    scratch = []
+    for level_rows, level_columns in grids[1:]:
+        scratch += [(level_rows, level_columns + 2 * PAD, lanes)] * 5
+        scratch += [(level_rows, level_columns, lanes)] * 9
+    scratch += [(3, grids[2][0], grids[1][1], lanes), (3, grids[3][0], grids[2][1], lanes)]
+    scratch += [(2, rows // 4 + 4, grids[1][1], lanes), (2, grids[3][0], grids[2][1], lanes)]
+    scratch += [(2, rows // 2 + 2, columns + 4 * PAD, lanes)] + [frame] * 4
+    args = (place, *gathered(packed), *kept)
+    specs = [pl.BlockSpec(memory_space=pltpu.SMEM)] + [whole_block()] * (len(args) - 1)
+    return call_kernel(coarse_kernel, (block, block), scratch, *args, specs=specs, vmem_mib=24)
+
+
 def body(conc_old, chem_old):
+    rows, columns, lanes = conc_old.shape
+    count_x, count_y = lax.axis_size("gx"), lax.axis_size("gy")
+    grid_bytes = count_x * rows * count_y * columns * lanes
+    if (
+        grid_bytes <= GRID_BYTES_MAX
+        and rows % 16 == 0
+        and columns % 16 == 0
+        and lanes % 128 == 0
+        and count_x * rows >= 64
+        and count_y * columns >= 64
+        and count_y >= 2
+        and count_x & (count_x - 1) == 0
+        and count_y & (count_y - 1) == 0
+        and rows & (rows - 1) == 0
+        and columns & (columns - 1) == 0
+    ):
+        return two_phase_solve(conc_old, chem_old)
     start_fields = jnp.stack([conc_old, chem_old])
     result = plain_solve(start_fields)
     return (result[0], result[1])

time: 304 us -> 41.2 us (0.14)
  local copies, waits for them, and re-layouts: 113 us -> 0 us
  starting transfers between devices: 113 us -> 13.2 us
  waiting for transfers between devices: 46.3 us -> 16.6 us
  other arithmetic: 27.2 us -> 1.1 us
  Pallas kernels: 0 us -> 9.39 us
    ppermute x84 -> x9, starting transfers between devices: 113 us -> 13.2 us  [the longest x4 6.96 us: shifted(): lax.ppermute(values, axis, [(i, (i + by) % count) for i in range(count)])]
    another operation x12 -> x0, local copies, waits for them, and re-layouts: 68.1 us -> none  [the longest x8 36.4 us: apply_operator(): return jnp.stack([first_eq, second_eq])]
    ppermute x84 -> x9, waiting for transfers between devices: 46.3 us -> 16.6 us  [the longest x5 11.3 us: swapped(): return lax.ppermute(values, axis, [(i, i ^ mask) for i in range(count)])]
    slice x113 -> x0, local copies, waits for them, and re-layouts: 20 us -> none  [the longest x50 13.5 us: neighbour_list(): jnp.roll(middle, 1, axis=2)]
    reshape x7 -> x0, local copies, waits for them, and re-layouts: 13.3 us -> none  [the longest x1 9.81 us: coarsen(): values.reshape(dims_now[:-3] + (dims_now[-3] // 2, 2, dims_now[-2] // 2,...]
    pallas_call x0 -> x4, Pallas kernels: none -> 9.39 us  [call_kernel(): pl.pallas_call(kernel, out_shape=shapes, in_specs=specs or [whole_block()...]
    another operation x52 -> x1, other arithmetic: 8.69 us -> 0.08 us  [two_phase_solve(): place = jnp.stack([lax.axis_index('gx'), lax.axis_index('gy')])]
    reduce_sum x6 -> x0, other arithmetic: 6.47 us -> none  [coarsen(): return jnp.sum(grouped, axis=(-5, -3, -1)) * 0.125]
  transfers between devices with their start and end apart: 84 -> 9, of which waited for: 37 -> 8; matrix products, arithmetic and copies ran while one was open for 33% -> 0% of each run, Pallas kernels for 0% -> 0%
where the time goes in v2:
time: 41.2 us; the launch traced here: 41 us
  waiting for transfers between devices  16.6 us (40%)
  starting transfers between devices  13.2 us (32%)
  Pallas kernels  9.39 us (23%)
  other arithmetic  1.1 us (3%)
  between operations  0.69 us (2%)
    ppermute x5, waiting for transfers between devices, swapped(): return lax.ppermute(values, axis, [(i, i ^ mask) for i in range(count)])  11.3 us
    pallas_call x4, Pallas kernels, call_kernel(): pl.pallas_call(kernel, out_shape=shapes, in_specs=specs or [whole_block()...  9.39 us
    ppermute x4, starting transfers between devices, shifted(): lax.ppermute(values, axis, [(i, (i + by) % count) for i in range(count)])  6.96 us
    ppermute x5, starting transfers between devices, swapped(): return lax.ppermute(values, axis, [(i, i ^ mask) for i in range(count)])  6.27 us
    ppermute x4, waiting for transfers between devices, shifted(): lax.ppermute(values, axis, [(i, (i + by) % count) for i in range(count)])  5.23 us
    concatenate x1, other arithmetic, two_phase_solve(): fields = jnp.concatenate([conc, chem], axis=0).reshape((2,) + block)  0.99 us
  transfers between devices with their start and end apart: 9, of which 8 were waited for; matrix products, arithmetic and copies ran while one was open for 0% of the time, Pallas kernels for 0%

profile of v2, /device:TPU:0, one launch (start us, length us, event | category | flops | bytes accessed | tf_op | source)
XLA Modules:
  0.0 41.0 jit_solution(18398296626434342082)
XLA Ops:
  0.6 1.0 %pad_maximum_fusion.1 = f32[32,16,128]{2,1,0:T(8,128)S(1)} fusion(f32[16,16,128]{2,1,0:T(8,128)} %param.3, f32[16,16,128]{2,1,0:T(8,128)} %param.2), kind=kLoop, calls=%fused_computation.1 | loop fusion | flops 65536 | bytes 524288 | tf_op jit(solution)/shard_map/concatenate | solution.py:621
  1.6 3.1 %collective-permute-start = (f32[2,4,16,128]{3,2,1,0:T(8,128)S(1)}, f32[2,4,16,128]{3,2,1,0:T(8,128)S(1)}, u32[]{:S(2)}, u32[]{:S(2)}) collective-permute-start(f32[2,4,16,128]{3,2,1,0:T(8,128)S(1)} %get-tuple-element.10), channel_id=1, source_target_pairs={{0,4},{4,8},{8,12},{12,0},{1,5},{5,9},{9,13},{13,1},{2,6},{6,10},{... | collective-permute-start | bytes 196616 | tf_op jit(solution)/shard_map/ppermute | solution.py:598
  4.7 2.1 %collective-permute-start.1 = (f32[2,4,16,128]{3,2,1,0:T(8,128)S(1)}, f32[2,4,16,128]{3,2,1,0:T(8,128)S(1)}, u32[]{:S(2)}, u32[]{:S(2)}) collective-permute-start(f32[2,4,16,128]{3,2,1,0:T(8,128)S(1)} %get-tuple-element.11), channel_id=1, source_target_pairs={{0,12},{4,0},{8,4},{12,8},{1,13},{5,1},{9,5},{13,9},{2,14},{6,2},{... | collective-permute-start | bytes 196616 | tf_op jit(solution)/shard_map/ppermute | solution.py:598
  6.8 2.3 %collective-permute-done.before = f32[2,4,16,128]{3,2,1,0:T(8,128)S(1)} collective-permute-done((f32[2,4,16,128]{3,2,1,0:T(8,128)S(1)}, f32[2,4,16,128]{3,2,1,0:T(8,128)S(1)}, u32[]{:S(2)}, u32[]{:S(2)}) %collective-permute-start) | collective-permute-done | bytes 65568 | tf_op jit(solution)/shard_map/ppermute | solution.py:598
  9.1 0.5 %collective-permute-done.1.after = f32[2,4,16,128]{3,2,1,0:T(8,128)S(1)} collective-permute-done((f32[2,4,16,128]{3,2,1,0:T(8,128)S(1)}, f32[2,4,16,128]{3,2,1,0:T(8,128)S(1)}, u32[]{:S(2)}, u32[]{:S(2)}) %collective-permute-start.1) | collective-permute-done | bytes 65568 | tf_op jit(solution)/shard_map/ppermute | solution.py:598
  9.7 0.1 collective-permute-start.2
  9.8 1.7 %collective-permute-start.3 = (f32[24,8,128]{2,1,0:T(8,128)S(1)}, f32[24,8,128]{2,1,0:T(8,128)S(1)}, u32[]{:S(2)}, u32[]{:S(2)}) collective-permute-start(f32[24,8,128]{2,1,0:T(8,128)S(1)} %get-tuple-element.13), channel_id=1, source_target_pairs={{0,3},{1,0},{2,1},{3,2},{4,7},{5,4},{6,5},{7,6},{8,11},{9,8},{10,9... | collective-permute-start | bytes 294920 | tf_op jit(solution)/shard_map/ppermute | solution.py:598
  11.5 2.3 %collective-permute-done.2.from_left = f32[24,8,128]{2,1,0:T(8,128)S(1)} collective-permute-done((f32[24,8,128]{2,1,0:T(8,128)S(1)}, f32[24,8,128]{2,1,0:T(8,128)S(1)}, u32[]{:S(2)}, u32[]{:S(2)}) %collective-permute-start.2) | collective-permute-done | bytes 98336 | tf_op jit(solution)/shard_map/ppermute | solution.py:598
  13.8 0.1 collective-permute-done.3.from_right
  13.9 1.6 %shard_map.43 = (f32[3,4,8,128]{3,2,1,0:T(8,128)S(1)}, f32[2,24,24,128]{3,2,1,0:T(8,128)S(1)}, f32[24,32,128]{2,1,0:T(8,128)S(1)}, f32[7,24,24,128]{3,2,1,0:T(8,128)S(1)}) custom-call(f32[2,16,16,128]{3,2,1,0:T(8,128)S(1)} %bitcast.11, f32[2,4,16,128]{3,2,1,0:T(8,128)S(1)} %collective-permute-done.before, ...), custom_call_target="tpu_custom_call" | custom-call | tf_op jit(solution)/shard_map/pallas_call | solution.py:586
  15.5 3.4 %collective-permute-start.6 = (f32[3,4,8,128]{3,2,1,0:T(8,128)S(1)}, f32[3,4,8,128]{3,2,1,0:T(8,128)S(1)}, u32[]{:S(2)}, u32[]{:S(2)}) collective-permute-start(f32[3,4,8,128]{3,2,1,0:T(8,128)S(1)} %get-tuple-element.14), channel_id=1, source_target_pairs={{0,12},{4,8},{8,4},{12,0},{1,13},{5,9},{9,5},{13,1},{2,14},{6,10},... | collective-permute-start | bytes 147464 | tf_op jit(solution)/shard_map/ppermute | solution.py:603
  18.9 0.0 collective-permute-start.5
  18.9 1.0 %collective-permute-start.4 = (f32[3,4,8,128]{3,2,1,0:T(8,128)S(1)}, f32[3,4,8,128]{3,2,1,0:T(8,128)S(1)}, u32[]{:S(2)}, u32[]{:S(2)}) collective-permute-start(f32[3,4,8,128]{3,2,1,0:T(8,128)S(1)} %get-tuple-element.14), channel_id=1, source_target_pairs={{0,4},{4,0},{8,12},{12,8},{1,5},{5,1},{9,13},{13,9},{2,6},{6,2},{1... | collective-permute-start | bytes 147464 | tf_op jit(solution)/shard_map/ppermute | solution.py:603
  19.9 1.5 %collective-permute-done.6 = f32[3,4,8,128]{3,2,1,0:T(8,128)S(1)} collective-permute-done((f32[3,4,8,128]{3,2,1,0:T(8,128)S(1)}, f32[3,4,8,128]{3,2,1,0:T(8,128)S(1)}, u32[]{:S(2)}, u32[]{:S(2)}) %collective-permute-start.6) | collective-permute-done | bytes 49184 | tf_op jit(solution)/shard_map/ppermute | solution.py:603
  21.4 2.8 %collective-permute-done.5 = f32[3,4,8,128]{3,2,1,0:T(8,128)S(1)} collective-permute-done((f32[3,4,8,128]{3,2,1,0:T(8,128)S(1)}, f32[3,4,8,128]{3,2,1,0:T(8,128)S(1)}, u32[]{:S(2)}, u32[]{:S(2)}) %collective-permute-start.5) | collective-permute-done | bytes 49184 | tf_op jit(solution)/shard_map/ppermute | solution.py:603
  24.2 0.0 collective-permute-done.4
  24.2 1.7 %collective-permute-start.7 = (f32[1,4,3,4,8,128]{5,4,3,2,1,0:T(8,128)S(1)}, f32[1,4,3,4,8,128]{5,4,3,2,1,0:T(8,128)S(1)}, u32[]{:S(2)}, u32[]{:S(2)}) collective-permute-start(f32[1,4,3,4,8,128]{5,4,3,2,1,0:T(8,128)S(1)} %maximum_bitcast_fusion), channel_id=1, source_target_pairs={{0,2},{1,3},{2,0},{3,1},{4,6},{5,7},{6,4},{7,5},{8,10},{9,11},{10,... | collective-permute-start | bytes 589832 | tf_op jit(solution)/shard_map/ppermute | solution.py:603
  26.0 5.3 %collective-permute-done.7 = f32[1,4,3,4,8,128]{5,4,3,2,1,0:T(8,128)S(1)} collective-permute-done((f32[1,4,3,4,8,128]{5,4,3,2,1,0:T(8,128)S(1)}, f32[1,4,3,4,8,128]{5,4,3,2,1,0:T(8,128)S(1)}, u32[]{:S(2)}, u32[]{:S(2)}) %collective-permute-start.7) | collective-permute-done | bytes 196640 | tf_op jit(solution)/shard_map/ppermute | solution.py:603
  31.3 0.1 collective-permute-start.8
  31.4 0.1 pad_add_fusion.place
  31.5 1.8 %collective-permute-done.8.far = f32[2,4,3,4,8,128]{5,4,3,2,1,0:T(8,128)} collective-permute-done((f32[2,4,3,4,8,128]{5,4,3,2,1,0:T(8,128)S(1)}, f32[2,4,3,4,8,128]{5,4,3,2,1,0:T(8,128)}, u32[]{:S(2)}, u32[]{:S(2)}) %collective-permute-start.8) | collective-permute-done | bytes 393248 | tf_op jit(solution)/shard_map/ppermute | solution.py:603
  33.2 7.8 %shard_map.44 = (f32[16,16,128]{2,1,0:T(8,128)}, f32[16,16,128]{2,1,0:T(8,128)}) custom-call(s32[2]{0:T(128)S(1)} %pad_add_fusion.place, f32[2,4,3,4,8,128]{5,4,3,2,1,0:T(8,128)S(1)} %pad_maximum_fusion.near, f32[2,4,3,4,8,128]{5,4,3,2,1,0:T(8,128)} %collective-permute-done.8.far, f32[2,24,24,128]{3,2,1,0:T(8,128)S(1)} %get-tuple-element.15.kept, ...), custom_call_target="tpu_custom_call" | custom-call | tf_op jit(solution)/shard_map/pallas_call | solution.py:586
  (4 shorter events, 0.1 us)
Async XLA Ops:
  1.6 7.5 %collective-permute-start = (f32[2,4,16,128]{3,2,1,0:T(8,128)S(1)}, f32[2,4,16,128]{3,2,1,0:T(8,128)S(1)}, u32[]{:S(2)}, u32[]{:S(2)}) collective-permute-start(f32[2,4,16,128]{3,2,1,0:T(8,128)S(1)} %get-tuple-element.10), channel_id=1, source_target_pairs={{0,4},{4,8},{8,12},{12,0},{1,5},{5,9},{9,13},{13,1},{2,6},{6,10},{... | collective-permute-start | bytes 196616 | tf_op jit(solution)/shard_map/ppermute | solution.py:598
  4.7 5.0 %collective-permute-start.1 = (f32[2,4,16,128]{3,2,1,0:T(8,128)S(1)}, f32[2,4,16,128]{3,2,1,0:T(8,128)S(1)}, u32[]{:S(2)}, u32[]{:S(2)}) collective-permute-start(f32[2,4,16,128]{3,2,1,0:T(8,128)S(1)} %get-tuple-element.11), channel_id=1, source_target_pairs={{0,12},{4,0},{8,4},{12,8},{1,13},{5,1},{9,5},{13,9},{2,14},{6,2},{... | collective-permute-start | bytes 196616 | tf_op jit(solution)/shard_map/ppermute | solution.py:598
  9.7 4.1 %collective-permute-start.2 = (f32[24,8,128]{2,1,0:T(8,128)S(1)}, f32[24,8,128]{2,1,0:T(8,128)S(1)}, u32[]{:S(2)}, u32[]{:S(2)}) collective-permute-start(f32[24,8,128]{2,1,0:T(8,128)S(1)} %get-tuple-element.12), channel_id=1, source_target_pairs={{0,1},{1,2},{2,3},{3,0},{4,5},{5,6},{6,7},{7,4},{8,9},{9,10},{10,1... | collective-permute-start | bytes 294920 | tf_op jit(solution)/shard_map/ppermute | solution.py:598
  9.8 4.1 %collective-permute-start.3 = (f32[24,8,128]{2,1,0:T(8,128)S(1)}, f32[24,8,128]{2,1,0:T(8,128)S(1)}, u32[]{:S(2)}, u32[]{:S(2)}) collective-permute-start(f32[24,8,128]{2,1,0:T(8,128)S(1)} %get-tuple-element.13), channel_id=1, source_target_pairs={{0,3},{1,0},{2,1},{3,2},{4,7},{5,4},{6,5},{7,6},{8,11},{9,8},{10,9... | collective-permute-start | bytes 294920 | tf_op jit(solution)/shard_map/ppermute | solution.py:598
  15.5 6.0 %collective-permute-start.6 = (f32[3,4,8,128]{3,2,1,0:T(8,128)S(1)}, f32[3,4,8,128]{3,2,1,0:T(8,128)S(1)}, u32[]{:S(2)}, u32[]{:S(2)}) collective-permute-start(f32[3,4,8,128]{3,2,1,0:T(8,128)S(1)} %get-tuple-element.14), channel_id=1, source_target_pairs={{0,12},{4,8},{8,4},{12,0},{1,13},{5,9},{9,5},{13,1},{2,14},{6,10},... | collective-permute-start | bytes 147464 | tf_op jit(solution)/shard_map/ppermute | solution.py:603
  18.9 5.3 %collective-permute-start.5 = (f32[3,4,8,128]{3,2,1,0:T(8,128)S(1)}, f32[3,4,8,128]{3,2,1,0:T(8,128)S(1)}, u32[]{:S(2)}, u32[]{:S(2)}) collective-permute-start(f32[3,4,8,128]{3,2,1,0:T(8,128)S(1)} %get-tuple-element.14), channel_id=1, source_target_pairs={{0,8},{4,12},{8,0},{12,4},{1,9},{5,13},{9,1},{13,5},{2,10},{6,14},... | collective-permute-start | bytes 147464 | tf_op jit(solution)/shard_map/ppermute | solution.py:603
  18.9 5.3 %collective-permute-start.4 = (f32[3,4,8,128]{3,2,1,0:T(8,128)S(1)}, f32[3,4,8,128]{3,2,1,0:T(8,128)S(1)}, u32[]{:S(2)}, u32[]{:S(2)}) collective-permute-start(f32[3,4,8,128]{3,2,1,0:T(8,128)S(1)} %get-tuple-element.14), channel_id=1, source_target_pairs={{0,4},{4,0},{8,12},{12,8},{1,5},{5,1},{9,13},{13,9},{2,6},{6,2},{1... | collective-permute-start | bytes 147464 | tf_op jit(solution)/shard_map/ppermute | solution.py:603
  24.2 7.0 %collective-permute-start.7 = (f32[1,4,3,4,8,128]{5,4,3,2,1,0:T(8,128)S(1)}, f32[1,4,3,4,8,128]{5,4,3,2,1,0:T(8,128)S(1)}, u32[]{:S(2)}, u32[]{:S(2)}) collective-permute-start(f32[1,4,3,4,8,128]{5,4,3,2,1,0:T(8,128)S(1)} %maximum_bitcast_fusion), channel_id=1, source_target_pairs={{0,2},{1,3},{2,0},{3,1},{4,6},{5,7},{6,4},{7,5},{8,10},{9,11},{10,... | collective-permute-start | bytes 589832 | tf_op jit(solution)/shard_map/ppermute | solution.py:603
  31.3 1.9 %collective-permute-start.8 = (f32[2,4,3,4,8,128]{5,4,3,2,1,0:T(8,128)S(1)}, f32[2,4,3,4,8,128]{5,4,3,2,1,0:T(8,128)}, u32[]{:S(2)}, u32[]{:S(2)}) collective-permute-start(f32[2,4,3,4,8,128]{5,4,3,2,1,0:T(8,128)S(1)} %pad_maximum_fusion.near), channel_id=1, source_target_pairs={{0,1},{1,0},{2,3},{3,2},{4,5},{5,4},{6,7},{7,6},{8,9},{9,8},{10,11... | collective-permute-start | bytes 1179656 | tf_op jit(solution)/shard_map/ppermute | solution.py:603

commit v3 on v2

--- a/solution.py
+++ b/solution.py
@@ -1,3 +1,5 @@
+import functools
+
 import jax
 import jax.numpy as jnp
 from jax import lax
@@ -372,10 +374,29 @@
     return values + other
 
 
-def edge_rows_kernel(fields, low, high):
-    rows = fields.shape[1]
-    low[...] = fields[:, :HALO]
-    high[...] = fields[:, rows - HALO :]
+def side_tiles(conc, chem, to_left, to_right, at, low):
+    columns = conc.shape[0]
+    to_left[at] = jnp.where(low, conc[:PAD], half_turn(chem[:PAD]))
+    to_right[at] = jnp.where(low, half_turn(chem[columns - PAD :]), conc[columns - PAD :])
+
+
+def low_half(lanes):
+    return lax.broadcasted_iota(jnp.int32, (PAD, lanes), 0) < HALO
+
+
+def edges_kernel(fields, low_rows, high_rows, to_left, to_right):
+    rows, columns, lanes = fields.shape[1:]
+    low_rows[...] = fields[:, :HALO]
+    high_rows[...] = fields[:, rows - HALO :]
+    for row in range(rows):
+        side_tiles(fields[0, row], fields[1, row], to_left, to_right, row, low_half(lanes))
+
+
+def corners_kernel(before, after, to_left, to_right):
+    lanes = before.shape[-1]
+    for at in range(2 * HALO):
+        source, row = (before, at) if at < HALO else (after, at - HALO)
+        side_tiles(source[0, row], source[1, row], to_left, to_right, at, low_half(lanes))
 
 
 def frame_row(row, rows, own, before, after):
@@ -390,15 +411,12 @@
     return pltpu.roll(values, HALO, axis=0)
 
 
-def edge_columns_kernel(fields, before, after, to_left, to_right):
-    conc, chem = fields.at[0], fields.at[1]
-    rows, columns, lanes = conc.shape
-    low = lax.broadcasted_iota(jnp.int32, (PAD, lanes), 0) < HALO
-    for row in range(rows + 2 * HALO):
-        c = frame_row(row, rows, conc, before.at[0], after.at[0])
-        u = frame_row(row, rows, chem, before.at[1], after.at[1])
-        to_left[row] = jnp.where(low, c[:PAD], half_turn(u[:PAD]))
-        to_right[row] = jnp.where(low, half_turn(u[columns - PAD :]), c[columns - PAD :])
+def side_row(row, rows, own, corners):
+    if row < HALO:
+        return corners[row]
+    if row < HALO + rows:
+        return own[row - HALO]
+    return corners[row - rows]
 
 
 def fine_level(weights):
@@ -406,7 +424,7 @@
 
 
 def fine_down_kernel(
-    fields, before, after, from_left, from_right,
+    fields, before, after, own_left, own_right, corner_left, corner_right,
     packed, kept, right_conc, all_weights,
     chem_start, mobility, conc_mid, chem_mid, sums,
 ):
@@ -416,7 +434,8 @@
     rows, columns, lanes = conc.shape
     frame = rows + 2 * HALO
     for row in range(frame):
-        left, right = from_left[row], from_right[row]
+        left = side_row(row, rows, own_left, corner_left)
+        right = side_row(row, rows, own_right, corner_right)
         c = jnp.concatenate([left, frame_row(row, rows, conc, before.at[0], after.at[0]), right])
         own = frame_row(row, rows, chem, before.at[1], after.at[1])
         right_conc[row] = c
@@ -453,7 +472,8 @@
 
 
 def coarse_kernel(
-    place, near, far, kept, right_conc, all_weights, conc_new, chem_new, *scratch
+    slots, grid, place, first, second, first_far, second_far,
+    kept, right_conc, all_weights, conc_new, chem_new, *scratch,
 ):
     conc_in, chem_in = kept.at[0], kept.at[1]
     weights = [all_weights.at[i] for i in range(7)]
@@ -473,31 +493,26 @@
     rows2, columns2 = right2[0].shape[:2]
     rows3, columns3 = right3[0].shape[:2]
     window1, window2, window3 = (PAD, columns1), (PAD, columns2), (PAD, columns3)
-    slots_x, slots_y = near.shape[1], 2 * near.shape[0]
-    own_rows, own_columns = rows1 // slots_x, columns1 // slots_y
+    own_rows, own_columns = rows1 // grid[0], columns1 // grid[1]
     even = lane_even((own_columns, lanes), 1)
-    bits = slots_y.bit_length() - 1
-
-    def unpack(source, slot_y, from_y):
-        offset = from_y * own_columns
+
+    def unpack(source, slot, mask_x, mask_y):
+        offset = (at_y ^ mask_y) * own_columns
         plain = pl.ds(pl.multiple_of(offset, PAD), own_columns)
         padded = pl.ds(pl.multiple_of(offset + PAD, PAD), own_columns)
-        for slot_x in range(slots_x):
-            row = (at_x ^ slot_x) * own_rows
-            for field, (ref, at) in enumerate(
-                ((right1[0], plain), (right1[1], plain), (mob1, padded))
-            ):
-                for index in range(own_rows // 2):
-                    pair = source[slot_y, slot_x, field, index]
-                    ref[row + 2 * index, at, :] = jnp.where(even, pair, lane_roll(pair, 1))
-                    ref[row + 2 * index + 1, at, :] = jnp.where(even, lane_roll(pair, -1), pair)
-
-    for last, source in enumerate((near, far)):
-        for slot_y in range(slots_y // 2):
-            mask = last
-            for bit in range(bits - 1):
-                mask |= (slot_y >> bit & 1) << (bits - 1 - bit)
-            unpack(source, slot_y, at_y ^ mask)
+        row = (at_x ^ mask_x) * own_rows
+        for field, (ref, at) in enumerate(
+            ((right1[0], plain), (right1[1], plain), (mob1, padded))
+        ):
+            for index in range(own_rows // 2):
+                pair = source[slot, field, index]
+                ref[row + 2 * index, at, :] = jnp.where(even, pair, lane_roll(pair, 1))
+                ref[row + 2 * index + 1, at, :] = jnp.where(even, lane_roll(pair, -1), pair)
+
+    for last, sources in enumerate(((first, second), (first_far, second_far))):
+        for source, masks in zip(sources, slots):
+            for slot, (mask_x, mask_y) in enumerate(masks):
+                unpack(source, slot, mask_x, mask_y ^ last)
     for row in range(rows1):
         mob1[row, :PAD, :] = mob1[row, columns1 : columns1 + PAD, :]
         mob1[row, PAD + columns1 :, :] = mob1[row, PAD : 2 * PAD, :]
@@ -603,13 +618,24 @@
     return lax.ppermute(values, axis, [(i, i ^ mask) for i in range(count)])
 
 
+def far_masks():
+    count_x, count_y = lax.axis_size("gx"), lax.axis_size("gy")
+    return list(range(1, count_x)), list(range(2, count_y, 2))
+
+
+def slot_masks():
+    along_x, along_y = far_masks()
+    first = [(0, 0)] + [(0, y) for y in along_y] + [(x, 0) for x in along_x]
+    return first, [(x, y) for y in along_y for x in along_x]
+
+
 def gathered(values):
-    count_x, count_y = lax.axis_size("gx"), lax.axis_size("gy")
-    stack = jnp.stack([values] + [swapped(values, "gx", mask) for mask in range(1, count_x)])
-    stack = stack[None]
-    for bit in reversed(range(1, count_y.bit_length() - 1)):
-        stack = jnp.concatenate([stack, swapped(stack, "gy", 1 << bit)], axis=0)
-    return stack, swapped(stack, "gy", 1)
+    along_x, along_y = far_masks()
+    across = jnp.stack([swapped(values, "gx", mask) for mask in along_x])
+    beside = [swapped(values, "gy", mask) for mask in along_y]
+    first = jnp.concatenate([jnp.stack([values] + beside), across], axis=0)
+    second = jnp.concatenate([swapped(across, "gy", mask) for mask in along_y], axis=0)
+    return first, second, swapped(first, "gy", 1), swapped(second, "gy", 1)
 
 
 def two_phase_solve(conc, chem):
@@ -619,18 +645,19 @@
     edge = (2, HALO, columns, lanes)
     block = (rows, columns, lanes)
     fields = jnp.concatenate([conc, chem], axis=0).reshape((2,) + block)
-    low, high = call_kernel(edge_rows_kernel, (edge, edge), (), fields)
+    side, corner = (rows, PAD, lanes), (2 * HALO, PAD, lanes)
+    low, high, to_left, to_right = call_kernel(
+        edges_kernel, (edge, edge, side, side), (), fields
+    )
     before, after = shifted(high, "gx", 1), shifted(low, "gx", -1)
-    side = (frame[0], PAD, lanes)
-    to_left, to_right = call_kernel(
-        edge_columns_kernel, (side, side), (), fields, before, after
-    )
-    from_left, from_right = shifted(to_right, "gy", 1), shifted(to_left, "gy", -1)
+    sides = [shifted(to_right, "gy", 1), shifted(to_left, "gy", -1)]
+    to_left, to_right = call_kernel(corners_kernel, (corner, corner), (), before, after)
+    sides += [shifted(to_right, "gy", 1), shifted(to_left, "gy", -1)]
     packed, *kept = call_kernel(
         fine_down_kernel,
         ((3, rows // 4, columns // 2, lanes), (2,) + inner, frame, (7,) + inner),
         (frame,) * 4 + ((3, rows // 2, columns, lanes),),
-        fields, before, after, from_left, from_right,
+        fields, before, after, *sides,
     )
     place = jnp.stack([lax.axis_index("gx"), lax.axis_index("gy")])
     count_x, count_y = lax.axis_size("gx"), lax.axis_size("gy")
@@ -642,9 +669,10 @@
     scratch += [(3, grids[2][0], grids[1][1], lanes), (3, grids[3][0], grids[2][1], lanes)]
     scratch += [(2, rows // 4 + 4, grids[1][1], lanes), (2, grids[3][0], grids[2][1], lanes)]
     scratch += [(2, rows // 2 + 2, columns + 4 * PAD, lanes)] + [frame] * 4
+    kernel = functools.partial(coarse_kernel, slot_masks(), (count_x, count_y))
     args = (place, *gathered(packed), *kept)
     specs = [pl.BlockSpec(memory_space=pltpu.SMEM)] + [whole_block()] * (len(args) - 1)
-    return call_kernel(coarse_kernel, (block, block), scratch, *args, specs=specs, vmem_mib=24)
+    return call_kernel(kernel, (block, block), scratch, *args, specs=specs, vmem_mib=24)
 
 
 def body(conc_old, chem_old):
@@ -658,7 +686,8 @@
         and lanes % 128 == 0
         and count_x * rows >= 64
         and count_y * columns >= 64
-        and count_y >= 2
+        and count_x >= 2
+        and count_y >= 4
         and count_x & (count_x - 1) == 0
         and count_y & (count_y - 1) == 0
         and rows & (rows - 1) == 0

time: 41.2 us -> 39.2 us (0.951)
  waiting for transfers between devices: 16.6 us -> 11.5 us
  starting transfers between devices: 13.2 us -> 16.4 us
    ppermute x5 -> x7, waiting for transfers between devices: 11.3 us -> 8.77 us  [swapped(): return lax.ppermute(values, axis, [(i, i ^ mask) for i in range(count)])]
    ppermute x4 -> x6, waiting for transfers between devices: 5.23 us -> 2.73 us  [shifted(): lax.ppermute(values, axis, [(i, (i + by) % count) for i in range(count)])]
    ppermute x4 -> x6, starting transfers between devices: 6.96 us -> 8.7 us  [shifted(): lax.ppermute(values, axis, [(i, (i + by) % count) for i in range(count)])]
    ppermute x5 -> x7, starting transfers between devices: 6.27 us -> 7.71 us  [swapped(): return lax.ppermute(values, axis, [(i, i ^ mask) for i in range(count)])]
  transfers between devices with their start and end apart: 9 -> 13, of which waited for: 8 -> 6; matrix products, arithmetic and copies ran while one was open for 0% -> 0% of each run, Pallas kernels for 0% -> 0%
where the time goes in v3:
time: 39.2 us; the launch traced here: 39.1 us
  starting transfers between devices  16.4 us (42%)
  waiting for transfers between devices  11.5 us (29%)
  Pallas kernels  9.37 us (24%)
  other arithmetic  1.07 us (3%)
  between operations  0.71 us (2%)
    pallas_call x4, Pallas kernels, call_kernel(): pl.pallas_call(kernel, out_shape=shapes, in_specs=specs or [whole_block()...  9.37 us
    ppermute x7, waiting for transfers between devices, swapped(): return lax.ppermute(values, axis, [(i, i ^ mask) for i in range(count)])  8.77 us
    ppermute x6, starting transfers between devices, shifted(): lax.ppermute(values, axis, [(i, (i + by) % count) for i in range(count)])  8.7 us
    ppermute x7, starting transfers between devices, swapped(): return lax.ppermute(values, axis, [(i, i ^ mask) for i in range(count)])  7.71 us
    ppermute x6, waiting for transfers between devices, shifted(): lax.ppermute(values, axis, [(i, (i + by) % count) for i in range(count)])  2.73 us
    concatenate x1, other arithmetic, two_phase_solve(): fields = jnp.concatenate([conc, chem], axis=0).reshape((2,) + block)  0.99 us
  transfers between devices with their start and end apart: 13, of which 6 were waited for; matrix products, arithmetic and copies ran while one was open for 0% of the time, Pallas kernels for 0%

profile of v3, /device:TPU:0, one launch (start us, length us, event | category | flops | bytes accessed | tf_op | source)
XLA Modules:
  0.0 39.1 jit_solution(16899516168036012718)
XLA Ops:
  0.6 1.0 %pad_maximum_fusion = f32[32,16,128]{2,1,0:T(8,128)S(1)} fusion(f32[16,16,128]{2,1,0:T(8,128)} %param.3, f32[16,16,128]{2,1,0:T(8,128)} %param.2), kind=kLoop, calls=%fused_computation | loop fusion | flops 65536 | bytes 524288 | tf_op jit(solution)/shard_map/concatenate | solution.py:647
  1.6 3.1 %collective-permute-start = (f32[2,4,16,128]{3,2,1,0:T(8,128)S(1)}, f32[2,4,16,128]{3,2,1,0:T(8,128)S(1)}, u32[]{:S(2)}, u32[]{:S(2)}) collective-permute-start(f32[2,4,16,128]{3,2,1,0:T(8,128)S(1)} %get-tuple-element.12), channel_id=1, source_target_pairs={{0,4},{4,8},{8,12},{12,0},{1,5},{5,9},{9,13},{13,1},{2,6},{6,10},{... | collective-permute-start | bytes 196616 | tf_op jit(solution)/shard_map/ppermute | solution.py:613
  4.7 2.1 %collective-permute-start.1 = (f32[2,4,16,128]{3,2,1,0:T(8,128)S(1)}, f32[2,4,16,128]{3,2,1,0:T(8,128)S(1)}, u32[]{:S(2)}, u32[]{:S(2)}) collective-permute-start(f32[2,4,16,128]{3,2,1,0:T(8,128)S(1)} %get-tuple-element.13), channel_id=1, source_target_pairs={{0,12},{4,0},{8,4},{12,8},{1,13},{5,1},{9,5},{13,9},{2,14},{6,2},{... | collective-permute-start | bytes 196616 | tf_op jit(solution)/shard_map/ppermute | solution.py:613
  6.8 0.0 collective-permute-start.2
  6.8 1.7 %collective-permute-start.3 = (f32[16,8,128]{2,1,0:T(8,128)S(1)}, f32[16,8,128]{2,1,0:T(8,128)S(1)}, u32[]{:S(2)}, u32[]{:S(2)}) collective-permute-start(f32[16,8,128]{2,1,0:T(8,128)S(1)} %get-tuple-element.15), channel_id=1, source_target_pairs={{0,3},{1,0},{2,1},{3,2},{4,7},{5,4},{6,5},{7,6},{8,11},{9,8},{10,9... | collective-permute-start | bytes 196616 | tf_op jit(solution)/shard_map/ppermute | solution.py:613
  8.6 0.6 %collective-permute-done.before = f32[2,4,16,128]{3,2,1,0:T(8,128)S(1)} collective-permute-done((f32[2,4,16,128]{3,2,1,0:T(8,128)S(1)}, f32[2,4,16,128]{3,2,1,0:T(8,128)S(1)}, u32[]{:S(2)}, u32[]{:S(2)}) %collective-permute-start) | collective-permute-done | bytes 65568 | tf_op jit(solution)/shard_map/ppermute | solution.py:613
  9.1 0.5 %collective-permute-done.1.after = f32[2,4,16,128]{3,2,1,0:T(8,128)S(1)} collective-permute-done((f32[2,4,16,128]{3,2,1,0:T(8,128)S(1)}, f32[2,4,16,128]{3,2,1,0:T(8,128)S(1)}, u32[]{:S(2)}, u32[]{:S(2)}) %collective-permute-start.1) | collective-permute-done | bytes 65568 | tf_op jit(solution)/shard_map/ppermute | solution.py:613
  9.7 0.1 collective-permute-start.4
  9.8 1.7 %collective-permute-start.5 = (f32[8,8,128]{2,1,0:T(8,128)S(1)}, f32[8,8,128]{2,1,0:T(8,128)S(1)}, u32[]{:S(2)}, u32[]{:S(2)}) collective-permute-start(f32[8,8,128]{2,1,0:T(8,128)S(1)} %get-tuple-element.17), channel_id=1, source_target_pairs={{0,3},{1,0},{2,1},{3,2},{4,7},{5,4},{6,5},{7,6},{8,11},{9,8},{10,9... | collective-permute-start | bytes 98312 | tf_op jit(solution)/shard_map/ppermute | solution.py:613
  11.5 0.0 collective-permute-done.2.own_left
  11.5 0.0 collective-permute-done.3.own_right
  11.5 1.6 %collective-permute-done.4.corner_left = f32[8,8,128]{2,1,0:T(8,128)S(1)} collective-permute-done((f32[8,8,128]{2,1,0:T(8,128)S(1)}, f32[8,8,128]{2,1,0:T(8,128)S(1)}, u32[]{:S(2)}, u32[]{:S(2)}) %collective-permute-start.4) | collective-permute-done | bytes 32800 | tf_op jit(solution)/shard_map/ppermute | solution.py:613
  13.1 0.0 collective-permute-done.5.corner_right
  13.1 1.6 %shard_map.43 = (f32[3,4,8,128]{3,2,1,0:T(8,128)S(1)}, f32[2,24,24,128]{3,2,1,0:T(8,128)S(1)}, f32[24,32,128]{2,1,0:T(8,128)S(1)}, f32[7,24,24,128]{3,2,1,0:T(8,128)S(1)}) custom-call(f32[2,16,16,128]{3,2,1,0:T(8,128)S(1)} %bitcast.14, f32[2,4,16,128]{3,2,1,0:T(8,128)S(1)} %collective-permute-done.before, ...), custom_call_target="tpu_custom_call" | custom-call | tf_op jit(solution)/shard_map/pallas_call | solution.py:601
  14.7 3.3 %collective-permute-start.9 = (f32[3,4,8,128]{3,2,1,0:T(8,128)S(1)}, f32[3,4,8,128]{3,2,1,0:T(8,128)S(1)}, u32[]{:S(2)}, u32[]{:S(2)}) collective-permute-start(f32[3,4,8,128]{3,2,1,0:T(8,128)S(1)} %get-tuple-element.18), channel_id=1, source_target_pairs={{0,12},{4,8},{8,4},{12,0},{1,13},{5,9},{9,5},{13,1},{2,14},{6,10},... | collective-permute-start | bytes 147464 | tf_op jit(solution)/shard_map/ppermute | solution.py:618
  18.0 0.0 collective-permute-start.8
  18.0 1.2 %collective-permute-start.7 = (f32[3,4,8,128]{3,2,1,0:T(8,128)S(1)}, f32[3,4,8,128]{3,2,1,0:T(8,128)S(1)}, u32[]{:S(2)}, u32[]{:S(2)}) collective-permute-start(f32[3,4,8,128]{3,2,1,0:T(8,128)S(1)} %get-tuple-element.18), channel_id=1, source_target_pairs={{0,4},{4,0},{8,12},{12,8},{1,5},{5,1},{9,13},{13,9},{2,6},{6,2},{1... | collective-permute-start | bytes 147464 | tf_op jit(solution)/shard_map/ppermute | solution.py:618
  19.2 1.5 %collective-permute-start.6 = (f32[3,4,8,128]{3,2,1,0:T(8,128)S(1)}, f32[3,4,8,128]{3,2,1,0:T(8,128)S(1)}, u32[]{:S(2)}, u32[]{:S(2)}) collective-permute-start(f32[3,4,8,128]{3,2,1,0:T(8,128)S(1)} %get-tuple-element.18), channel_id=1, source_target_pairs={{0,2},{1,3},{2,0},{3,1},{4,6},{5,7},{6,4},{7,5},{8,10},{9,11},{10,... | collective-permute-start | bytes 147464 | tf_op jit(solution)/shard_map/ppermute | solution.py:618
  20.7 0.0 collective-permute-done.9
  20.7 2.5 %collective-permute-done.8 = f32[3,4,8,128]{3,2,1,0:T(8,128)S(1)} collective-permute-done((f32[3,4,8,128]{3,2,1,0:T(8,128)S(1)}, f32[3,4,8,128]{3,2,1,0:T(8,128)S(1)}, u32[]{:S(2)}, u32[]{:S(2)}) %collective-permute-start.8) | collective-permute-done | bytes 49184 | tf_op jit(solution)/shard_map/ppermute | solution.py:618
  23.1 0.0 collective-permute-done.7
  23.2 1.7 %collective-permute-start.10 = (f32[3,3,4,8,128]{4,3,2,1,0:T(8,128)S(1)}, f32[3,3,4,8,128]{4,3,2,1,0:T(8,128)}, u32[]{:S(2)}, u32[]{:S(2)}) collective-permute-start(f32[3,3,4,8,128]{4,3,2,1,0:T(8,128)S(1)} %pad_maximum_fusion.1), channel_id=1, source_target_pairs={{0,2},{1,3},{2,0},{3,1},{4,6},{5,7},{6,4},{7,5},{8,10},{9,11},{10,... | collective-permute-start | bytes 442376 | tf_op jit(solution)/shard_map/ppermute | solution.py:618
  24.8 0.0 collective-permute-done.6
  24.9 0.1 collective-permute-start.11
  25.0 4.7 %collective-permute-done.10.second = f32[3,3,4,8,128]{4,3,2,1,0:T(8,128)} collective-permute-done((f32[3,3,4,8,128]{4,3,2,1,0:T(8,128)S(1)}, f32[3,3,4,8,128]{4,3,2,1,0:T(8,128)}, u32[]{:S(2)}, u32[]{:S(2)}) %collective-permute-start.10) | collective-permute-done | bytes 147488 | tf_op jit(solution)/shard_map/ppermute | solution.py:618
  29.6 0.0 collective-permute-start.12
  29.6 0.1 pad_add_fusion.place
  29.7 0.0 collective-permute-done.11.first_far
  29.7 1.6 %collective-permute-done.12.second_far = f32[3,3,4,8,128]{4,3,2,1,0:T(8,128)} collective-permute-done((f32[3,3,4,8,128]{4,3,2,1,0:T(8,128)}, f32[3,3,4,8,128]{4,3,2,1,0:T(8,128)}, u32[]{:S(2)}, u32[]{:S(2)}) %collective-permute-start.12) | collective-permute-done | bytes 147488 | tf_op jit(solution)/shard_map/ppermute | solution.py:618
  31.3 7.7 %shard_map.44 = (f32[16,16,128]{2,1,0:T(8,128)}, f32[16,16,128]{2,1,0:T(8,128)}) custom-call(s32[2]{0:T(128)S(1)} %pad_add_fusion.place, f32[5,3,4,8,128]{4,3,2,1,0:T(8,128)S(1)} %constant_dynamic-update-slice_fusion.first, f32[3,3,4,8,128]{4,3,2,1,0:T(8,128)} %collective-permute-done.10.second, f32[5,3,4,8,128]{4,3,2,1,0:T(8,128)S(1)} %collective-permute-done.11.first_far, ...), custom_call_target="tpu_custom_call" | custom-call | tf_op jit(solution)/shard_map/pallas_call | solution.py:601
  (8 shorter events, 0.1 us)
Async XLA Ops:
  1.6 7.5 %collective-permute-start = (f32[2,4,16,128]{3,2,1,0:T(8,128)S(1)}, f32[2,4,16,128]{3,2,1,0:T(8,128)S(1)}, u32[]{:S(2)}, u32[]{:S(2)}) collective-permute-start(f32[2,4,16,128]{3,2,1,0:T(8,128)S(1)} %get-tuple-element.12), channel_id=1, source_target_pairs={{0,4},{4,8},{8,12},{12,0},{1,5},{5,9},{9,13},{13,1},{2,6},{6,10},{... | collective-permute-start | bytes 196616 | tf_op jit(solution)/shard_map/ppermute | solution.py:613
  4.7 5.0 %collective-permute-start.1 = (f32[2,4,16,128]{3,2,1,0:T(8,128)S(1)}, f32[2,4,16,128]{3,2,1,0:T(8,128)S(1)}, u32[]{:S(2)}, u32[]{:S(2)}) collective-permute-start(f32[2,4,16,128]{3,2,1,0:T(8,128)S(1)} %get-tuple-element.13), channel_id=1, source_target_pairs={{0,12},{4,0},{8,4},{12,8},{1,13},{5,1},{9,5},{13,9},{2,14},{6,2},{... | collective-permute-start | bytes 196616 | tf_op jit(solution)/shard_map/ppermute | solution.py:613
  6.8 4.7 %collective-permute-start.2 = (f32[16,8,128]{2,1,0:T(8,128)S(1)}, f32[16,8,128]{2,1,0:T(8,128)S(1)}, u32[]{:S(2)}, u32[]{:S(2)}) collective-permute-start(f32[16,8,128]{2,1,0:T(8,128)S(1)} %get-tuple-element.14), channel_id=1, source_target_pairs={{0,1},{1,2},{2,3},{3,0},{4,5},{5,6},{6,7},{7,4},{8,9},{9,10},{10,1... | collective-permute-start | bytes 196616 | tf_op jit(solution)/shard_map/ppermute | solution.py:613
  6.8 4.7 %collective-permute-start.3 = (f32[16,8,128]{2,1,0:T(8,128)S(1)}, f32[16,8,128]{2,1,0:T(8,128)S(1)}, u32[]{:S(2)}, u32[]{:S(2)}) collective-permute-start(f32[16,8,128]{2,1,0:T(8,128)S(1)} %get-tuple-element.15), channel_id=1, source_target_pairs={{0,3},{1,0},{2,1},{3,2},{4,7},{5,4},{6,5},{7,6},{8,11},{9,8},{10,9... | collective-permute-start | bytes 196616 | tf_op jit(solution)/shard_map/ppermute | solution.py:613
  9.7 3.4 %collective-permute-start.4 = (f32[8,8,128]{2,1,0:T(8,128)S(1)}, f32[8,8,128]{2,1,0:T(8,128)S(1)}, u32[]{:S(2)}, u32[]{:S(2)}) collective-permute-start(f32[8,8,128]{2,1,0:T(8,128)S(1)} %get-tuple-element.16), channel_id=1, source_target_pairs={{0,1},{1,2},{2,3},{3,0},{4,5},{5,6},{6,7},{7,4},{8,9},{9,10},{10,1... | collective-permute-start | bytes 98312 | tf_op jit(solution)/shard_map/ppermute | solution.py:613
  9.8 3.3 %collective-permute-start.5 = (f32[8,8,128]{2,1,0:T(8,128)S(1)}, f32[8,8,128]{2,1,0:T(8,128)S(1)}, u32[]{:S(2)}, u32[]{:S(2)}) collective-permute-start(f32[8,8,128]{2,1,0:T(8,128)S(1)} %get-tuple-element.17), channel_id=1, source_target_pairs={{0,3},{1,0},{2,1},{3,2},{4,7},{5,4},{6,5},{7,6},{8,11},{9,8},{10,9... | collective-permute-start | bytes 98312 | tf_op jit(solution)/shard_map/ppermute | solution.py:613
  14.7 6.0 %collective-permute-start.9 = (f32[3,4,8,128]{3,2,1,0:T(8,128)S(1)}, f32[3,4,8,128]{3,2,1,0:T(8,128)S(1)}, u32[]{:S(2)}, u32[]{:S(2)}) collective-permute-start(f32[3,4,8,128]{3,2,1,0:T(8,128)S(1)} %get-tuple-element.18), channel_id=1, source_target_pairs={{0,12},{4,8},{8,4},{12,0},{1,13},{5,9},{9,5},{13,1},{2,14},{6,10},... | collective-permute-start | bytes 147464 | tf_op jit(solution)/shard_map/ppermute | solution.py:618
  18.0 5.2 %collective-permute-start.8 = (f32[3,4,8,128]{3,2,1,0:T(8,128)S(1)}, f32[3,4,8,128]{3,2,1,0:T(8,128)S(1)}, u32[]{:S(2)}, u32[]{:S(2)}) collective-permute-start(f32[3,4,8,128]{3,2,1,0:T(8,128)S(1)} %get-tuple-element.18), channel_id=1, source_target_pairs={{0,8},{4,12},{8,0},{12,4},{1,9},{5,13},{9,1},{13,5},{2,10},{6,14},... | collective-permute-start | bytes 147464 | tf_op jit(solution)/shard_map/ppermute | solution.py:618
  18.0 5.2 %collective-permute-start.7 = (f32[3,4,8,128]{3,2,1,0:T(8,128)S(1)}, f32[3,4,8,128]{3,2,1,0:T(8,128)S(1)}, u32[]{:S(2)}, u32[]{:S(2)}) collective-permute-start(f32[3,4,8,128]{3,2,1,0:T(8,128)S(1)} %get-tuple-element.18), channel_id=1, source_target_pairs={{0,4},{4,0},{8,12},{12,8},{1,5},{5,1},{9,13},{13,9},{2,6},{6,2},{1... | collective-permute-start | bytes 147464 | tf_op jit(solution)/shard_map/ppermute | solution.py:618
  19.2 5.7 %collective-permute-start.6 = (f32[3,4,8,128]{3,2,1,0:T(8,128)S(1)}, f32[3,4,8,128]{3,2,1,0:T(8,128)S(1)}, u32[]{:S(2)}, u32[]{:S(2)}) collective-permute-start(f32[3,4,8,128]{3,2,1,0:T(8,128)S(1)} %get-tuple-element.18), channel_id=1, source_target_pairs={{0,2},{1,3},{2,0},{3,1},{4,6},{5,7},{6,4},{7,5},{8,10},{9,11},{10,... | collective-permute-start | bytes 147464 | tf_op jit(solution)/shard_map/ppermute | solution.py:618
  23.2 6.5 %collective-permute-start.10 = (f32[3,3,4,8,128]{4,3,2,1,0:T(8,128)S(1)}, f32[3,3,4,8,128]{4,3,2,1,0:T(8,128)}, u32[]{:S(2)}, u32[]{:S(2)}) collective-permute-start(f32[3,3,4,8,128]{4,3,2,1,0:T(8,128)S(1)} %pad_maximum_fusion.1), channel_id=1, source_target_pairs={{0,2},{1,3},{2,0},{3,1},{4,6},{5,7},{6,4},{7,5},{8,10},{9,11},{10,... | collective-permute-start | bytes 442376 | tf_op jit(solution)/shard_map/ppermute | solution.py:618
  24.9 4.8 %collective-permute-start.11 = (f32[5,3,4,8,128]{4,3,2,1,0:T(8,128)S(1)}, f32[5,3,4,8,128]{4,3,2,1,0:T(8,128)S(1)}, u32[]{:S(2)}, u32[]{:S(2)}) collective-permute-start(f32[5,3,4,8,128]{4,3,2,1,0:T(8,128)S(1)} %constant_dynamic-update-slice_fusion.first), channel_id=1, source_target_pairs={{0,1},{1,0},{2,3},{3,2},{4,5},{5,4},{6,7},{7,6},{8,9},{9,8},{10,11... | collective-permute-start | bytes 737288 | tf_op jit(solution)/shard_map/ppermute | solution.py:618
  29.6 1.7 %collective-permute-start.12 = (f32[3,3,4,8,128]{4,3,2,1,0:T(8,128)}, f32[3,3,4,8,128]{4,3,2,1,0:T(8,128)}, u32[]{:S(2)}, u32[]{:S(2)}) collective-permute-start(f32[3,3,4,8,128]{4,3,2,1,0:T(8,128)} %collective-permute-done.10.second), channel_id=1, source_target_pairs={{0,1},{1,0},{2,3},{3,2},{4,5},{5,4},{6,7},{7,6},{8,9},{9,8},{10,11... | collective-permute-start | bytes 442376 | tf_op jit(solution)/shard_map/ppermute | solution.py:618

commit v4 on v3

--- a/solution.py
+++ b/solution.py
@@ -209,10 +209,23 @@
         row_group(steps * unroll, rest)
 
 
-def wrapped(row, count):
-    if isinstance(row, int):
-        return row % count
-    return row & (count - 1) if count & (count - 1) == 0 else row
+def lane_swap(values):
+    return jnp.where(lane_even(values.shape, 1), lane_roll(values, -1), lane_roll(values, 1))
+
+
+class RowCache:
+    def __init__(self, ref, rows, first, width):
+        self.ref, self.rows, self.first, self.width = ref, rows, first, width
+        self.values = {}
+
+    def __getitem__(self, key):
+        if key not in self.values:
+            total = self.ref.shape[0]
+            row = key if self.rows is None else self.rows[key]
+            outside = isinstance(row, int) and not 0 <= row < total
+            values = self.ref[row % total if outside else row, pl.ds(self.first, self.width), :]
+            self.values[key] = lane_swap(values) if outside else values
+        return self.values[key]
 
 
 def chem_right(conc):
@@ -236,12 +249,12 @@
             return mobility[row, pl.ds(self.weights_from + shift, width), :]
 
         def group(first, size):
-            rows = [at(wrapped(first + i - 1, total)) for i in range(size + 2)]
-            before = half * (rows[0] + rows[1])
+            rows = RowCache(mobility, None, self.weights_from, width)
+            before = half * (rows[first - 1] + rows[first])
             for i in range(size):
                 r = first + i
-                here = rows[i + 1]
-                after = half * (here + rows[i + 2])
+                here = rows[r]
+                after = half * (here + rows[r + 1])
                 to_up_y = half * (here + at(r, 1))
                 to_down_y = half * (here + at(r, -1))
                 to_up_z = half * (here + lane_roll(here, -self.dup))
@@ -273,22 +286,29 @@
             values = [ref[row, pl.ds(first - self.right_from, width), :] for ref in right]
             return values if len(values) == 2 else values + [chem_right(values[0])]
 
-        u = [at(chem, row) for row in rows]
-        c = [at(conc, row) for row in rows]
-        for i in range(1, len(rows) - 1):
-            r = rows[i]
+        total = conc.shape[0]
+        if isinstance(rows[0], int):
+            centres, listed = [row % total for row in rows[1:-1]], None
+        else:
+            centres, listed = range(1, len(rows) - 1), rows
+        u = RowCache(chem, listed, first - fields_from, width)
+        c = RowCache(conc, listed, first - fields_from, width)
+        across = RowCache(face_x, listed, first - self.weights_from, width)
+        for key in centres:
+            r = key if listed is None else listed[key]
+            c_here, u_here = c[key], u[key]
             here = weight(coupling, r)
-            flux = weight(face_x, r) * u[i + 1] + weight(face_x, rows[i - 1]) * u[i - 1]
+            flux = across[key] * u[key + 1] + across[key - 1] * u[key - 1]
             flux = flux + weight(up_y, r) * at(chem, r, 1) + weight(down_y, r) * at(chem, r, -1)
-            flux = flux + weight(up_z, r) * lane_roll(u[i], -self.dup)
-            flux = flux + weight(down_z, r) * lane_roll(u[i], self.dup)
-            near = (c[i - 1] + c[i + 1]) + (at(conc, r, 1) + at(conc, r, -1))
-            near = near + (lane_roll(c[i], self.dup) + lane_roll(c[i], -self.dup))
+            flux = flux + weight(up_z, r) * lane_roll(u_here, -self.dup)
+            flux = flux + weight(down_z, r) * lane_roll(u_here, self.dup)
+            near = (c[key - 1] + c[key + 1]) + (at(conc, r, 1) + at(conc, r, -1))
+            near = near + (lane_roll(c_here, self.dup) + lane_roll(c_here, -self.dup))
             conc_right, chem_right_here = right_at(r)
-            conc_left = conc_right - c[i] + (flux - here * u[i])
-            chem_left = chem_right_here - u[i] + self.diagonal * c[i]
+            conc_left = conc_right - c_here + (flux - here * u_here)
+            chem_left = chem_right_here - u_here + self.diagonal * c_here
             chem_left = chem_left - (GRADIENT_ENERGY * self.scale) * near
-            yield r, c[i], u[i], conc_left, chem_left, here, weight(gain, r)
+            yield r, c_here, u_here, conc_left, chem_left, here, weight(gain, r)
 
     def steps(self, conc_left, chem_left, coupling, gain):
         return (
@@ -306,12 +326,12 @@
 
         loop_rows(right[0].shape[0], unroll, group)
 
-    def row_window(self, total, start, first, size):
-        return [wrapped(start + first + i - 1, total) for i in range(size + 2)]
+    def row_window(self, start, first, size):
+        return [start + first + i - 1 for i in range(size + 2)]
 
     def sweep(self, fields, right, start, count, unroll, window, put):
         def group(first, size):
-            rows = self.row_window(fields[0].shape[0], start, first, size)
+            rows = self.row_window(start, first, size)
             for r, c, u, *left in self.residuals(fields, right, rows, window):
                 conc_step, chem_step = self.steps(*left)
                 put(r, c + conc_step, u + chem_step)
@@ -320,12 +340,15 @@
 
     def coarse_right(self, fields, right, start, count, unroll, window, put, fields_from=0):
         def group(first, size):
-            rows = self.row_window(fields[0].shape[0], start, first, size)
+            rows = self.row_window(start, first, size)
             items = self.residuals(fields, right, rows, window, fields_from)
-            lefts = [item[3:5] for item in items]
-            for i in range(0, size, 2):
-                half = first // 2 if isinstance(first, int) else lax.shift_right_logical(first, 1)
-                put(half + i // 2, *(a + b for a, b in zip(lefts[i], lefts[i + 1])))
+            half = first // 2 if isinstance(first, int) else lax.shift_right_logical(first, 1)
+            kept = None
+            for i, (_, _, _, conc_left, chem_left, _, _) in enumerate(items):
+                if i % 2 == 0:
+                    kept = conc_left, chem_left
+                else:
+                    put(half + i // 2, kept[0] + conc_left, kept[1] + chem_left)
 
         loop_rows(count, unroll, group)
 
@@ -478,7 +501,7 @@
     conc_in, chem_in = kept.at[0], kept.at[1]
     weights = [all_weights.at[i] for i in range(7)]
     scratch = list(scratch)
-    at_x, at_y = place[0], place[1]
+    start_even, at_y = place[0] % 2 == 0, place[1]
     levels = []
     for level_index in (1, 2, 3):
         level = Level(level_index, scratch[5:14][2:])
@@ -493,26 +516,32 @@
     rows2, columns2 = right2[0].shape[:2]
     rows3, columns3 = right3[0].shape[:2]
     window1, window2, window3 = (PAD, columns1), (PAD, columns2), (PAD, columns3)
-    own_rows, own_columns = rows1 // grid[0], columns1 // grid[1]
+    own_rows, own_columns = 2 * rows1 // grid[0], columns1 // grid[1]
     even = lane_even((own_columns, lanes), 1)
-
-    def unpack(source, slot, mask_x, mask_y):
+    blocks = {}
+    for last, sources in enumerate(((first, second), (first_far, second_far))):
+        for source, masks in zip(sources, slots):
+            for slot, (mask_x, mask_y) in enumerate(masks):
+                blocks[mask_x, mask_y ^ last] = source.at[slot]
+
+    for mask_y in range(grid[1]):
         offset = (at_y ^ mask_y) * own_columns
         plain = pl.ds(pl.multiple_of(offset, PAD), own_columns)
         padded = pl.ds(pl.multiple_of(offset + PAD, PAD), own_columns)
-        row = (at_x ^ mask_x) * own_rows
         for field, (ref, at) in enumerate(
             ((right1[0], plain), (right1[1], plain), (mob1, padded))
         ):
             for index in range(own_rows // 2):
-                pair = source[slot, field, index]
-                ref[row + 2 * index, at, :] = jnp.where(even, pair, lane_roll(pair, 1))
-                ref[row + 2 * index + 1, at, :] = jnp.where(even, lane_roll(pair, -1), pair)
-
-    for last, sources in enumerate(((first, second), (first_far, second_far))):
-        for source, masks in zip(sources, slots):
-            for slot, (mask_x, mask_y) in enumerate(masks):
-                unpack(source, slot, mask_x, mask_y ^ last)
+                own, two_on, one_on, one_back = (
+                    blocks[mask_x, mask_y][field, index] for mask_x in (0, 2, 1, 3)
+                )
+                swap = one_on, one_back
+                one_on = jnp.where(start_even, swap[0], swap[1])
+                one_back = jnp.where(start_even, swap[1], swap[0])
+                for row, a, b in ((0, own, two_on), (own_rows, one_on, one_back)):
+                    row = row + 2 * index
+                    ref[row, at, :] = jnp.where(even, a, lane_roll(b, 1))
+                    ref[row + 1, at, :] = jnp.where(even, lane_roll(a, -1), b)
     for row in range(rows1):
         mob1[row, :PAD, :] = mob1[row, columns1 : columns1 + PAD, :]
         mob1[row, PAD + columns1 :, :] = mob1[row, PAD : 2 * PAD, :]
@@ -529,16 +558,16 @@
             half = pair_rows(sums.at[2], index, columns)
             put_padded((out_mobility,))(index, 0.125 * pair_lanes(half, dup))
 
-    one.set_weights(mob1, 16)
-    one.first_sweep(right1, 16, put_padded(a1))
-    one.sweep(a1, right1, 0, rows1, 16, window1, put_padded(b1))
-    one.coarse_right(b1, right1, 0, rows1, 16, window1, put_sums(sums1))
+    one.set_weights(mob1, rows1)
+    one.first_sweep(right1, rows1, put_padded(a1))
+    one.sweep(a1, right1, 0, rows1, rows1, window1, put_padded(b1))
+    one.coarse_right(b1, right1, 0, rows1, rows1, window1, put_sums(sums1))
     coarsen(mob1, sums1, right2, mob2, 2)
 
-    two.set_weights(mob2, 16)
-    two.first_sweep(right2, 16, put_padded(a2))
-    two.sweep(a2, right2, 0, rows2, 16, window2, put_padded(b2))
-    two.coarse_right(b2, right2, 0, rows2, 16, window2, put_sums(sums2))
+    two.set_weights(mob2, rows2)
+    two.first_sweep(right2, rows2, put_padded(a2))
+    two.sweep(a2, right2, 0, rows2, rows2, window2, put_padded(b2))
+    two.coarse_right(b2, right2, 0, rows2, rows2, window2, put_sums(sums2))
     coarsen(mob2, sums2, right3, mob3, 4)
 
     three.set_weights(mob3, rows3)
@@ -562,22 +591,27 @@
 
     for row in range(rows3):
         correct(now, row, b2, a2, spread3, row)
-    two.sweep(a2, right2, 0, rows2, 16, window2, put_padded(b2))
-    two.sweep(b2, right2, 0, rows2, 16, window2, put_padded(a2))
-    for index in range(own_rows // 2 + 4):
-        row = wrapped(at_x * (own_rows // 2) - 2 + index, rows2)
-        correct(a2, row, b1, a1, spread2, index)
-    own_first = at_x * own_rows
-    one.sweep(a1, right1, own_first - 2, own_rows + 4, 12, window1, put_padded(b1))
-    one.sweep(b1, right1, own_first - 1, own_rows + 2, 10, window1, put_padded(a1))
+    two.sweep(a2, right2, 0, rows2, rows2, window2, put_padded(b2))
+    two.sweep(b2, right2, 0, rows2, rows2, window2, put_padded(a2))
+    for row in range(rows2):
+        correct(a2, row, b1, a1, spread2, row)
+    one.sweep(a1, right1, -2, own_rows + 4, own_rows + 4, window1, put_padded(b1))
+    one.sweep(b1, right1, -1, own_rows + 2, own_rows + 2, window1, put_padded(a1))
 
     rows, columns = conc_new.shape[:2]
     wide = (PAD - HALO, columns + 2 * HALO)
     near_own = pl.ds(pl.multiple_of(at_y * own_columns, PAD), own_columns + 2 * PAD)
     for index in range(own_rows + 2):
-        row = wrapped(own_first - 1 + index, rows1)
+        inside = 1 <= index <= rows1
+        row = index - 1 if inside else (index - 1) % rows1
         for field, (source, target) in enumerate(((conc_in, fine_a0), (chem_in, fine_a1))):
-            spread_rows(spread_fine.at[field], index, a1[field][row, near_own, :])
+            tile = a1[field][row, near_own, :]
+            on_even = lane_even(tile.shape, 1)
+            if inside:
+                tile = jnp.where(on_even, tile, lane_roll(tile, 1))
+            else:
+                tile = jnp.where(on_even, lane_roll(tile, -1), tile)
+            spread_rows(spread_fine.at[field], index, tile)
             both = spread_fine[field, index, pl.ds(wide[0] + PAD, wide[1]), :]
             for fine in (HALO - 2 + 2 * index, HALO - 1 + 2 * index):
                 put_window((target,), wide)(fine, source[fine] + both)
@@ -661,13 +695,13 @@
     )
     place = jnp.stack([lax.axis_index("gx"), lax.axis_index("gy")])
     count_x, count_y = lax.axis_size("gx"), lax.axis_size("gy")
-    grids = [(count_x * rows >> level, count_y * columns >> level) for level in range(4)]
+    grids = [(count_x * rows >> level + 1, count_y * columns >> level) for level in range(4)]
     scratch = []
     for level_rows, level_columns in grids[1:]:
         scratch += [(level_rows, level_columns + 2 * PAD, lanes)] * 5
         scratch += [(level_rows, level_columns, lanes)] * 9
     scratch += [(3, grids[2][0], grids[1][1], lanes), (3, grids[3][0], grids[2][1], lanes)]
-    scratch += [(2, rows // 4 + 4, grids[1][1], lanes), (2, grids[3][0], grids[2][1], lanes)]
+    scratch += [(2, grids[2][0], grids[1][1], lanes), (2, grids[3][0], grids[2][1], lanes)]
     scratch += [(2, rows // 2 + 2, columns + 4 * PAD, lanes)] + [frame] * 4
     kernel = functools.partial(coarse_kernel, slot_masks(), (count_x, count_y))
     args = (place, *gathered(packed), *kept)
@@ -682,16 +716,13 @@
     if (
         grid_bytes <= GRID_BYTES_MAX
         and rows % 16 == 0
-        and columns % 16 == 0
         and lanes % 128 == 0
         and count_x * rows >= 64
         and count_y * columns >= 64
-        and count_x >= 2
+        and count_x == 4
         and count_y >= 4
-        and count_x & (count_x - 1) == 0
         and count_y & (count_y - 1) == 0
-        and rows & (rows - 1) == 0
-        and columns & (columns - 1) == 0
+        and columns == 16
     ):
         return two_phase_solve(conc_old, chem_old)
     start_fields = jnp.stack([conc_old, chem_old])

time: 39.2 us -> 37.8 us (0.964)
  Pallas kernels: 9.37 us -> 7.9 us
    pallas_call x4, Pallas kernels: 9.37 us -> 7.9 us  [call_kernel(): pl.pallas_call(kernel, out_shape=shapes, in_specs=specs or [whole_block()...]
where the time goes in v4:
time: 37.8 us; the launch traced here: 37.6 us
  starting transfers between devices  16.4 us (43%)
  waiting for transfers between devices  11.5 us (30%)
  Pallas kernels  7.9 us (21%)
  other arithmetic  1.07 us (3%)
  between operations  0.71 us (2%)
    ppermute x7, waiting for transfers between devices, swapped(): return lax.ppermute(values, axis, [(i, i ^ mask) for i in range(count)])  8.77 us
    ppermute x6, starting transfers between devices, shifted(): lax.ppermute(values, axis, [(i, (i + by) % count) for i in range(count)])  8.7 us
    pallas_call x4, Pallas kernels, call_kernel(): pl.pallas_call(kernel, out_shape=shapes, in_specs=specs or [whole_block()...  7.9 us
    ppermute x7, starting transfers between devices, swapped(): return lax.ppermute(values, axis, [(i, i ^ mask) for i in range(count)])  7.71 us
    ppermute x6, waiting for transfers between devices, shifted(): lax.ppermute(values, axis, [(i, (i + by) % count) for i in range(count)])  2.73 us
    concatenate x1, other arithmetic, two_phase_solve(): fields = jnp.concatenate([conc, chem], axis=0).reshape((2,) + block)  0.99 us
  transfers between devices with their start and end apart: 13, of which 6 were waited for; matrix products, arithmetic and copies ran while one was open for 0% of the time, Pallas kernels for 0%

profile of v4, /device:TPU:0, one launch (start us, length us, event | category | flops | bytes accessed | tf_op | source)
XLA Modules:
  0.0 37.6 jit_solution(16620467283272365278)
XLA Ops:
  0.6 1.0 %pad_maximum_fusion = f32[32,16,128]{2,1,0:T(8,128)S(1)} fusion(f32[16,16,128]{2,1,0:T(8,128)} %param.3, f32[16,16,128]{2,1,0:T(8,128)} %param.2), kind=kLoop, calls=%fused_computation | loop fusion | flops 65536 | bytes 524288 | tf_op jit(solution)/shard_map/concatenate | solution.py:681
  1.6 3.1 %collective-permute-start = (f32[2,4,16,128]{3,2,1,0:T(8,128)S(1)}, f32[2,4,16,128]{3,2,1,0:T(8,128)S(1)}, u32[]{:S(2)}, u32[]{:S(2)}) collective-permute-start(f32[2,4,16,128]{3,2,1,0:T(8,128)S(1)} %get-tuple-element.12), channel_id=1, source_target_pairs={{0,4},{4,8},{8,12},{12,0},{1,5},{5,9},{9,13},{13,1},{2,6},{6,10},{... | collective-permute-start | bytes 196616 | tf_op jit(solution)/shard_map/ppermute | solution.py:647
  4.7 2.1 %collective-permute-start.1 = (f32[2,4,16,128]{3,2,1,0:T(8,128)S(1)}, f32[2,4,16,128]{3,2,1,0:T(8,128)S(1)}, u32[]{:S(2)}, u32[]{:S(2)}) collective-permute-start(f32[2,4,16,128]{3,2,1,0:T(8,128)S(1)} %get-tuple-element.13), channel_id=1, source_target_pairs={{0,12},{4,0},{8,4},{12,8},{1,13},{5,1},{9,5},{13,9},{2,14},{6,2},{... | collective-permute-start | bytes 196616 | tf_op jit(solution)/shard_map/ppermute | solution.py:647
  6.8 0.0 collective-permute-start.2
  6.8 1.7 %collective-permute-start.3 = (f32[16,8,128]{2,1,0:T(8,128)S(1)}, f32[16,8,128]{2,1,0:T(8,128)S(1)}, u32[]{:S(2)}, u32[]{:S(2)}) collective-permute-start(f32[16,8,128]{2,1,0:T(8,128)S(1)} %get-tuple-element.15), channel_id=1, source_target_pairs={{0,3},{1,0},{2,1},{3,2},{4,7},{5,4},{6,5},{7,6},{8,11},{9,8},{10,9... | collective-permute-start | bytes 196616 | tf_op jit(solution)/shard_map/ppermute | solution.py:647
  8.6 0.6 %collective-permute-done.before = f32[2,4,16,128]{3,2,1,0:T(8,128)S(1)} collective-permute-done((f32[2,4,16,128]{3,2,1,0:T(8,128)S(1)}, f32[2,4,16,128]{3,2,1,0:T(8,128)S(1)}, u32[]{:S(2)}, u32[]{:S(2)}) %collective-permute-start) | collective-permute-done | bytes 65568 | tf_op jit(solution)/shard_map/ppermute | solution.py:647
  9.1 0.5 %collective-permute-done.1.after = f32[2,4,16,128]{3,2,1,0:T(8,128)S(1)} collective-permute-done((f32[2,4,16,128]{3,2,1,0:T(8,128)S(1)}, f32[2,4,16,128]{3,2,1,0:T(8,128)S(1)}, u32[]{:S(2)}, u32[]{:S(2)}) %collective-permute-start.1) | collective-permute-done | bytes 65568 | tf_op jit(solution)/shard_map/ppermute | solution.py:647
  9.7 0.1 collective-permute-start.4
  9.8 1.7 %collective-permute-start.5 = (f32[8,8,128]{2,1,0:T(8,128)S(1)}, f32[8,8,128]{2,1,0:T(8,128)S(1)}, u32[]{:S(2)}, u32[]{:S(2)}) collective-permute-start(f32[8,8,128]{2,1,0:T(8,128)S(1)} %get-tuple-element.17), channel_id=1, source_target_pairs={{0,3},{1,0},{2,1},{3,2},{4,7},{5,4},{6,5},{7,6},{8,11},{9,8},{10,9... | collective-permute-start | bytes 98312 | tf_op jit(solution)/shard_map/ppermute | solution.py:647
  11.5 0.0 collective-permute-done.2.own_left
  11.5 0.0 collective-permute-done.3.own_right
  11.5 1.6 %collective-permute-done.4.corner_left = f32[8,8,128]{2,1,0:T(8,128)S(1)} collective-permute-done((f32[8,8,128]{2,1,0:T(8,128)S(1)}, f32[8,8,128]{2,1,0:T(8,128)S(1)}, u32[]{:S(2)}, u32[]{:S(2)}) %collective-permute-start.4) | collective-permute-done | bytes 32800 | tf_op jit(solution)/shard_map/ppermute | solution.py:647
  13.1 0.0 collective-permute-done.5.corner_right
  13.1 1.6 %shard_map.43 = (f32[3,4,8,128]{3,2,1,0:T(8,128)S(1)}, f32[2,24,24,128]{3,2,1,0:T(8,128)S(1)}, f32[24,32,128]{2,1,0:T(8,128)S(1)}, f32[7,24,24,128]{3,2,1,0:T(8,128)S(1)}) custom-call(f32[2,16,16,128]{3,2,1,0:T(8,128)S(1)} %bitcast.14, f32[2,4,16,128]{3,2,1,0:T(8,128)S(1)} %collective-permute-done.before, ...), custom_call_target="tpu_custom_call" | custom-call | tf_op jit(solution)/shard_map/pallas_call | solution.py:635
  14.7 3.3 %collective-permute-start.9 = (f32[3,4,8,128]{3,2,1,0:T(8,128)S(1)}, f32[3,4,8,128]{3,2,1,0:T(8,128)S(1)}, u32[]{:S(2)}, u32[]{:S(2)}) collective-permute-start(f32[3,4,8,128]{3,2,1,0:T(8,128)S(1)} %get-tuple-element.18), channel_id=1, source_target_pairs={{0,12},{4,8},{8,4},{12,0},{1,13},{5,9},{9,5},{13,1},{2,14},{6,10},... | collective-permute-start | bytes 147464 | tf_op jit(solution)/shard_map/ppermute | solution.py:652
  18.0 0.0 collective-permute-start.8
  18.0 1.2 %collective-permute-start.7 = (f32[3,4,8,128]{3,2,1,0:T(8,128)S(1)}, f32[3,4,8,128]{3,2,1,0:T(8,128)S(1)}, u32[]{:S(2)}, u32[]{:S(2)}) collective-permute-start(f32[3,4,8,128]{3,2,1,0:T(8,128)S(1)} %get-tuple-element.18), channel_id=1, source_target_pairs={{0,4},{4,0},{8,12},{12,8},{1,5},{5,1},{9,13},{13,9},{2,6},{6,2},{1... | collective-permute-start | bytes 147464 | tf_op jit(solution)/shard_map/ppermute | solution.py:652
  19.2 1.5 %collective-permute-start.6 = (f32[3,4,8,128]{3,2,1,0:T(8,128)S(1)}, f32[3,4,8,128]{3,2,1,0:T(8,128)S(1)}, u32[]{:S(2)}, u32[]{:S(2)}) collective-permute-start(f32[3,4,8,128]{3,2,1,0:T(8,128)S(1)} %get-tuple-element.18), channel_id=1, source_target_pairs={{0,2},{1,3},{2,0},{3,1},{4,6},{5,7},{6,4},{7,5},{8,10},{9,11},{10,... | collective-permute-start | bytes 147464 | tf_op jit(solution)/shard_map/ppermute | solution.py:652
  20.7 0.0 collective-permute-done.9
  20.7 2.5 %collective-permute-done.8 = f32[3,4,8,128]{3,2,1,0:T(8,128)S(1)} collective-permute-done((f32[3,4,8,128]{3,2,1,0:T(8,128)S(1)}, f32[3,4,8,128]{3,2,1,0:T(8,128)S(1)}, u32[]{:S(2)}, u32[]{:S(2)}) %collective-permute-start.8) | collective-permute-done | bytes 49184 | tf_op jit(solution)/shard_map/ppermute | solution.py:652
  23.2 0.0 collective-permute-done.7
  23.2 1.7 %collective-permute-start.10 = (f32[3,3,4,8,128]{4,3,2,1,0:T(8,128)S(1)}, f32[3,3,4,8,128]{4,3,2,1,0:T(8,128)}, u32[]{:S(2)}, u32[]{:S(2)}) collective-permute-start(f32[3,3,4,8,128]{4,3,2,1,0:T(8,128)S(1)} %pad_maximum_fusion.1), channel_id=1, source_target_pairs={{0,2},{1,3},{2,0},{3,1},{4,6},{5,7},{6,4},{7,5},{8,10},{9,11},{10,... | collective-permute-start | bytes 442376 | tf_op jit(solution)/shard_map/ppermute | solution.py:652
  24.9 0.0 collective-permute-done.6
  24.9 0.1 collective-permute-start.11
  25.0 4.7 %collective-permute-done.10.second = f32[3,3,4,8,128]{4,3,2,1,0:T(8,128)} collective-permute-done((f32[3,3,4,8,128]{4,3,2,1,0:T(8,128)S(1)}, f32[3,3,4,8,128]{4,3,2,1,0:T(8,128)}, u32[]{:S(2)}, u32[]{:S(2)}) %collective-permute-start.10) | collective-permute-done | bytes 147488 | tf_op jit(solution)/shard_map/ppermute | solution.py:652
  29.6 0.0 collective-permute-start.12
  29.7 0.1 pad_add_fusion.place
  29.7 0.0 collective-permute-done.11.first_far
  29.7 1.6 %collective-permute-done.12.second_far = f32[3,3,4,8,128]{4,3,2,1,0:T(8,128)} collective-permute-done((f32[3,3,4,8,128]{4,3,2,1,0:T(8,128)}, f32[3,3,4,8,128]{4,3,2,1,0:T(8,128)}, u32[]{:S(2)}, u32[]{:S(2)}) %collective-permute-start.12) | collective-permute-done | bytes 147488 | tf_op jit(solution)/shard_map/ppermute | solution.py:652
  31.4 6.2 %shard_map.44 = (f32[16,16,128]{2,1,0:T(8,128)}, f32[16,16,128]{2,1,0:T(8,128)}) custom-call(s32[2]{0:T(128)S(1)} %pad_add_fusion.place, f32[5,3,4,8,128]{4,3,2,1,0:T(8,128)S(1)} %constant_dynamic-update-slice_fusion.first, f32[3,3,4,8,128]{4,3,2,1,0:T(8,128)} %collective-permute-done.10.second, f32[5,3,4,8,128]{4,3,2,1,0:T(8,128)S(1)} %collective-permute-done.11.first_far, ...), custom_call_target="tpu_custom_call" | custom-call | tf_op jit(solution)/shard_map/pallas_call | solution.py:635
  (8 shorter events, 0.1 us)
Async XLA Ops:
  1.6 7.5 %collective-permute-start = (f32[2,4,16,128]{3,2,1,0:T(8,128)S(1)}, f32[2,4,16,128]{3,2,1,0:T(8,128)S(1)}, u32[]{:S(2)}, u32[]{:S(2)}) collective-permute-start(f32[2,4,16,128]{3,2,1,0:T(8,128)S(1)} %get-tuple-element.12), channel_id=1, source_target_pairs={{0,4},{4,8},{8,12},{12,0},{1,5},{5,9},{9,13},{13,1},{2,6},{6,10},{... | collective-permute-start | bytes 196616 | tf_op jit(solution)/shard_map/ppermute | solution.py:647
  4.7 5.0 %collective-permute-start.1 = (f32[2,4,16,128]{3,2,1,0:T(8,128)S(1)}, f32[2,4,16,128]{3,2,1,0:T(8,128)S(1)}, u32[]{:S(2)}, u32[]{:S(2)}) collective-permute-start(f32[2,4,16,128]{3,2,1,0:T(8,128)S(1)} %get-tuple-element.13), channel_id=1, source_target_pairs={{0,12},{4,0},{8,4},{12,8},{1,13},{5,1},{9,5},{13,9},{2,14},{6,2},{... | collective-permute-start | bytes 196616 | tf_op jit(solution)/shard_map/ppermute | solution.py:647
  6.8 4.7 %collective-permute-start.2 = (f32[16,8,128]{2,1,0:T(8,128)S(1)}, f32[16,8,128]{2,1,0:T(8,128)S(1)}, u32[]{:S(2)}, u32[]{:S(2)}) collective-permute-start(f32[16,8,128]{2,1,0:T(8,128)S(1)} %get-tuple-element.14), channel_id=1, source_target_pairs={{0,1},{1,2},{2,3},{3,0},{4,5},{5,6},{6,7},{7,4},{8,9},{9,10},{10,1... | collective-permute-start | bytes 196616 | tf_op jit(solution)/shard_map/ppermute | solution.py:647
  6.8 4.7 %collective-permute-start.3 = (f32[16,8,128]{2,1,0:T(8,128)S(1)}, f32[16,8,128]{2,1,0:T(8,128)S(1)}, u32[]{:S(2)}, u32[]{:S(2)}) collective-permute-start(f32[16,8,128]{2,1,0:T(8,128)S(1)} %get-tuple-element.15), channel_id=1, source_target_pairs={{0,3},{1,0},{2,1},{3,2},{4,7},{5,4},{6,5},{7,6},{8,11},{9,8},{10,9... | collective-permute-start | bytes 196616 | tf_op jit(solution)/shard_map/ppermute | solution.py:647
  9.7 3.4 %collective-permute-start.4 = (f32[8,8,128]{2,1,0:T(8,128)S(1)}, f32[8,8,128]{2,1,0:T(8,128)S(1)}, u32[]{:S(2)}, u32[]{:S(2)}) collective-permute-start(f32[8,8,128]{2,1,0:T(8,128)S(1)} %get-tuple-element.16), channel_id=1, source_target_pairs={{0,1},{1,2},{2,3},{3,0},{4,5},{5,6},{6,7},{7,4},{8,9},{9,10},{10,1... | collective-permute-start | bytes 98312 | tf_op jit(solution)/shard_map/ppermute | solution.py:647
  9.8 3.3 %collective-permute-start.5 = (f32[8,8,128]{2,1,0:T(8,128)S(1)}, f32[8,8,128]{2,1,0:T(8,128)S(1)}, u32[]{:S(2)}, u32[]{:S(2)}) collective-permute-start(f32[8,8,128]{2,1,0:T(8,128)S(1)} %get-tuple-element.17), channel_id=1, source_target_pairs={{0,3},{1,0},{2,1},{3,2},{4,7},{5,4},{6,5},{7,6},{8,11},{9,8},{10,9... | collective-permute-start | bytes 98312 | tf_op jit(solution)/shard_map/ppermute | solution.py:647
  14.7 6.0 %collective-permute-start.9 = (f32[3,4,8,128]{3,2,1,0:T(8,128)S(1)}, f32[3,4,8,128]{3,2,1,0:T(8,128)S(1)}, u32[]{:S(2)}, u32[]{:S(2)}) collective-permute-start(f32[3,4,8,128]{3,2,1,0:T(8,128)S(1)} %get-tuple-element.18), channel_id=1, source_target_pairs={{0,12},{4,8},{8,4},{12,0},{1,13},{5,9},{9,5},{13,1},{2,14},{6,10},... | collective-permute-start | bytes 147464 | tf_op jit(solution)/shard_map/ppermute | solution.py:652
  18.0 5.2 %collective-permute-start.8 = (f32[3,4,8,128]{3,2,1,0:T(8,128)S(1)}, f32[3,4,8,128]{3,2,1,0:T(8,128)S(1)}, u32[]{:S(2)}, u32[]{:S(2)}) collective-permute-start(f32[3,4,8,128]{3,2,1,0:T(8,128)S(1)} %get-tuple-element.18), channel_id=1, source_target_pairs={{0,8},{4,12},{8,0},{12,4},{1,9},{5,13},{9,1},{13,5},{2,10},{6,14},... | collective-permute-start | bytes 147464 | tf_op jit(solution)/shard_map/ppermute | solution.py:652
  18.0 5.2 %collective-permute-start.7 = (f32[3,4,8,128]{3,2,1,0:T(8,128)S(1)}, f32[3,4,8,128]{3,2,1,0:T(8,128)S(1)}, u32[]{:S(2)}, u32[]{:S(2)}) collective-permute-start(f32[3,4,8,128]{3,2,1,0:T(8,128)S(1)} %get-tuple-element.18), channel_id=1, source_target_pairs={{0,4},{4,0},{8,12},{12,8},{1,5},{5,1},{9,13},{13,9},{2,6},{6,2},{1... | collective-permute-start | bytes 147464 | tf_op jit(solution)/shard_map/ppermute | solution.py:652
  19.2 5.7 %collective-permute-start.6 = (f32[3,4,8,128]{3,2,1,0:T(8,128)S(1)}, f32[3,4,8,128]{3,2,1,0:T(8,128)S(1)}, u32[]{:S(2)}, u32[]{:S(2)}) collective-permute-start(f32[3,4,8,128]{3,2,1,0:T(8,128)S(1)} %get-tuple-element.18), channel_id=1, source_target_pairs={{0,2},{1,3},{2,0},{3,1},{4,6},{5,7},{6,4},{7,5},{8,10},{9,11},{10,... | collective-permute-start | bytes 147464 | tf_op jit(solution)/shard_map/ppermute | solution.py:652
  23.2 6.5 %collective-permute-start.10 = (f32[3,3,4,8,128]{4,3,2,1,0:T(8,128)S(1)}, f32[3,3,4,8,128]{4,3,2,1,0:T(8,128)}, u32[]{:S(2)}, u32[]{:S(2)}) collective-permute-start(f32[3,3,4,8,128]{4,3,2,1,0:T(8,128)S(1)} %pad_maximum_fusion.1), channel_id=1, source_target_pairs={{0,2},{1,3},{2,0},{3,1},{4,6},{5,7},{6,4},{7,5},{8,10},{9,11},{10,... | collective-permute-start | bytes 442376 | tf_op jit(solution)/shard_map/ppermute | solution.py:652
  24.9 4.8 %collective-permute-start.11 = (f32[5,3,4,8,128]{4,3,2,1,0:T(8,128)S(1)}, f32[5,3,4,8,128]{4,3,2,1,0:T(8,128)S(1)}, u32[]{:S(2)}, u32[]{:S(2)}) collective-permute-start(f32[5,3,4,8,128]{4,3,2,1,0:T(8,128)S(1)} %constant_dynamic-update-slice_fusion.first), channel_id=1, source_target_pairs={{0,1},{1,0},{2,3},{3,2},{4,5},{5,4},{6,7},{7,6},{8,9},{9,8},{10,11... | collective-permute-start | bytes 737288 | tf_op jit(solution)/shard_map/ppermute | solution.py:652
  29.6 1.7 %collective-permute-start.12 = (f32[3,3,4,8,128]{4,3,2,1,0:T(8,128)}, f32[3,3,4,8,128]{4,3,2,1,0:T(8,128)}, u32[]{:S(2)}, u32[]{:S(2)}) collective-permute-start(f32[3,3,4,8,128]{4,3,2,1,0:T(8,128)} %collective-permute-done.10.second), channel_id=1, source_target_pairs={{0,1},{1,0},{2,3},{3,2},{4,5},{5,4},{6,7},{7,6},{8,9},{9,8},{10,11... | collective-permute-start | bytes 442376 | tf_op jit(solution)/shard_map/ppermute | solution.py:652

commit v5 on v4

--- a/solution.py
+++ b/solution.py
@@ -226,6 +226,10 @@
             values = self.ref[row % total if outside else row, pl.ds(self.first, self.width), :]
             self.values[key] = lane_swap(values) if outside else values
         return self.values[key]
+
+
+def stage(run, *args):
+    pl.when(lax.axis_index("gy") >= 0)(functools.partial(run, *args))
 
 
 def chem_right(conc):
@@ -470,15 +474,15 @@
     right_side = (right_conc,)
     wide = (PAD - HALO, columns + 2 * HALO)
     level.sweep(
-        (right_conc, chem_start), right_side, 1, frame - 2, 11, wide,
+        (right_conc, chem_start), right_side, 1, frame - 2, frame - 2, wide,
         put_window((conc_mid, chem_mid), wide),
     )
     level.sweep(
-        (conc_mid, chem_mid), right_side, 2, frame - 4, 10, wide,
+        (conc_mid, chem_mid), right_side, 2, frame - 4, frame - 4, wide,
         put_window((conc_out, chem_out), (0, wide[1])),
     )
     level.coarse_right(
-        (conc_out, chem_out), right_side, HALO, rows, 8, (PAD, columns), put_sums(sums), wide[0]
+        (conc_out, chem_out), right_side, HALO, rows, rows, (PAD, columns), put_sums(sums), wide[0]
     )
     for index in range(rows // 2):
         row = HALO + 2 * index
@@ -495,13 +499,13 @@
 
 
 def coarse_kernel(
-    slots, grid, place, first, second, first_far, second_far,
+    slots, grid, first, second, first_far, second_far,
     kept, right_conc, all_weights, conc_new, chem_new, *scratch,
 ):
     conc_in, chem_in = kept.at[0], kept.at[1]
     weights = [all_weights.at[i] for i in range(7)]
     scratch = list(scratch)
-    start_even, at_y = place[0] % 2 == 0, place[1]
+    start_even, at_y = lax.axis_index("gx") % 2 == 0, lax.axis_index("gy")
     levels = []
     for level_index in (1, 2, 3):
         level = Level(level_index, scratch[5:14][2:])
@@ -558,23 +562,23 @@
             half = pair_rows(sums.at[2], index, columns)
             put_padded((out_mobility,))(index, 0.125 * pair_lanes(half, dup))
 
-    one.set_weights(mob1, rows1)
-    one.first_sweep(right1, rows1, put_padded(a1))
-    one.sweep(a1, right1, 0, rows1, rows1, window1, put_padded(b1))
-    one.coarse_right(b1, right1, 0, rows1, rows1, window1, put_sums(sums1))
-    coarsen(mob1, sums1, right2, mob2, 2)
-
-    two.set_weights(mob2, rows2)
-    two.first_sweep(right2, rows2, put_padded(a2))
-    two.sweep(a2, right2, 0, rows2, rows2, window2, put_padded(b2))
-    two.coarse_right(b2, right2, 0, rows2, rows2, window2, put_sums(sums2))
-    coarsen(mob2, sums2, right3, mob3, 4)
-
-    three.set_weights(mob3, rows3)
-    three.first_sweep(right3, rows3, put_padded(a3))
+    stage(one.set_weights, mob1, rows1)
+    stage(one.first_sweep, right1, rows1, put_padded(a1))
+    stage(one.sweep, a1, right1, 0, rows1, rows1, window1, put_padded(b1))
+    stage(one.coarse_right, b1, right1, 0, rows1, rows1, window1, put_sums(sums1))
+    stage(coarsen, mob1, sums1, right2, mob2, 2)
+
+    stage(two.set_weights, mob2, rows2)
+    stage(two.first_sweep, right2, rows2, put_padded(a2))
+    stage(two.sweep, a2, right2, 0, rows2, rows2, window2, put_padded(b2))
+    stage(two.coarse_right, b2, right2, 0, rows2, rows2, window2, put_sums(sums2))
+    stage(coarsen, mob2, sums2, right3, mob3, 4)
+
+    stage(three.set_weights, mob3, rows3)
+    stage(three.first_sweep, right3, rows3, put_padded(a3))
     now, other = a3, b3
     for sweep_index in range(COARSE - 1):
-        three.sweep(now, right3, 0, rows3, rows3, window3, put_padded(other))
+        stage(three.sweep, now, right3, 0, rows3, rows3, window3, put_padded(other))
         now, other = other, now
 
     def correct(coarse, coarse_row, fine_in, fine_out, spread, index):
@@ -591,12 +595,12 @@
 
     for row in range(rows3):
         correct(now, row, b2, a2, spread3, row)
-    two.sweep(a2, right2, 0, rows2, rows2, window2, put_padded(b2))
-    two.sweep(b2, right2, 0, rows2, rows2, window2, put_padded(a2))
+    stage(two.sweep, a2, right2, 0, rows2, rows2, window2, put_padded(b2))
+    stage(two.sweep, b2, right2, 0, rows2, rows2, window2, put_padded(a2))
     for row in range(rows2):
         correct(a2, row, b1, a1, spread2, row)
-    one.sweep(a1, right1, -2, own_rows + 4, own_rows + 4, window1, put_padded(b1))
-    one.sweep(b1, right1, -1, own_rows + 2, own_rows + 2, window1, put_padded(a1))
+    stage(one.sweep, a1, right1, -2, own_rows + 4, own_rows + 4, window1, put_padded(b1))
+    stage(one.sweep, b1, right1, -1, own_rows + 2, own_rows + 2, window1, put_padded(a1))
 
     rows, columns = conc_new.shape[:2]
     wide = (PAD - HALO, columns + 2 * HALO)
@@ -618,7 +622,7 @@
     fine = fine_level(weights)
     right_side = (right_conc,)
     fine.sweep(
-        (fine_a0, fine_a1), right_side, HALO - 1, rows + 2, 9, wide,
+        (fine_a0, fine_a1), right_side, HALO - 1, rows + 2, rows + 2, wide,
         put_window((fine_b0, fine_b1), wide),
     )
 
@@ -626,18 +630,17 @@
         conc_new[row - HALO] = conc_value
         chem_new[row - HALO] = chem_value
 
-    fine.sweep((fine_b0, fine_b1), right_side, HALO, rows, 8, (PAD, columns), put_new)
-
-
-def call_kernel(kernel, outs, scratch, *args, specs=None, vmem_mib=8):
+    fine.sweep((fine_b0, fine_b1), right_side, HALO, rows, rows, (PAD, columns), put_new)
+
+
+def call_kernel(kernel, outs, scratch, *args, vmem_mib=8):
     shapes = tuple(jax.ShapeDtypeStruct(shape, jnp.float32) for shape in outs)
-    scratch = [pltpu.VMEM(shape, jnp.float32) if isinstance(shape, tuple) else shape for shape in scratch]
     return pl.pallas_call(
         kernel,
         out_shape=shapes,
-        in_specs=specs or [whole_block()] * len(args),
+        in_specs=[whole_block()] * len(args),
         out_specs=tuple(whole_block() for _ in outs),
-        scratch_shapes=scratch,
+        scratch_shapes=[pltpu.VMEM(shape, jnp.float32) for shape in scratch],
         compiler_params=pltpu.CompilerParams(vmem_limit_bytes=vmem_mib * 1024 * 1024),
     )(*args)
 
@@ -693,7 +696,6 @@
         (frame,) * 4 + ((3, rows // 2, columns, lanes),),
         fields, before, after, *sides,
     )
-    place = jnp.stack([lax.axis_index("gx"), lax.axis_index("gy")])
     count_x, count_y = lax.axis_size("gx"), lax.axis_size("gy")
     grids = [(count_x * rows >> level + 1, count_y * columns >> level) for level in range(4)]
     scratch = []
@@ -704,9 +706,8 @@
     scratch += [(2, grids[2][0], grids[1][1], lanes), (2, grids[3][0], grids[2][1], lanes)]
     scratch += [(2, rows // 2 + 2, columns + 4 * PAD, lanes)] + [frame] * 4
     kernel = functools.partial(coarse_kernel, slot_masks(), (count_x, count_y))
-    args = (place, *gathered(packed), *kept)
-    specs = [pl.BlockSpec(memory_space=pltpu.SMEM)] + [whole_block()] * (len(args) - 1)
-    return call_kernel(kernel, (block, block), scratch, *args, specs=specs, vmem_mib=24)
+    args = (*gathered(packed), *kept)
+    return call_kernel(kernel, (block, block), scratch, *args, vmem_mib=24)
 
 
 def body(conc_old, chem_old):

time: 37.8 us -> 35.2 us (0.931)
  Pallas kernels: 7.9 us -> 5.79 us
  waiting for transfers between devices: 11.5 us -> 11.1 us
    pallas_call x4, Pallas kernels: 7.9 us -> 5.79 us  [call_kernel(): pl.pallas_call(kernel, out_shape=shapes, in_specs=[whole_block()] * len(a...]
where the time goes in v5:
time: 35.2 us; the launch traced here: 35.1 us
  starting transfers between devices  16.4 us (47%)
  waiting for transfers between devices  11.1 us (32%)
  Pallas kernels  5.79 us (16%)
  other arithmetic  1 us (3%)
  between operations  0.71 us (2%)
    ppermute x6, starting transfers between devices, shifted(): lax.ppermute(values, axis, [(i, (i + by) % count) for i in range(count)])  8.7 us
    ppermute x7, waiting for transfers between devices, swapped(): return lax.ppermute(values, axis, [(i, i ^ mask) for i in range(count)])  8.39 us
    ppermute x7, starting transfers between devices, swapped(): return lax.ppermute(values, axis, [(i, i ^ mask) for i in range(count)])  7.71 us
    pallas_call x4, Pallas kernels, call_kernel(): pl.pallas_call(kernel, out_shape=shapes, in_specs=[whole_block()] * len(a...  5.79 us
    ppermute x6, waiting for transfers between devices, shifted(): lax.ppermute(values, axis, [(i, (i + by) % count) for i in range(count)])  2.73 us
    concatenate x1, other arithmetic, two_phase_solve(): fields = jnp.concatenate([conc, chem], axis=0).reshape((2,) + block)  0.99 us
  transfers between devices with their start and end apart: 13, of which 6 were waited for; matrix products, arithmetic and copies ran while one was open for 0% of the time, Pallas kernels for 0%

profile of v5, /device:TPU:0, one launch (start us, length us, event | category | flops | bytes accessed | tf_op | source)
XLA Modules:
  0.0 35.1 jit_solution(6888829535159393707)
XLA Ops:
  0.6 1.0 %pad_maximum_fusion = f32[32,16,128]{2,1,0:T(8,128)S(1)} fusion(f32[16,16,128]{2,1,0:T(8,128)} %param.3, f32[16,16,128]{2,1,0:T(8,128)} %param.2), kind=kLoop, calls=%fused_computation | loop fusion | flops 65536 | bytes 524288 | tf_op jit(solution)/shard_map/concatenate | solution.py:684
  1.6 3.1 %collective-permute-start = (f32[2,4,16,128]{3,2,1,0:T(8,128)S(1)}, f32[2,4,16,128]{3,2,1,0:T(8,128)S(1)}, u32[]{:S(2)}, u32[]{:S(2)}) collective-permute-start(f32[2,4,16,128]{3,2,1,0:T(8,128)S(1)} %get-tuple-element.12), channel_id=1, source_target_pairs={{0,4},{4,8},{8,12},{12,0},{1,5},{5,9},{9,13},{13,1},{2,6},{6,10},{... | collective-permute-start | bytes 196616 | tf_op jit(solution)/shard_map/ppermute | solution.py:650
  4.7 2.1 %collective-permute-start.1 = (f32[2,4,16,128]{3,2,1,0:T(8,128)S(1)}, f32[2,4,16,128]{3,2,1,0:T(8,128)S(1)}, u32[]{:S(2)}, u32[]{:S(2)}) collective-permute-start(f32[2,4,16,128]{3,2,1,0:T(8,128)S(1)} %get-tuple-element.13), channel_id=1, source_target_pairs={{0,12},{4,0},{8,4},{12,8},{1,13},{5,1},{9,5},{13,9},{2,14},{6,2},{... | collective-permute-start | bytes 196616 | tf_op jit(solution)/shard_map/ppermute | solution.py:650
  6.8 0.0 collective-permute-start.2
  6.8 1.7 %collective-permute-start.3 = (f32[16,8,128]{2,1,0:T(8,128)S(1)}, f32[16,8,128]{2,1,0:T(8,128)S(1)}, u32[]{:S(2)}, u32[]{:S(2)}) collective-permute-start(f32[16,8,128]{2,1,0:T(8,128)S(1)} %get-tuple-element.15), channel_id=1, source_target_pairs={{0,3},{1,0},{2,1},{3,2},{4,7},{5,4},{6,5},{7,6},{8,11},{9,8},{10,9... | collective-permute-start | bytes 196616 | tf_op jit(solution)/shard_map/ppermute | solution.py:650
  8.6 0.6 %collective-permute-done.before = f32[2,4,16,128]{3,2,1,0:T(8,128)S(1)} collective-permute-done((f32[2,4,16,128]{3,2,1,0:T(8,128)S(1)}, f32[2,4,16,128]{3,2,1,0:T(8,128)S(1)}, u32[]{:S(2)}, u32[]{:S(2)}) %collective-permute-start) | collective-permute-done | bytes 65568 | tf_op jit(solution)/shard_map/ppermute | solution.py:650
  9.1 0.5 %collective-permute-done.1.after = f32[2,4,16,128]{3,2,1,0:T(8,128)S(1)} collective-permute-done((f32[2,4,16,128]{3,2,1,0:T(8,128)S(1)}, f32[2,4,16,128]{3,2,1,0:T(8,128)S(1)}, u32[]{:S(2)}, u32[]{:S(2)}) %collective-permute-start.1) | collective-permute-done | bytes 65568 | tf_op jit(solution)/shard_map/ppermute | solution.py:650
  9.7 0.1 collective-permute-start.4
  9.8 1.7 %collective-permute-start.5 = (f32[8,8,128]{2,1,0:T(8,128)S(1)}, f32[8,8,128]{2,1,0:T(8,128)S(1)}, u32[]{:S(2)}, u32[]{:S(2)}) collective-permute-start(f32[8,8,128]{2,1,0:T(8,128)S(1)} %get-tuple-element.17), channel_id=1, source_target_pairs={{0,3},{1,0},{2,1},{3,2},{4,7},{5,4},{6,5},{7,6},{8,11},{9,8},{10,9... | collective-permute-start | bytes 98312 | tf_op jit(solution)/shard_map/ppermute | solution.py:650
  11.5 0.0 collective-permute-done.2.own_left
  11.5 0.0 collective-permute-done.3.own_right
  11.5 1.6 %collective-permute-done.4.corner_left = f32[8,8,128]{2,1,0:T(8,128)S(1)} collective-permute-done((f32[8,8,128]{2,1,0:T(8,128)S(1)}, f32[8,8,128]{2,1,0:T(8,128)S(1)}, u32[]{:S(2)}, u32[]{:S(2)}) %collective-permute-start.4) | collective-permute-done | bytes 32800 | tf_op jit(solution)/shard_map/ppermute | solution.py:650
  13.1 0.0 collective-permute-done.5.corner_right
  13.1 1.2 %shard_map.43 = (f32[3,4,8,128]{3,2,1,0:T(8,128)S(1)}, f32[2,24,24,128]{3,2,1,0:T(8,128)S(1)}, f32[24,32,128]{2,1,0:T(8,128)S(1)}, f32[7,24,24,128]{3,2,1,0:T(8,128)S(1)}) custom-call(f32[2,16,16,128]{3,2,1,0:T(8,128)S(1)} %bitcast.12, f32[2,4,16,128]{3,2,1,0:T(8,128)S(1)} %collective-permute-done.before, ...), custom_call_target="tpu_custom_call" | custom-call | tf_op jit(solution)/shard_map/pallas_call | solution.py:638
  14.3 3.3 %collective-permute-start.9 = (f32[3,4,8,128]{3,2,1,0:T(8,128)S(1)}, f32[3,4,8,128]{3,2,1,0:T(8,128)S(1)}, u32[]{:S(2)}, u32[]{:S(2)}) collective-permute-start(f32[3,4,8,128]{3,2,1,0:T(8,128)S(1)} %get-tuple-element.18), channel_id=1, source_target_pairs={{0,12},{4,8},{8,4},{12,0},{1,13},{5,9},{9,5},{13,1},{2,14},{6,10},... | collective-permute-start | bytes 147464 | tf_op jit(solution)/shard_map/ppermute | solution.py:655
  17.5 0.0 collective-permute-start.8
  17.5 1.2 %collective-permute-start.7 = (f32[3,4,8,128]{3,2,1,0:T(8,128)S(1)}, f32[3,4,8,128]{3,2,1,0:T(8,128)S(1)}, u32[]{:S(2)}, u32[]{:S(2)}) collective-permute-start(f32[3,4,8,128]{3,2,1,0:T(8,128)S(1)} %get-tuple-element.18), channel_id=1, source_target_pairs={{0,4},{4,0},{8,12},{12,8},{1,5},{5,1},{9,13},{13,9},{2,6},{6,2},{1... | collective-permute-start | bytes 147464 | tf_op jit(solution)/shard_map/ppermute | solution.py:655
  18.7 1.5 %collective-permute-start.6 = (f32[3,4,8,128]{3,2,1,0:T(8,128)S(1)}, f32[3,4,8,128]{3,2,1,0:T(8,128)S(1)}, u32[]{:S(2)}, u32[]{:S(2)}) collective-permute-start(f32[3,4,8,128]{3,2,1,0:T(8,128)S(1)} %get-tuple-element.18), channel_id=1, source_target_pairs={{0,2},{1,3},{2,0},{3,1},{4,6},{5,7},{6,4},{7,5},{8,10},{9,11},{10,... | collective-permute-start | bytes 147464 | tf_op jit(solution)/shard_map/ppermute | solution.py:655
  20.2 0.0 collective-permute-done.9
  20.2 2.5 %collective-permute-done.8 = f32[3,4,8,128]{3,2,1,0:T(8,128)S(1)} collective-permute-done((f32[3,4,8,128]{3,2,1,0:T(8,128)S(1)}, f32[3,4,8,128]{3,2,1,0:T(8,128)S(1)}, u32[]{:S(2)}, u32[]{:S(2)}) %collective-permute-start.8) | collective-permute-done | bytes 49184 | tf_op jit(solution)/shard_map/ppermute | solution.py:655
  22.7 0.0 collective-permute-done.7
  22.7 1.7 %collective-permute-start.10 = (f32[3,3,4,8,128]{4,3,2,1,0:T(8,128)S(1)}, f32[3,3,4,8,128]{4,3,2,1,0:T(8,128)S(1)}, u32[]{:S(2)}, u32[]{:S(2)}) collective-permute-start(f32[3,3,4,8,128]{4,3,2,1,0:T(8,128)S(1)} %pad_maximum_fusion.1), channel_id=1, source_target_pairs={{0,2},{1,3},{2,0},{3,1},{4,6},{5,7},{6,4},{7,5},{8,10},{9,11},{10,... | collective-permute-start | bytes 442376 | tf_op jit(solution)/shard_map/ppermute | solution.py:655
  24.4 0.0 collective-permute-done.6
  24.5 0.1 collective-permute-start.11
  24.5 4.6 %collective-permute-done.10.second = f32[3,3,4,8,128]{4,3,2,1,0:T(8,128)S(1)} collective-permute-done((f32[3,3,4,8,128]{4,3,2,1,0:T(8,128)S(1)}, f32[3,3,4,8,128]{4,3,2,1,0:T(8,128)S(1)}, u32[]{:S(2)}, u32[]{:S(2)}) %collective-permute-start.10) | collective-permute-done | bytes 147488 | tf_op jit(solution)/shard_map/ppermute | solution.py:655
  29.1 0.0 collective-permute-start.12
  29.1 0.0 collective-permute-done.11.first_far
  29.1 1.4 %collective-permute-done.12.second_far = f32[3,3,4,8,128]{4,3,2,1,0:T(8,128)S(1)} collective-permute-done((f32[3,3,4,8,128]{4,3,2,1,0:T(8,128)S(1)}, f32[3,3,4,8,128]{4,3,2,1,0:T(8,128)S(1)}, u32[]{:S(2)}, u32[]{:S(2)}) %collective-permute-start.12) | collective-permute-done | bytes 147488 | tf_op jit(solution)/shard_map/ppermute | solution.py:655
  30.5 4.6 %shard_map.44 = (f32[16,16,128]{2,1,0:T(8,128)}, f32[16,16,128]{2,1,0:T(8,128)}) custom-call(f32[5,3,4,8,128]{4,3,2,1,0:T(8,128)S(1)} %constant_dynamic-update-slice_fusion.first, f32[3,3,4,8,128]{4,3,2,1,0:T(8,128)S(1)} %collective-permute-done.10.second, f32[5,3,4,8,128]{4,3,2,1,0:T(8,128)S(1)} %collective-permute-done.11.first_far, ...), custom_call_target="tpu_custom_call" | custom-call | tf_op jit(solution)/shard_map/pallas_call | solution.py:638
  (8 shorter events, 0.1 us)
Async XLA Ops:
  1.6 7.5 %collective-permute-start = (f32[2,4,16,128]{3,2,1,0:T(8,128)S(1)}, f32[2,4,16,128]{3,2,1,0:T(8,128)S(1)}, u32[]{:S(2)}, u32[]{:S(2)}) collective-permute-start(f32[2,4,16,128]{3,2,1,0:T(8,128)S(1)} %get-tuple-element.12), channel_id=1, source_target_pairs={{0,4},{4,8},{8,12},{12,0},{1,5},{5,9},{9,13},{13,1},{2,6},{6,10},{... | collective-permute-start | bytes 196616 | tf_op jit(solution)/shard_map/ppermute | solution.py:650
  4.7 5.0 %collective-permute-start.1 = (f32[2,4,16,128]{3,2,1,0:T(8,128)S(1)}, f32[2,4,16,128]{3,2,1,0:T(8,128)S(1)}, u32[]{:S(2)}, u32[]{:S(2)}) collective-permute-start(f32[2,4,16,128]{3,2,1,0:T(8,128)S(1)} %get-tuple-element.13), channel_id=1, source_target_pairs={{0,12},{4,0},{8,4},{12,8},{1,13},{5,1},{9,5},{13,9},{2,14},{6,2},{... | collective-permute-start | bytes 196616 | tf_op jit(solution)/shard_map/ppermute | solution.py:650
  6.8 4.7 %collective-permute-start.2 = (f32[16,8,128]{2,1,0:T(8,128)S(1)}, f32[16,8,128]{2,1,0:T(8,128)S(1)}, u32[]{:S(2)}, u32[]{:S(2)}) collective-permute-start(f32[16,8,128]{2,1,0:T(8,128)S(1)} %get-tuple-element.14), channel_id=1, source_target_pairs={{0,1},{1,2},{2,3},{3,0},{4,5},{5,6},{6,7},{7,4},{8,9},{9,10},{10,1... | collective-permute-start | bytes 196616 | tf_op jit(solution)/shard_map/ppermute | solution.py:650
  6.8 4.7 %collective-permute-start.3 = (f32[16,8,128]{2,1,0:T(8,128)S(1)}, f32[16,8,128]{2,1,0:T(8,128)S(1)}, u32[]{:S(2)}, u32[]{:S(2)}) collective-permute-start(f32[16,8,128]{2,1,0:T(8,128)S(1)} %get-tuple-element.15), channel_id=1, source_target_pairs={{0,3},{1,0},{2,1},{3,2},{4,7},{5,4},{6,5},{7,6},{8,11},{9,8},{10,9... | collective-permute-start | bytes 196616 | tf_op jit(solution)/shard_map/ppermute | solution.py:650
  9.7 3.4 %collective-permute-start.4 = (f32[8,8,128]{2,1,0:T(8,128)S(1)}, f32[8,8,128]{2,1,0:T(8,128)S(1)}, u32[]{:S(2)}, u32[]{:S(2)}) collective-permute-start(f32[8,8,128]{2,1,0:T(8,128)S(1)} %get-tuple-element.16), channel_id=1, source_target_pairs={{0,1},{1,2},{2,3},{3,0},{4,5},{5,6},{6,7},{7,4},{8,9},{9,10},{10,1... | collective-permute-start | bytes 98312 | tf_op jit(solution)/shard_map/ppermute | solution.py:650
  9.8 3.3 %collective-permute-start.5 = (f32[8,8,128]{2,1,0:T(8,128)S(1)}, f32[8,8,128]{2,1,0:T(8,128)S(1)}, u32[]{:S(2)}, u32[]{:S(2)}) collective-permute-start(f32[8,8,128]{2,1,0:T(8,128)S(1)} %get-tuple-element.17), channel_id=1, source_target_pairs={{0,3},{1,0},{2,1},{3,2},{4,7},{5,4},{6,5},{7,6},{8,11},{9,8},{10,9... | collective-permute-start | bytes 98312 | tf_op jit(solution)/shard_map/ppermute | solution.py:650
  14.3 6.0 %collective-permute-start.9 = (f32[3,4,8,128]{3,2,1,0:T(8,128)S(1)}, f32[3,4,8,128]{3,2,1,0:T(8,128)S(1)}, u32[]{:S(2)}, u32[]{:S(2)}) collective-permute-start(f32[3,4,8,128]{3,2,1,0:T(8,128)S(1)} %get-tuple-element.18), channel_id=1, source_target_pairs={{0,12},{4,8},{8,4},{12,0},{1,13},{5,9},{9,5},{13,1},{2,14},{6,10},... | collective-permute-start | bytes 147464 | tf_op jit(solution)/shard_map/ppermute | solution.py:655
  17.5 5.2 %collective-permute-start.8 = (f32[3,4,8,128]{3,2,1,0:T(8,128)S(1)}, f32[3,4,8,128]{3,2,1,0:T(8,128)S(1)}, u32[]{:S(2)}, u32[]{:S(2)}) collective-permute-start(f32[3,4,8,128]{3,2,1,0:T(8,128)S(1)} %get-tuple-element.18), channel_id=1, source_target_pairs={{0,8},{4,12},{8,0},{12,4},{1,9},{5,13},{9,1},{13,5},{2,10},{6,14},... | collective-permute-start | bytes 147464 | tf_op jit(solution)/shard_map/ppermute | solution.py:655
  17.5 5.2 %collective-permute-start.7 = (f32[3,4,8,128]{3,2,1,0:T(8,128)S(1)}, f32[3,4,8,128]{3,2,1,0:T(8,128)S(1)}, u32[]{:S(2)}, u32[]{:S(2)}) collective-permute-start(f32[3,4,8,128]{3,2,1,0:T(8,128)S(1)} %get-tuple-element.18), channel_id=1, source_target_pairs={{0,4},{4,0},{8,12},{12,8},{1,5},{5,1},{9,13},{13,9},{2,6},{6,2},{1... | collective-permute-start | bytes 147464 | tf_op jit(solution)/shard_map/ppermute | solution.py:655
  18.7 5.7 %collective-permute-start.6 = (f32[3,4,8,128]{3,2,1,0:T(8,128)S(1)}, f32[3,4,8,128]{3,2,1,0:T(8,128)S(1)}, u32[]{:S(2)}, u32[]{:S(2)}) collective-permute-start(f32[3,4,8,128]{3,2,1,0:T(8,128)S(1)} %get-tuple-element.18), channel_id=1, source_target_pairs={{0,2},{1,3},{2,0},{3,1},{4,6},{5,7},{6,4},{7,5},{8,10},{9,11},{10,... | collective-permute-start | bytes 147464 | tf_op jit(solution)/shard_map/ppermute | solution.py:655
  22.7 6.4 %collective-permute-start.10 = (f32[3,3,4,8,128]{4,3,2,1,0:T(8,128)S(1)}, f32[3,3,4,8,128]{4,3,2,1,0:T(8,128)S(1)}, u32[]{:S(2)}, u32[]{:S(2)}) collective-permute-start(f32[3,3,4,8,128]{4,3,2,1,0:T(8,128)S(1)} %pad_maximum_fusion.1), channel_id=1, source_target_pairs={{0,2},{1,3},{2,0},{3,1},{4,6},{5,7},{6,4},{7,5},{8,10},{9,11},{10,... | collective-permute-start | bytes 442376 | tf_op jit(solution)/shard_map/ppermute | solution.py:655
  24.5 4.6 %collective-permute-start.11 = (f32[5,3,4,8,128]{4,3,2,1,0:T(8,128)S(1)}, f32[5,3,4,8,128]{4,3,2,1,0:T(8,128)S(1)}, u32[]{:S(2)}, u32[]{:S(2)}) collective-permute-start(f32[5,3,4,8,128]{4,3,2,1,0:T(8,128)S(1)} %constant_dynamic-update-slice_fusion.first), channel_id=1, source_target_pairs={{0,1},{1,0},{2,3},{3,2},{4,5},{5,4},{6,7},{7,6},{8,9},{9,8},{10,11... | collective-permute-start | bytes 737288 | tf_op jit(solution)/shard_map/ppermute | solution.py:655
  29.1 1.4 %collective-permute-start.12 = (f32[3,3,4,8,128]{4,3,2,1,0:T(8,128)S(1)}, f32[3,3,4,8,128]{4,3,2,1,0:T(8,128)S(1)}, u32[]{:S(2)}, u32[]{:S(2)}) collective-permute-start(f32[3,3,4,8,128]{4,3,2,1,0:T(8,128)S(1)} %collective-permute-done.10.second), channel_id=1, source_target_pairs={{0,1},{1,0},{2,3},{3,2},{4,5},{5,4},{6,7},{7,6},{8,9},{9,8},{10,11... | collective-permute-start | bytes 442376 | tf_op jit(solution)/shard_map/ppermute | solution.py:655

commit v6 on v5

--- a/solution.py
+++ b/solution.py
@@ -236,6 +236,27 @@
     return conc * (conc * conc - (1.0 + STABILIZER))
 
 
+class Rows:
+    def __init__(self, total, *parts):
+        self.places = {
+            row: (ref, index) for ref, rows in parts for index, row in enumerate(rows)
+        }
+        self.shape = (total,) + parts[0][0].shape[1:]
+
+    def place(self, at):
+        row, *rest = at if isinstance(at, tuple) else (at,)
+        ref, index = self.places[row]
+        return ref, (index, *rest)
+
+    def __getitem__(self, at):
+        ref, index = self.place(at)
+        return ref[index]
+
+    def __setitem__(self, at, values):
+        ref, index = self.place(at)
+        ref[index] = values
+
+
 class Level:
     def __init__(self, level_index, weights, weights_from=PAD, right_from=PAD):
         self.scale = 0.25**level_index
@@ -244,8 +265,8 @@
         self.weights = weights
         self.weights_from, self.right_from = weights_from, right_from
 
-    def set_weights(self, mobility, unroll):
-        total, width = mobility.shape[0], self.weights[0].shape[1]
+    def set_weights(self, mobility, count, start=0):
+        width = self.weights[0].shape[1]
         half = 0.5 * self.scale * TIME_STEP
         face_x, up_y, down_y, up_z, down_z, coupling, gain = self.weights
 
@@ -254,9 +275,9 @@
 
         def group(first, size):
             rows = RowCache(mobility, None, self.weights_from, width)
-            before = half * (rows[first - 1] + rows[first])
+            before = half * (rows[start + first - 1] + rows[start + first])
             for i in range(size):
-                r = first + i
+                r = start + first + i
                 here = rows[r]
                 after = half * (here + rows[r + 1])
                 to_up_y = half * (here + at(r, 1))
@@ -273,7 +294,7 @@
                 gain[r] = DAMPING / (1.0 + total_weight * self.diagonal)
                 before = after
 
-        loop_rows(total, unroll, group)
+        loop_rows(count, count, group)
 
     def residuals(self, fields, right, rows, window, fields_from=0):
         conc, chem = fields
@@ -376,10 +397,10 @@
     return put
 
 
-def put_sums(sums):
+def put_sums(sums, offset=0):
     def put(row, *values):
         for field, value in enumerate(values):
-            sums[field, row] = value
+            sums[field, offset + row] = value
 
     return put
 
@@ -438,72 +459,165 @@
     return pltpu.roll(values, HALO, axis=0)
 
 
-def side_row(row, rows, own, corners):
-    if row < HALO:
-        return corners[row]
-    if row < HALO + rows:
-        return own[row - HALO]
-    return corners[row - rows]
+class FrameRows:
+    def __init__(self, rows):
+        self.total = rows + 2 * HALO
+        end = self.total
+        self.own = range(HALO, end - HALO)
+        self.weights_early = range(HALO + 1, end - HALO - 1)
+        self.swept_early = range(HALO + 2, end - HALO - 2)
+        self.joined = [HALO + 1, HALO + 2, end - HALO - 3, end - HALO - 2]
+        self.weights_late = [*range(2, HALO + 1), *range(end - HALO - 1, end - 3)]
+        self.weights_outer = [0, 1, end - 3, end - 2, end - 1]
+        self.right_late = [HALO - 1, end - HALO]
+        self.right_outer = [*range(HALO - 1), *range(end - HALO + 1, end)]
+        self.swept_late = [*range(2, HALO + 2), *range(end - HALO - 2, end - 2)]
+        self.mid_late = [*range(1, HALO + 1), *range(end - HALO - 1, end - 1)]
+
+    def weights(self, early, late):
+        return [
+            Rows(self.total, (early.at[i], self.weights_early), (late.at[i], self.weights_late))
+            for i in range(7)
+        ]
+
+    def swept(self, early, late):
+        return [
+            Rows(self.total, (early.at[i], self.swept_early), (late.at[i], self.swept_late))
+            for i in range(2)
+        ]
 
 
 def fine_level(weights):
     return Level(0, weights, HALO, 0)
 
 
-def fine_down_kernel(
-    fields, before, after, own_left, own_right, corner_left, corner_right,
-    packed, kept, right_conc, all_weights,
-    chem_start, mobility, conc_mid, chem_mid, sums,
+def set_row(conc, chem, left, right, row, conc_at, chem_at, mobility):
+    c = jnp.concatenate([left, conc, right])
+    if conc_at is not None:
+        conc_at[row] = c
+    chem_at[row] = jnp.concatenate([half_turn(left), chem, half_turn(right)])
+    gap = 1.0 - c * c
+    mobility[row] = 0.1 + gap * gap
+
+
+def pack(sums, field, index, out):
+    count = sums.shape[2] // 2
+    even = lane_even((count, sums.shape[3]), 1)
+    a = pair_rows(sums.at[field], 2 * index, count)
+    b = pair_rows(sums.at[field], 2 * index + 1, count)
+    out[field, index] = 0.125 * jnp.where(even, a + lane_roll(a, -1), b + lane_roll(b, 1))
+
+
+def early_kernel(
+    fields, own_left, own_right,
+    packed, kept, right_conc, all_weights, joined,
+    chem_start, mobility, mid, outer, sums,
 ):
-    conc, chem = fields.at[0], fields.at[1]
-    conc_out, chem_out = kept.at[0], kept.at[1]
-    weights = [all_weights.at[i] for i in range(7)]
-    rows, columns, lanes = conc.shape
-    frame = rows + 2 * HALO
-    for row in range(frame):
-        left = side_row(row, rows, own_left, corner_left)
-        right = side_row(row, rows, own_right, corner_right)
-        c = jnp.concatenate([left, frame_row(row, rows, conc, before.at[0], after.at[0]), right])
-        own = frame_row(row, rows, chem, before.at[1], after.at[1])
-        right_conc[row] = c
-        chem_start[row] = jnp.concatenate([half_turn(left), own, half_turn(right)])
-        gap = 1.0 - c * c
-        mobility[row] = 0.1 + gap * gap
+    rows, columns = fields.shape[1:3]
+    at = FrameRows(rows)
+    right_side = (Rows(at.total, (right_conc, at.own)),)
+    for row in at.own:
+        i = row - HALO
+        set_row(
+            fields[0, i], fields[1, i], own_left[i], own_right[i],
+            row, right_side[0], chem_start, mobility,
+        )
+    weights = [
+        Rows(at.total, (all_weights.at[i], at.weights_early), (outer.at[i], [HALO]))
+        for i in range(7)
+    ]
     level = fine_level(weights)
-    level.set_weights(mobility, frame)
-    right_side = (right_conc,)
+    level.set_weights(mobility, rows - 1, HALO)
     wide = (PAD - HALO, columns + 2 * HALO)
+    middle = [r for r in at.weights_early if r not in at.joined]
+    mids = [
+        Rows(at.total, (mid.at[i], middle), (joined.at[i], at.joined)) for i in range(2)
+    ]
+    swept = [Rows(at.total, (kept.at[i], at.swept_early)) for i in range(2)]
     level.sweep(
-        (right_conc, chem_start), right_side, 1, frame - 2, frame - 2, wide,
-        put_window((conc_mid, chem_mid), wide),
+        (right_side[0], chem_start), right_side, HALO + 1, rows - 2, rows - 2, wide,
+        put_window(mids, wide),
     )
     level.sweep(
-        (conc_mid, chem_mid), right_side, 2, frame - 4, frame - 4, wide,
-        put_window((conc_out, chem_out), (0, wide[1])),
+        mids, right_side, HALO + 2, rows - 4, rows - 4, wide, put_window(swept, (0, wide[1]))
     )
     level.coarse_right(
-        (conc_out, chem_out), right_side, HALO, rows, rows, (PAD, columns), put_sums(sums), wide[0]
-    )
+        swept, right_side, 2 * HALO, rows - 2 * HALO, rows - 2 * HALO, (PAD, columns),
+        put_sums(sums, HALO // 2), wide[0],
+    )
+    own = slice(PAD, PAD + columns)
     for index in range(rows // 2):
         row = HALO + 2 * index
-        own = slice(PAD, PAD + columns)
         sums[2, index] = mobility[row, own, :] + mobility[row + 1, own, :]
-    even = lane_even((columns // 2, lanes), 1)
-    for field in range(3):
-        for index in range(rows // 4):
-            a = pair_rows(sums.at[field], 2 * index, columns // 2)
-            b = pair_rows(sums.at[field], 2 * index + 1, columns // 2)
-            packed[field, index] = 0.125 * jnp.where(
-                even, a + lane_roll(a, -1), b + lane_roll(b, 1)
-            )
+    for index in range(rows // 4):
+        pack(sums, 2, index, packed)
+        if HALO // 4 <= index < (rows - HALO) // 4:
+            pack(sums, 0, index, packed)
+            pack(sums, 1, index, packed)
+        else:
+            packed[0, index] = jnp.zeros(packed.shape[2:], jnp.float32)
+            packed[1, index] = jnp.zeros(packed.shape[2:], jnp.float32)
+
+
+def late_kernel(
+    fields, before, after, own_left, own_right, corner_left, corner_right,
+    packed_early, kept_early, right_early, weights_early, joined,
+    packed, kept, right_conc, all_weights,
+    chem_start, mobility, mid, outer, right_outer, sums,
+):
+    rows, columns = fields.shape[1:3]
+    at = FrameRows(rows)
+    end = at.total
+    right = Rows(
+        end, (right_early, at.own), (right_conc, at.right_late), (right_outer, at.right_outer)
+    )
+    for row in [*range(HALO + 2), *range(end - HALO - 2, end)]:
+        if row in at.own:
+            i = row - HALO
+            values = fields[0, i], fields[1, i], own_left[i], own_right[i]
+            set_row(*values, row, None, chem_start, mobility)
+        else:
+            source, i = (before, row) if row < HALO else (after, row - rows - HALO)
+            corner = row if row < HALO else row - rows
+            values = source[0, i], source[1, i], corner_left[corner], corner_right[corner]
+            set_row(*values, row, right, chem_start, mobility)
+    weights = at.weights(weights_early, all_weights)
+    for i, one in enumerate(weights):
+        for index, row in enumerate(at.weights_outer):
+            one.places[row] = outer.at[i], index
+    level = fine_level(weights)
+    level.set_weights(mobility, HALO + 1, 0)
+    level.set_weights(mobility, HALO + 1, end - HALO - 1)
+    wide = (PAD - HALO, columns + 2 * HALO)
+    mids = [Rows(end, (joined.at[i], at.joined), (mid.at[i], at.mid_late)) for i in range(2)]
+    swept = at.swept(kept_early, kept)
+    for start in (1, end - HALO - 1):
+        level.sweep(
+            (right, chem_start), (right,), start, HALO, HALO, wide, put_window(mids, wide)
+        )
+    for start in (2, end - HALO - 2):
+        level.sweep(mids, (right,), start, HALO, HALO, wide, put_window(swept, (0, wide[1])))
+    for start in (HALO, end - 2 * HALO):
+        level.coarse_right(
+            swept, (right,), start, HALO, HALO, (PAD, columns),
+            put_sums(sums, (start - HALO) // 2), wide[0],
+        )
+    packed[...] = packed_early[...]
+    for index in range(rows // 4):
+        if not HALO // 4 <= index < (rows - HALO) // 4:
+            pack(sums, 0, index, packed)
+            pack(sums, 1, index, packed)
 
 
 def coarse_kernel(
     slots, grid, first, second, first_far, second_far,
-    kept, right_conc, all_weights, conc_new, chem_new, *scratch,
+    kept_early, right_early, weights_early, kept_late, right_late, weights_late,
+    conc_new, chem_new, *scratch,
 ):
-    conc_in, chem_in = kept.at[0], kept.at[1]
-    weights = [all_weights.at[i] for i in range(7)]
+    at = FrameRows(conc_new.shape[0])
+    conc_in, chem_in = at.swept(kept_early, kept_late)
+    weights = at.weights(weights_early, weights_late)
+    right_conc = Rows(at.total, (right_early, at.own), (right_late, at.right_late))
     scratch = list(scratch)
     start_even, at_y = lax.axis_index("gx") % 2 == 0, lax.axis_index("gy")
     levels = []
@@ -678,7 +792,6 @@
 def two_phase_solve(conc, chem):
     rows, columns, lanes = conc.shape
     frame = (rows + 2 * HALO, columns + 2 * PAD, lanes)
-    inner = (frame[0], columns + 2 * HALO, lanes)
     edge = (2, HALO, columns, lanes)
     block = (rows, columns, lanes)
     fields = jnp.concatenate([conc, chem], axis=0).reshape((2,) + block)
@@ -690,11 +803,33 @@
     sides = [shifted(to_right, "gy", 1), shifted(to_left, "gy", -1)]
     to_left, to_right = call_kernel(corners_kernel, (corner, corner), (), before, after)
     sides += [shifted(to_right, "gy", 1), shifted(to_left, "gy", -1)]
-    packed, *kept = call_kernel(
-        fine_down_kernel,
-        ((3, rows // 4, columns // 2, lanes), (2,) + inner, frame, (7,) + inner),
-        (frame,) * 4 + ((3, rows // 2, columns, lanes),),
-        fields, before, after, *sides,
+    at, width = FrameRows(rows), columns + 2 * HALO
+    packed_shape, sums = (3, rows // 4, columns // 2, lanes), (3, rows // 2, columns, lanes)
+
+    def part(count, listed, wide):
+        return (count, len(listed), wide, lanes)
+
+    right_shapes = [part(0, listed, frame[1])[1:] for listed in (at.own, at.right_late, at.right_outer)]
+    early, *kept = call_kernel(
+        early_kernel,
+        (
+            packed_shape, part(2, at.swept_early, width), right_shapes[0],
+            part(7, at.weights_early, width), part(2, at.joined, frame[1]),
+        ),
+        (frame, frame, part(2, at.weights_early, frame[1]), part(7, [0], width), sums),
+        fields, *sides[:2],
+    )
+    packed, *kept_late = call_kernel(
+        late_kernel,
+        (
+            packed_shape, part(2, at.swept_late, width), right_shapes[1],
+            part(7, at.weights_late, width),
+        ),
+        (
+            frame, frame, part(2, at.mid_late, frame[1]), part(7, at.weights_outer, width),
+            right_shapes[2], sums,
+        ),
+        fields, before, after, *sides, early, *kept,
     )
     count_x, count_y = lax.axis_size("gx"), lax.axis_size("gy")
     grids = [(count_x * rows >> level + 1, count_y * columns >> level) for level in range(4)]
@@ -706,7 +841,7 @@
     scratch += [(2, grids[2][0], grids[1][1], lanes), (2, grids[3][0], grids[2][1], lanes)]
     scratch += [(2, rows // 2 + 2, columns + 4 * PAD, lanes)] + [frame] * 4
     kernel = functools.partial(coarse_kernel, slot_masks(), (count_x, count_y))
-    args = (*gathered(packed), *kept)
+    args = (*gathered(packed), *kept[:3], *kept_late)
     return call_kernel(kernel, (block, block), scratch, *args, vmem_mib=24)
 
 

time: 35.2 us -> 34.7 us (0.986)
  waiting for transfers between devices: 11.1 us -> 10.3 us
  Pallas kernels: 5.79 us -> 6.22 us
    ppermute x6, waiting for transfers between devices: 2.73 us -> 1.86 us  [shifted(): lax.ppermute(values, axis, [(i, (i + by) % count) for i in range(count)])]
    pallas_call x4 -> x5, Pallas kernels: 5.79 us -> 6.22 us  [call_kernel(): pl.pallas_call(kernel, out_shape=shapes, in_specs=[whole_block()] * len(a...]
  transfers between devices with their start and end apart: 13 -> 13, of which waited for: 6 -> 6; matrix products, arithmetic and copies ran while one was open for 0% -> 0% of each run, Pallas kernels for 0% -> 3%
where the time goes in v6:
time: 34.7 us; the launch traced here: 34.6 us
  starting transfers between devices  16.4 us (47%)
  waiting for transfers between devices  10.3 us (30%)
  Pallas kernels  6.22 us (18%)
  other arithmetic  1 us (3%)
  between operations  0.71 us (2%)
    ppermute x6, starting transfers between devices, shifted(): lax.ppermute(values, axis, [(i, (i + by) % count) for i in range(count)])  8.7 us
    ppermute x7, waiting for transfers between devices, swapped(): return lax.ppermute(values, axis, [(i, i ^ mask) for i in range(count)])  8.39 us
    ppermute x7, starting transfers between devices, swapped(): return lax.ppermute(values, axis, [(i, i ^ mask) for i in range(count)])  7.69 us
    pallas_call x5, Pallas kernels, call_kernel(): pl.pallas_call(kernel, out_shape=shapes, in_specs=[whole_block()] * len(a...  6.22 us
    ppermute x6, waiting for transfers between devices, shifted(): lax.ppermute(values, axis, [(i, (i + by) % count) for i in range(count)])  1.86 us
    concatenate x1, other arithmetic, two_phase_solve(): fields = jnp.concatenate([conc, chem], axis=0).reshape((2,) + block)  0.99 us
  transfers between devices with their start and end apart: 13, of which 6 were waited for; matrix products, arithmetic and copies ran while one was open for 0% of the time, Pallas kernels for 3%

profile of v6, /device:TPU:0, one launch (start us, length us, event | category | flops | bytes accessed | tf_op | source)
XLA Modules:
  0.0 34.6 jit_solution(9530489209378563351)
XLA Ops:
  0.6 1.0 %pad_maximum_fusion = f32[32,16,128]{2,1,0:T(8,128)S(1)} fusion(f32[16,16,128]{2,1,0:T(8,128)} %param.3, f32[16,16,128]{2,1,0:T(8,128)} %param.2), kind=kLoop, calls=%fused_computation | loop fusion | flops 65536 | bytes 524288 | tf_op jit(solution)/shard_map/concatenate | solution.py:797
  1.6 3.1 %collective-permute-start = (f32[2,4,16,128]{3,2,1,0:T(8,128)S(1)}, f32[2,4,16,128]{3,2,1,0:T(8,128)S(1)}, u32[]{:S(2)}, u32[]{:S(2)}) collective-permute-start(f32[2,4,16,128]{3,2,1,0:T(8,128)S(1)} %get-tuple-element.17), channel_id=1, source_target_pairs={{0,4},{4,8},{8,12},{12,0},{1,5},{5,9},{9,13},{13,1},{2,6},{6,10},{... | collective-permute-start | bytes 196616 | tf_op jit(solution)/shard_map/ppermute | solution.py:764
  4.7 2.1 %collective-permute-start.1 = (f32[2,4,16,128]{3,2,1,0:T(8,128)S(1)}, f32[2,4,16,128]{3,2,1,0:T(8,128)S(1)}, u32[]{:S(2)}, u32[]{:S(2)}) collective-permute-start(f32[2,4,16,128]{3,2,1,0:T(8,128)S(1)} %get-tuple-element.18), channel_id=1, source_target_pairs={{0,12},{4,0},{8,4},{12,8},{1,13},{5,1},{9,5},{13,9},{2,14},{6,2},{... | collective-permute-start | bytes 196616 | tf_op jit(solution)/shard_map/ppermute | solution.py:764
  6.8 0.0 collective-permute-start.2
  6.8 1.7 %collective-permute-start.3 = (f32[16,8,128]{2,1,0:T(8,128)S(1)}, f32[16,8,128]{2,1,0:T(8,128)S(1)}, u32[]{:S(2)}, u32[]{:S(2)}) collective-permute-start(f32[16,8,128]{2,1,0:T(8,128)S(1)} %get-tuple-element.20), channel_id=1, source_target_pairs={{0,3},{1,0},{2,1},{3,2},{4,7},{5,4},{6,5},{7,6},{8,11},{9,8},{10,9... | collective-permute-start | bytes 196616 | tf_op jit(solution)/shard_map/ppermute | solution.py:764
  8.6 0.6 %collective-permute-done.before = f32[2,4,16,128]{3,2,1,0:T(8,128)S(1)} collective-permute-done((f32[2,4,16,128]{3,2,1,0:T(8,128)S(1)}, f32[2,4,16,128]{3,2,1,0:T(8,128)S(1)}, u32[]{:S(2)}, u32[]{:S(2)}) %collective-permute-start) | collective-permute-done | bytes 65568 | tf_op jit(solution)/shard_map/ppermute | solution.py:764
  9.1 0.5 %collective-permute-done.1.after = f32[2,4,16,128]{3,2,1,0:T(8,128)S(1)} collective-permute-done((f32[2,4,16,128]{3,2,1,0:T(8,128)S(1)}, f32[2,4,16,128]{3,2,1,0:T(8,128)S(1)}, u32[]{:S(2)}, u32[]{:S(2)}) %collective-permute-start.1) | collective-permute-done | bytes 65568 | tf_op jit(solution)/shard_map/ppermute | solution.py:764
  9.7 0.1 collective-permute-start.4
  9.8 1.7 %collective-permute-start.5 = (f32[8,8,128]{2,1,0:T(8,128)S(1)}, f32[8,8,128]{2,1,0:T(8,128)S(1)}, u32[]{:S(2)}, u32[]{:S(2)}) collective-permute-start(f32[8,8,128]{2,1,0:T(8,128)S(1)} %get-tuple-element.22), channel_id=1, source_target_pairs={{0,3},{1,0},{2,1},{3,2},{4,7},{5,4},{6,5},{7,6},{8,11},{9,8},{10,9... | collective-permute-start | bytes 98312 | tf_op jit(solution)/shard_map/ppermute | solution.py:764
  11.5 0.0 collective-permute-done.2.own_left
  11.5 0.0 collective-permute-done.3.own_right
  11.5 0.9 %shard_map.43 = (f32[3,4,8,128]{3,2,1,0:T(8,128)S(1)}, f32[2,12,24,128]{3,2,1,0:T(8,128)S(1)}, f32[16,32,128]{2,1,0:T(8,128)S(1)}, f32[7,14,24,128]{3,2,1,0:T(8,128)S(1)}, f32[2,4,32,128]{3,2,1,0:T(8,128)S(1)}) custom-call(f32[2,16,16,128]{3,2,1,0:T(8,128)S(1)} %bitcast.12, f32[16,8,128]{2,1,0:T(8,128)S(1)} %collective-permute-done.2.own_left, ...), custom_call_target="tpu_custom_call" | custom-call | tf_op jit(solution)/shard_map/pallas_call | solution.py:752
  12.4 0.7 %collective-permute-done.4.corner_left = f32[8,8,128]{2,1,0:T(8,128)S(1)} collective-permute-done((f32[8,8,128]{2,1,0:T(8,128)S(1)}, f32[8,8,128]{2,1,0:T(8,128)S(1)}, u32[]{:S(2)}, u32[]{:S(2)}) %collective-permute-start.4) | collective-permute-done | bytes 32800 | tf_op jit(solution)/shard_map/ppermute | solution.py:764
  13.1 0.0 collective-permute-done.5.corner_right
  13.1 0.7 %shard_map.44 = (f32[3,4,8,128]{3,2,1,0:T(8,128)S(1)}, f32[2,8,24,128]{3,2,1,0:T(8,128)S(1)}, f32[2,32,128]{2,1,0:T(8,128)S(1)}, f32[7,5,24,128]{3,2,1,0:T(8,128)S(1)}) custom-call(f32[2,16,16,128]{3,2,1,0:T(8,128)S(1)} %bitcast.13, f32[2,4,16,128]{3,2,1,0:T(8,128)S(1)} %collective-permute-done.before, f32[2,4,16,128]{3,2,1,0:T(8,128)S(1)} %collective-permute-done.1.after, ...), custom_call_target="tpu_custom_call" | custom-call | tf_op jit(solution)/shard_map/pallas_call | solution.py:752
  13.8 3.2 %collective-permute-start.9 = (f32[3,4,8,128]{3,2,1,0:T(8,128)S(1)}, f32[3,4,8,128]{3,2,1,0:T(8,128)S(1)}, u32[]{:S(2)}, u32[]{:S(2)}) collective-permute-start(f32[3,4,8,128]{3,2,1,0:T(8,128)S(1)} %get-tuple-element.28), channel_id=1, source_target_pairs={{0,12},{4,8},{8,4},{12,0},{1,13},{5,9},{9,5},{13,1},{2,14},{6,10},... | collective-permute-start | bytes 147464 | tf_op jit(solution)/shard_map/ppermute | solution.py:769
  17.0 0.0 collective-permute-start.8
  17.0 1.2 %collective-permute-start.7 = (f32[3,4,8,128]{3,2,1,0:T(8,128)S(1)}, f32[3,4,8,128]{3,2,1,0:T(8,128)S(1)}, u32[]{:S(2)}, u32[]{:S(2)}) collective-permute-start(f32[3,4,8,128]{3,2,1,0:T(8,128)S(1)} %get-tuple-element.28), channel_id=1, source_target_pairs={{0,4},{4,0},{8,12},{12,8},{1,5},{5,1},{9,13},{13,9},{2,6},{6,2},{1... | collective-permute-start | bytes 147464 | tf_op jit(solution)/shard_map/ppermute | solution.py:769
  18.2 1.5 %collective-permute-start.6 = (f32[3,4,8,128]{3,2,1,0:T(8,128)S(1)}, f32[3,4,8,128]{3,2,1,0:T(8,128)S(1)}, u32[]{:S(2)}, u32[]{:S(2)}) collective-permute-start(f32[3,4,8,128]{3,2,1,0:T(8,128)S(1)} %get-tuple-element.28), channel_id=1, source_target_pairs={{0,2},{1,3},{2,0},{3,1},{4,6},{5,7},{6,4},{7,5},{8,10},{9,11},{10,... | collective-permute-start | bytes 147464 | tf_op jit(solution)/shard_map/ppermute | solution.py:769
  19.7 0.0 collective-permute-done.9
  19.7 2.5 %collective-permute-done.8 = f32[3,4,8,128]{3,2,1,0:T(8,128)S(1)} collective-permute-done((f32[3,4,8,128]{3,2,1,0:T(8,128)S(1)}, f32[3,4,8,128]{3,2,1,0:T(8,128)S(1)}, u32[]{:S(2)}, u32[]{:S(2)}) %collective-permute-start.8) | collective-permute-done | bytes 49184 | tf_op jit(solution)/shard_map/ppermute | solution.py:769
  22.2 0.0 collective-permute-done.7
  22.2 1.7 %collective-permute-start.10 = (f32[3,3,4,8,128]{4,3,2,1,0:T(8,128)S(1)}, f32[3,3,4,8,128]{4,3,2,1,0:T(8,128)S(1)}, u32[]{:S(2)}, u32[]{:S(2)}) collective-permute-start(f32[3,3,4,8,128]{4,3,2,1,0:T(8,128)S(1)} %pad_maximum_fusion.1), channel_id=1, source_target_pairs={{0,2},{1,3},{2,0},{3,1},{4,6},{5,7},{6,4},{7,5},{8,10},{9,11},{10,... | collective-permute-start | bytes 442376 | tf_op jit(solution)/shard_map/ppermute | solution.py:769
  23.9 0.0 collective-permute-done.6
  23.9 0.1 collective-permute-start.11
  24.0 4.6 %collective-permute-done.10.second = f32[3,3,4,8,128]{4,3,2,1,0:T(8,128)S(1)} collective-permute-done((f32[3,3,4,8,128]{4,3,2,1,0:T(8,128)S(1)}, f32[3,3,4,8,128]{4,3,2,1,0:T(8,128)S(1)}, u32[]{:S(2)}, u32[]{:S(2)}) %collective-permute-start.10) | collective-permute-done | bytes 147488 | tf_op jit(solution)/shard_map/ppermute | solution.py:769
  28.6 0.0 collective-permute-start.12
  28.6 0.0 collective-permute-done.11.first_far
  28.6 1.4 %collective-permute-done.12.second_far = f32[3,3,4,8,128]{4,3,2,1,0:T(8,128)S(1)} collective-permute-done((f32[3,3,4,8,128]{4,3,2,1,0:T(8,128)S(1)}, f32[3,3,4,8,128]{4,3,2,1,0:T(8,128)S(1)}, u32[]{:S(2)}, u32[]{:S(2)}) %collective-permute-start.12) | collective-permute-done | bytes 147488 | tf_op jit(solution)/shard_map/ppermute | solution.py:769
  29.9 4.7 %shard_map.45 = (f32[16,16,128]{2,1,0:T(8,128)}, f32[16,16,128]{2,1,0:T(8,128)}) custom-call(f32[5,3,4,8,128]{4,3,2,1,0:T(8,128)S(1)} %constant_dynamic-update-slice_fusion.first, f32[3,3,4,8,128]{4,3,2,1,0:T(8,128)S(1)} %collective-permute-done.10.second, f32[5,3,4,8,128]{4,3,2,1,0:T(8,128)S(1)} %collective-permute-done.11.first_far, ...), custom_call_target="tpu_custom_call" | custom-call | tf_op jit(solution)/shard_map/pallas_call | solution.py:752
  (8 shorter events, 0.1 us)
Async XLA Ops:
  1.6 7.5 %collective-permute-start = (f32[2,4,16,128]{3,2,1,0:T(8,128)S(1)}, f32[2,4,16,128]{3,2,1,0:T(8,128)S(1)}, u32[]{:S(2)}, u32[]{:S(2)}) collective-permute-start(f32[2,4,16,128]{3,2,1,0:T(8,128)S(1)} %get-tuple-element.17), channel_id=1, source_target_pairs={{0,4},{4,8},{8,12},{12,0},{1,5},{5,9},{9,13},{13,1},{2,6},{6,10},{... | collective-permute-start | bytes 196616 | tf_op jit(solution)/shard_map/ppermute | solution.py:764
  4.7 5.0 %collective-permute-start.1 = (f32[2,4,16,128]{3,2,1,0:T(8,128)S(1)}, f32[2,4,16,128]{3,2,1,0:T(8,128)S(1)}, u32[]{:S(2)}, u32[]{:S(2)}) collective-permute-start(f32[2,4,16,128]{3,2,1,0:T(8,128)S(1)} %get-tuple-element.18), channel_id=1, source_target_pairs={{0,12},{4,0},{8,4},{12,8},{1,13},{5,1},{9,5},{13,9},{2,14},{6,2},{... | collective-permute-start | bytes 196616 | tf_op jit(solution)/shard_map/ppermute | solution.py:764
  6.8 4.7 %collective-permute-start.2 = (f32[16,8,128]{2,1,0:T(8,128)S(1)}, f32[16,8,128]{2,1,0:T(8,128)S(1)}, u32[]{:S(2)}, u32[]{:S(2)}) collective-permute-start(f32[16,8,128]{2,1,0:T(8,128)S(1)} %get-tuple-element.19), channel_id=1, source_target_pairs={{0,1},{1,2},{2,3},{3,0},{4,5},{5,6},{6,7},{7,4},{8,9},{9,10},{10,1... | collective-permute-start | bytes 196616 | tf_op jit(solution)/shard_map/ppermute | solution.py:764
  6.8 4.7 %collective-permute-start.3 = (f32[16,8,128]{2,1,0:T(8,128)S(1)}, f32[16,8,128]{2,1,0:T(8,128)S(1)}, u32[]{:S(2)}, u32[]{:S(2)}) collective-permute-start(f32[16,8,128]{2,1,0:T(8,128)S(1)} %get-tuple-element.20), channel_id=1, source_target_pairs={{0,3},{1,0},{2,1},{3,2},{4,7},{5,4},{6,5},{7,6},{8,11},{9,8},{10,9... | collective-permute-start | bytes 196616 | tf_op jit(solution)/shard_map/ppermute | solution.py:764
  9.7 3.4 %collective-permute-start.4 = (f32[8,8,128]{2,1,0:T(8,128)S(1)}, f32[8,8,128]{2,1,0:T(8,128)S(1)}, u32[]{:S(2)}, u32[]{:S(2)}) collective-permute-start(f32[8,8,128]{2,1,0:T(8,128)S(1)} %get-tuple-element.21), channel_id=1, source_target_pairs={{0,1},{1,2},{2,3},{3,0},{4,5},{5,6},{6,7},{7,4},{8,9},{9,10},{10,1... | collective-permute-start | bytes 98312 | tf_op jit(solution)/shard_map/ppermute | solution.py:764
  9.8 3.3 %collective-permute-start.5 = (f32[8,8,128]{2,1,0:T(8,128)S(1)}, f32[8,8,128]{2,1,0:T(8,128)S(1)}, u32[]{:S(2)}, u32[]{:S(2)}) collective-permute-start(f32[8,8,128]{2,1,0:T(8,128)S(1)} %get-tuple-element.22), channel_id=1, source_target_pairs={{0,3},{1,0},{2,1},{3,2},{4,7},{5,4},{6,5},{7,6},{8,11},{9,8},{10,9... | collective-permute-start | bytes 98312 | tf_op jit(solution)/shard_map/ppermute | solution.py:764
  13.8 5.9 %collective-permute-start.9 = (f32[3,4,8,128]{3,2,1,0:T(8,128)S(1)}, f32[3,4,8,128]{3,2,1,0:T(8,128)S(1)}, u32[]{:S(2)}, u32[]{:S(2)}) collective-permute-start(f32[3,4,8,128]{3,2,1,0:T(8,128)S(1)} %get-tuple-element.28), channel_id=1, source_target_pairs={{0,12},{4,8},{8,4},{12,0},{1,13},{5,9},{9,5},{13,1},{2,14},{6,10},... | collective-permute-start | bytes 147464 | tf_op jit(solution)/shard_map/ppermute | solution.py:769
  17.0 5.2 %collective-permute-start.8 = (f32[3,4,8,128]{3,2,1,0:T(8,128)S(1)}, f32[3,4,8,128]{3,2,1,0:T(8,128)S(1)}, u32[]{:S(2)}, u32[]{:S(2)}) collective-permute-start(f32[3,4,8,128]{3,2,1,0:T(8,128)S(1)} %get-tuple-element.28), channel_id=1, source_target_pairs={{0,8},{4,12},{8,0},{12,4},{1,9},{5,13},{9,1},{13,5},{2,10},{6,14},... | collective-permute-start | bytes 147464 | tf_op jit(solution)/shard_map/ppermute | solution.py:769
  17.0 5.2 %collective-permute-start.7 = (f32[3,4,8,128]{3,2,1,0:T(8,128)S(1)}, f32[3,4,8,128]{3,2,1,0:T(8,128)S(1)}, u32[]{:S(2)}, u32[]{:S(2)}) collective-permute-start(f32[3,4,8,128]{3,2,1,0:T(8,128)S(1)} %get-tuple-element.28), channel_id=1, source_target_pairs={{0,4},{4,0},{8,12},{12,8},{1,5},{5,1},{9,13},{13,9},{2,6},{6,2},{1... | collective-permute-start | bytes 147464 | tf_op jit(solution)/shard_map/ppermute | solution.py:769
  18.2 5.7 %collective-permute-start.6 = (f32[3,4,8,128]{3,2,1,0:T(8,128)S(1)}, f32[3,4,8,128]{3,2,1,0:T(8,128)S(1)}, u32[]{:S(2)}, u32[]{:S(2)}) collective-permute-start(f32[3,4,8,128]{3,2,1,0:T(8,128)S(1)} %get-tuple-element.28), channel_id=1, source_target_pairs={{0,2},{1,3},{2,0},{3,1},{4,6},{5,7},{6,4},{7,5},{8,10},{9,11},{10,... | collective-permute-start | bytes 147464 | tf_op jit(solution)/shard_map/ppermute | solution.py:769
  22.2 6.4 %collective-permute-start.10 = (f32[3,3,4,8,128]{4,3,2,1,0:T(8,128)S(1)}, f32[3,3,4,8,128]{4,3,2,1,0:T(8,128)S(1)}, u32[]{:S(2)}, u32[]{:S(2)}) collective-permute-start(f32[3,3,4,8,128]{4,3,2,1,0:T(8,128)S(1)} %pad_maximum_fusion.1), channel_id=1, source_target_pairs={{0,2},{1,3},{2,0},{3,1},{4,6},{5,7},{6,4},{7,5},{8,10},{9,11},{10,... | collective-permute-start | bytes 442376 | tf_op jit(solution)/shard_map/ppermute | solution.py:769
  23.9 4.6 %collective-permute-start.11 = (f32[5,3,4,8,128]{4,3,2,1,0:T(8,128)S(1)}, f32[5,3,4,8,128]{4,3,2,1,0:T(8,128)S(1)}, u32[]{:S(2)}, u32[]{:S(2)}) collective-permute-start(f32[5,3,4,8,128]{4,3,2,1,0:T(8,128)S(1)} %constant_dynamic-update-slice_fusion.first), channel_id=1, source_target_pairs={{0,1},{1,0},{2,3},{3,2},{4,5},{5,4},{6,7},{7,6},{8,9},{9,8},{10,11... | collective-permute-start | bytes 737288 | tf_op jit(solution)/shard_map/ppermute | solution.py:769
  28.6 1.4 %collective-permute-start.12 = (f32[3,3,4,8,128]{4,3,2,1,0:T(8,128)S(1)}, f32[3,3,4,8,128]{4,3,2,1,0:T(8,128)S(1)}, u32[]{:S(2)}, u32[]{:S(2)}) collective-permute-start(f32[3,3,4,8,128]{4,3,2,1,0:T(8,128)S(1)} %collective-permute-done.10.second), channel_id=1, source_target_pairs={{0,1},{1,0},{2,3},{3,2},{4,5},{5,4},{6,7},{7,6},{8,9},{9,8},{10,11... | collective-permute-start | bytes 442376 | tf_op jit(solution)/shard_map/ppermute | solution.py:769

commit v7 on v6

--- a/solution.py
+++ b/solution.py
@@ -777,15 +777,30 @@
 def slot_masks():
     along_x, along_y = far_masks()
     first = [(0, 0)] + [(0, y) for y in along_y] + [(x, 0) for x in along_x]
-    return first, [(x, y) for y in along_y for x in along_x]
+    second = [(x, y) for y in along_y for x in along_x[1:]]
+    return first, second + [(along_x[0], y) for y in along_y]
+
+
+def swapped_both(values, mask_x, mask_y):
+    count_x, count_y = lax.axis_size("gx"), lax.axis_size("gy")
+    pairs = [
+        (x * count_y + y, (x ^ mask_x) * count_y + (y ^ mask_y))
+        for x in range(count_x)
+        for y in range(count_y)
+    ]
+    return lax.ppermute(values, ("gx", "gy"), pairs)
 
 
 def gathered(values):
     along_x, along_y = far_masks()
-    across = jnp.stack([swapped(values, "gx", mask) for mask in along_x])
+    across = [swapped(values, "gx", mask) for mask in along_x]
     beside = [swapped(values, "gy", mask) for mask in along_y]
-    first = jnp.concatenate([jnp.stack([values] + beside), across], axis=0)
-    second = jnp.concatenate([swapped(across, "gy", mask) for mask in along_y], axis=0)
+    later, _ = lax.optimization_barrier((values, across[2]))
+    corner = [swapped_both(later, along_x[0], mask) for mask in along_y]
+    last = jnp.stack(across[1:])
+    first = jnp.stack([values] + beside + across)
+    second = [swapped(last, "gy", mask) for mask in along_y]
+    second = jnp.concatenate(second + [jnp.stack(corner)], axis=0)
     return first, second, swapped(first, "gy", 1), swapped(second, "gy", 1)
 
 

time: 34.7 us -> 33.5 us (0.965)
  waiting for transfers between devices: 10.3 us -> 8.16 us
  starting transfers between devices: 16.4 us -> 17.2 us
    ppermute x7, waiting for transfers between devices: 8.39 us -> 5.25 us  [swapped(): return lax.ppermute(values, axis, [(i, i ^ mask) for i in range(count)])]
    ppermute x0 -> x1, waiting for transfers between devices: none -> 1.04 us  [swapped_both(): return lax.ppermute(values, ('gx', 'gy'), pairs)]
    ppermute x0 -> x1, starting transfers between devices: none -> 0.85 us  [swapped_both(): return lax.ppermute(values, ('gx', 'gy'), pairs)]
  transfers between devices with their start and end apart: 13 -> 14, of which waited for: 6 -> 7; matrix products, arithmetic and copies ran while one was open for 0% -> 0% of each run, Pallas kernels for 3% -> 3%
where the time goes in v7:
time: 33.5 us; the launch traced here: 33.3 us
  starting transfers between devices  17.2 us (51%)
  waiting for transfers between devices  8.16 us (24%)
  Pallas kernels  6.22 us (19%)
  other arithmetic  1 us (3%)
  between operations  0.72 us (2%)
    ppermute x6, starting transfers between devices, shifted(): lax.ppermute(values, axis, [(i, (i + by) % count) for i in range(count)])  8.7 us
    ppermute x7, starting transfers between devices, swapped(): return lax.ppermute(values, axis, [(i, i ^ mask) for i in range(count)])  7.66 us
    pallas_call x5, Pallas kernels, call_kernel(): pl.pallas_call(kernel, out_shape=shapes, in_specs=[whole_block()] * len(a...  6.22 us
    ppermute x7, waiting for transfers between devices, swapped(): return lax.ppermute(values, axis, [(i, i ^ mask) for i in range(count)])  5.25 us
    ppermute x6, waiting for transfers between devices, shifted(): lax.ppermute(values, axis, [(i, (i + by) % count) for i in range(count)])  1.86 us
    ppermute x1, waiting for transfers between devices, swapped_both(): return lax.ppermute(values, ('gx', 'gy'), pairs)  1.04 us
    concatenate x1, other arithmetic, two_phase_solve(): fields = jnp.concatenate([conc, chem], axis=0).reshape((2,) + block)  0.99 us
    ppermute x1, starting transfers between devices, swapped_both(): return lax.ppermute(values, ('gx', 'gy'), pairs)  0.85 us
  transfers between devices with their start and end apart: 14, of which 7 were waited for; matrix products, arithmetic and copies ran while one was open for 0% of the time, Pallas kernels for 3%

profile of v7, /device:TPU:0, one launch (start us, length us, event | category | flops | bytes accessed | tf_op | source)
XLA Modules:
  0.0 33.3 jit_solution(17186946190229728720)
XLA Ops:
  0.6 1.0 %pad_maximum_fusion = f32[32,16,128]{2,1,0:T(8,128)S(1)} fusion(f32[16,16,128]{2,1,0:T(8,128)} %param.3, f32[16,16,128]{2,1,0:T(8,128)} %param.2), kind=kLoop, calls=%fused_computation | loop fusion | flops 65536 | bytes 524288 | tf_op jit(solution)/shard_map/concatenate | solution.py:812
  1.6 3.1 %collective-permute-start = (f32[2,4,16,128]{3,2,1,0:T(8,128)S(1)}, f32[2,4,16,128]{3,2,1,0:T(8,128)S(1)}, u32[]{:S(2)}, u32[]{:S(2)}) collective-permute-start(f32[2,4,16,128]{3,2,1,0:T(8,128)S(1)} %get-tuple-element.18), channel_id=1, source_target_pairs={{0,4},{4,8},{8,12},{12,0},{1,5},{5,9},{9,13},{13,1},{2,6},{6,10},{... | collective-permute-start | bytes 196616 | tf_op jit(solution)/shard_map/ppermute | solution.py:764
  4.7 2.1 %collective-permute-start.1 = (f32[2,4,16,128]{3,2,1,0:T(8,128)S(1)}, f32[2,4,16,128]{3,2,1,0:T(8,128)S(1)}, u32[]{:S(2)}, u32[]{:S(2)}) collective-permute-start(f32[2,4,16,128]{3,2,1,0:T(8,128)S(1)} %get-tuple-element.19), channel_id=1, source_target_pairs={{0,12},{4,0},{8,4},{12,8},{1,13},{5,1},{9,5},{13,9},{2,14},{6,2},{... | collective-permute-start | bytes 196616 | tf_op jit(solution)/shard_map/ppermute | solution.py:764
  6.8 0.0 collective-permute-start.2
  6.8 1.7 %collective-permute-start.3 = (f32[16,8,128]{2,1,0:T(8,128)S(1)}, f32[16,8,128]{2,1,0:T(8,128)S(1)}, u32[]{:S(2)}, u32[]{:S(2)}) collective-permute-start(f32[16,8,128]{2,1,0:T(8,128)S(1)} %get-tuple-element.21), channel_id=1, source_target_pairs={{0,3},{1,0},{2,1},{3,2},{4,7},{5,4},{6,5},{7,6},{8,11},{9,8},{10,9... | collective-permute-start | bytes 196616 | tf_op jit(solution)/shard_map/ppermute | solution.py:764
  8.6 0.6 %collective-permute-done.before = f32[2,4,16,128]{3,2,1,0:T(8,128)S(1)} collective-permute-done((f32[2,4,16,128]{3,2,1,0:T(8,128)S(1)}, f32[2,4,16,128]{3,2,1,0:T(8,128)S(1)}, u32[]{:S(2)}, u32[]{:S(2)}) %collective-permute-start) | collective-permute-done | bytes 65568 | tf_op jit(solution)/shard_map/ppermute | solution.py:764
  9.1 0.5 %collective-permute-done.1.after = f32[2,4,16,128]{3,2,1,0:T(8,128)S(1)} collective-permute-done((f32[2,4,16,128]{3,2,1,0:T(8,128)S(1)}, f32[2,4,16,128]{3,2,1,0:T(8,128)S(1)}, u32[]{:S(2)}, u32[]{:S(2)}) %collective-permute-start.1) | collective-permute-done | bytes 65568 | tf_op jit(solution)/shard_map/ppermute | solution.py:764
  9.7 0.1 collective-permute-start.4
  9.8 1.7 %collective-permute-start.5 = (f32[8,8,128]{2,1,0:T(8,128)S(1)}, f32[8,8,128]{2,1,0:T(8,128)S(1)}, u32[]{:S(2)}, u32[]{:S(2)}) collective-permute-start(f32[8,8,128]{2,1,0:T(8,128)S(1)} %get-tuple-element.23), channel_id=1, source_target_pairs={{0,3},{1,0},{2,1},{3,2},{4,7},{5,4},{6,5},{7,6},{8,11},{9,8},{10,9... | collective-permute-start | bytes 98312 | tf_op jit(solution)/shard_map/ppermute | solution.py:764
  11.5 0.0 collective-permute-done.2.own_left
  11.5 0.0 collective-permute-done.3.own_right
  11.5 0.9 %shard_map.43 = (f32[3,4,8,128]{3,2,1,0:T(8,128)S(1)}, f32[2,12,24,128]{3,2,1,0:T(8,128)S(1)}, f32[16,32,128]{2,1,0:T(8,128)S(1)}, f32[7,14,24,128]{3,2,1,0:T(8,128)S(1)}, f32[2,4,32,128]{3,2,1,0:T(8,128)S(1)}) custom-call(f32[2,16,16,128]{3,2,1,0:T(8,128)S(1)} %bitcast.13, f32[16,8,128]{2,1,0:T(8,128)S(1)} %collective-permute-done.2.own_left, ...), custom_call_target="tpu_custom_call" | custom-call | tf_op jit(solution)/shard_map/pallas_call | solution.py:752
  12.4 0.7 %collective-permute-done.4.corner_left = f32[8,8,128]{2,1,0:T(8,128)S(1)} collective-permute-done((f32[8,8,128]{2,1,0:T(8,128)S(1)}, f32[8,8,128]{2,1,0:T(8,128)S(1)}, u32[]{:S(2)}, u32[]{:S(2)}) %collective-permute-start.4) | collective-permute-done | bytes 32800 | tf_op jit(solution)/shard_map/ppermute | solution.py:764
  13.1 0.0 collective-permute-done.5.corner_right
  13.1 0.7 %shard_map.44 = (f32[3,4,8,128]{3,2,1,0:T(8,128)S(1)}, f32[2,8,24,128]{3,2,1,0:T(8,128)S(1)}, f32[2,32,128]{2,1,0:T(8,128)S(1)}, f32[7,5,24,128]{3,2,1,0:T(8,128)S(1)}) custom-call(f32[2,16,16,128]{3,2,1,0:T(8,128)S(1)} %bitcast.14, f32[2,4,16,128]{3,2,1,0:T(8,128)S(1)} %collective-permute-done.before, f32[2,4,16,128]{3,2,1,0:T(8,128)S(1)} %collective-permute-done.1.after, ...), custom_call_target="tpu_custom_call" | custom-call | tf_op jit(solution)/shard_map/pallas_call | solution.py:752
  13.8 3.2 %collective-permute-start.9 = (f32[3,4,8,128]{3,2,1,0:T(8,128)S(1)}, f32[3,4,8,128]{3,2,1,0:T(8,128)S(1)}, u32[]{:S(2)}, u32[]{:S(2)}) collective-permute-start(f32[3,4,8,128]{3,2,1,0:T(8,128)S(1)} %get-tuple-element.30), channel_id=1, source_target_pairs={{0,12},{4,8},{8,4},{12,0},{1,13},{5,9},{9,5},{13,1},{2,14},{6,10},... | collective-permute-start | bytes 147464 | tf_op jit(solution)/shard_map/ppermute | solution.py:769
  17.0 0.0 collective-permute-start.8
  17.0 1.2 %collective-permute-start.7 = (f32[3,4,8,128]{3,2,1,0:T(8,128)S(1)}, f32[3,4,8,128]{3,2,1,0:T(8,128)S(1)}, u32[]{:S(2)}, u32[]{:S(2)}) collective-permute-start(f32[3,4,8,128]{3,2,1,0:T(8,128)S(1)} %get-tuple-element.30), channel_id=1, source_target_pairs={{0,4},{4,0},{8,12},{12,8},{1,5},{5,1},{9,13},{13,9},{2,6},{6,2},{1... | collective-permute-start | bytes 147464 | tf_op jit(solution)/shard_map/ppermute | solution.py:769
  18.2 1.5 %collective-permute-start.6 = (f32[3,4,8,128]{3,2,1,0:T(8,128)S(1)}, f32[3,4,8,128]{3,2,1,0:T(8,128)S(1)}, u32[]{:S(2)}, u32[]{:S(2)}) collective-permute-start(f32[3,4,8,128]{3,2,1,0:T(8,128)S(1)} %get-tuple-element.30), channel_id=1, source_target_pairs={{0,2},{1,3},{2,0},{3,1},{4,6},{5,7},{6,4},{7,5},{8,10},{9,11},{10,... | collective-permute-start | bytes 147464 | tf_op jit(solution)/shard_map/ppermute | solution.py:769
  19.7 0.0 collective-permute-done.9
  19.7 0.8 %collective-permute-start.11 = (f32[3,4,8,128]{3,2,1,0:T(8,128)S(1)}, f32[3,4,8,128]{3,2,1,0:T(8,128)S(1)}, u32[]{:S(2)}, u32[]{:S(2)}) collective-permute-start(f32[3,4,8,128]{3,2,1,0:T(8,128)S(1)} %get-tuple-element.30), channel_id=1, source_target_pairs={{0,6},{1,7},{2,4},{3,5},{4,2},{5,3},{6,0},{7,1},{8,14},{9,15},{10,... | collective-permute-start | bytes 147464 | tf_op jit(solution)/shard_map/ppermute | solution.py:791
  20.6 1.6 %collective-permute-done.8 = f32[3,4,8,128]{3,2,1,0:T(8,128)S(1)} collective-permute-done((f32[3,4,8,128]{3,2,1,0:T(8,128)S(1)}, f32[3,4,8,128]{3,2,1,0:T(8,128)S(1)}, u32[]{:S(2)}, u32[]{:S(2)}) %collective-permute-start.8) | collective-permute-done | bytes 49184 | tf_op jit(solution)/shard_map/ppermute | solution.py:769
  22.2 1.6 %collective-permute-start.10 = (f32[2,3,4,8,128]{4,3,2,1,0:T(8,128)S(1)}, f32[2,3,4,8,128]{4,3,2,1,0:T(8,128)S(1)}, u32[]{:S(2)}, u32[]{:S(2)}) collective-permute-start(f32[2,3,4,8,128]{4,3,2,1,0:T(8,128)S(1)} %pad_maximum_fusion.2), channel_id=1, source_target_pairs={{0,2},{1,3},{2,0},{3,1},{4,6},{5,7},{6,4},{7,5},{8,10},{9,11},{10,... | collective-permute-start | bytes 294920 | tf_op jit(solution)/shard_map/ppermute | solution.py:769
  23.8 0.0 collective-permute-done.6
  23.8 0.0 collective-permute-done.7
  23.8 0.1 collective-permute-start.12
  23.9 1.0 %collective-permute-done.11 = f32[3,4,8,128]{3,2,1,0:T(8,128)S(1)} collective-permute-done((f32[3,4,8,128]{3,2,1,0:T(8,128)S(1)}, f32[3,4,8,128]{3,2,1,0:T(8,128)S(1)}, u32[]{:S(2)}, u32[]{:S(2)}) %collective-permute-start.11) | collective-permute-done | bytes 49184 | tf_op jit(solution)/shard_map/ppermute | solution.py:791
  25.0 2.3 %collective-permute-done.10 = f32[2,3,4,8,128]{4,3,2,1,0:T(8,128)S(1)} collective-permute-done((f32[2,3,4,8,128]{4,3,2,1,0:T(8,128)S(1)}, f32[2,3,4,8,128]{4,3,2,1,0:T(8,128)S(1)}, u32[]{:S(2)}, u32[]{:S(2)}) %collective-permute-start.10) | collective-permute-done | bytes 98336 | tf_op jit(solution)/shard_map/ppermute | solution.py:769
  27.2 0.1 collective-permute-start.13
  27.3 1.4 %collective-permute-done.13.second_far = f32[3,3,4,8,128]{4,3,2,1,0:T(8,128)S(1)} collective-permute-done((f32[3,3,4,8,128]{4,3,2,1,0:T(8,128)S(1)}, f32[3,3,4,8,128]{4,3,2,1,0:T(8,128)S(1)}, u32[]{:S(2)}, u32[]{:S(2)}) %collective-permute-start.13) | collective-permute-done | bytes 147488 | tf_op jit(solution)/shard_map/ppermute | solution.py:769
  28.7 0.0 collective-permute-done.12.first_far
  28.7 4.7 %shard_map.45 = (f32[16,16,128]{2,1,0:T(8,128)}, f32[16,16,128]{2,1,0:T(8,128)}) custom-call(f32[5,3,4,8,128]{4,3,2,1,0:T(8,128)S(1)} %constant_dynamic-update-slice_fusion.first, f32[3,3,4,8,128]{4,3,2,1,0:T(8,128)S(1)} %pad_maximum_fusion.1.second, f32[5,3,4,8,128]{4,3,2,1,0:T(8,128)S(1)} %collective-permute-done.12.first_far, ...), custom_call_target="tpu_custom_call" | custom-call | tf_op jit(solution)/shard_map/pallas_call | solution.py:752
  (9 shorter events, 0.1 us)
Async XLA Ops:
  1.6 7.5 %collective-permute-start = (f32[2,4,16,128]{3,2,1,0:T(8,128)S(1)}, f32[2,4,16,128]{3,2,1,0:T(8,128)S(1)}, u32[]{:S(2)}, u32[]{:S(2)}) collective-permute-start(f32[2,4,16,128]{3,2,1,0:T(8,128)S(1)} %get-tuple-element.18), channel_id=1, source_target_pairs={{0,4},{4,8},{8,12},{12,0},{1,5},{5,9},{9,13},{13,1},{2,6},{6,10},{... | collective-permute-start | bytes 196616 | tf_op jit(solution)/shard_map/ppermute | solution.py:764
  4.7 5.0 %collective-permute-start.1 = (f32[2,4,16,128]{3,2,1,0:T(8,128)S(1)}, f32[2,4,16,128]{3,2,1,0:T(8,128)S(1)}, u32[]{:S(2)}, u32[]{:S(2)}) collective-permute-start(f32[2,4,16,128]{3,2,1,0:T(8,128)S(1)} %get-tuple-element.19), channel_id=1, source_target_pairs={{0,12},{4,0},{8,4},{12,8},{1,13},{5,1},{9,5},{13,9},{2,14},{6,2},{... | collective-permute-start | bytes 196616 | tf_op jit(solution)/shard_map/ppermute | solution.py:764
  6.8 4.7 %collective-permute-start.2 = (f32[16,8,128]{2,1,0:T(8,128)S(1)}, f32[16,8,128]{2,1,0:T(8,128)S(1)}, u32[]{:S(2)}, u32[]{:S(2)}) collective-permute-start(f32[16,8,128]{2,1,0:T(8,128)S(1)} %get-tuple-element.20), channel_id=1, source_target_pairs={{0,1},{1,2},{2,3},{3,0},{4,5},{5,6},{6,7},{7,4},{8,9},{9,10},{10,1... | collective-permute-start | bytes 196616 | tf_op jit(solution)/shard_map/ppermute | solution.py:764
  6.8 4.7 %collective-permute-start.3 = (f32[16,8,128]{2,1,0:T(8,128)S(1)}, f32[16,8,128]{2,1,0:T(8,128)S(1)}, u32[]{:S(2)}, u32[]{:S(2)}) collective-permute-start(f32[16,8,128]{2,1,0:T(8,128)S(1)} %get-tuple-element.21), channel_id=1, source_target_pairs={{0,3},{1,0},{2,1},{3,2},{4,7},{5,4},{6,5},{7,6},{8,11},{9,8},{10,9... | collective-permute-start | bytes 196616 | tf_op jit(solution)/shard_map/ppermute | solution.py:764
  9.7 3.4 %collective-permute-start.4 = (f32[8,8,128]{2,1,0:T(8,128)S(1)}, f32[8,8,128]{2,1,0:T(8,128)S(1)}, u32[]{:S(2)}, u32[]{:S(2)}) collective-permute-start(f32[8,8,128]{2,1,0:T(8,128)S(1)} %get-tuple-element.22), channel_id=1, source_target_pairs={{0,1},{1,2},{2,3},{3,0},{4,5},{5,6},{6,7},{7,4},{8,9},{9,10},{10,1... | collective-permute-start | bytes 98312 | tf_op jit(solution)/shard_map/ppermute | solution.py:764
  9.8 3.3 %collective-permute-start.5 = (f32[8,8,128]{2,1,0:T(8,128)S(1)}, f32[8,8,128]{2,1,0:T(8,128)S(1)}, u32[]{:S(2)}, u32[]{:S(2)}) collective-permute-start(f32[8,8,128]{2,1,0:T(8,128)S(1)} %get-tuple-element.23), channel_id=1, source_target_pairs={{0,3},{1,0},{2,1},{3,2},{4,7},{5,4},{6,5},{7,6},{8,11},{9,8},{10,9... | collective-permute-start | bytes 98312 | tf_op jit(solution)/shard_map/ppermute | solution.py:764
  13.8 5.9 %collective-permute-start.9 = (f32[3,4,8,128]{3,2,1,0:T(8,128)S(1)}, f32[3,4,8,128]{3,2,1,0:T(8,128)S(1)}, u32[]{:S(2)}, u32[]{:S(2)}) collective-permute-start(f32[3,4,8,128]{3,2,1,0:T(8,128)S(1)} %get-tuple-element.30), channel_id=1, source_target_pairs={{0,12},{4,8},{8,4},{12,0},{1,13},{5,9},{9,5},{13,1},{2,14},{6,10},... | collective-permute-start | bytes 147464 | tf_op jit(solution)/shard_map/ppermute | solution.py:769
  17.0 5.2 %collective-permute-start.8 = (f32[3,4,8,128]{3,2,1,0:T(8,128)S(1)}, f32[3,4,8,128]{3,2,1,0:T(8,128)S(1)}, u32[]{:S(2)}, u32[]{:S(2)}) collective-permute-start(f32[3,4,8,128]{3,2,1,0:T(8,128)S(1)} %get-tuple-element.30), channel_id=1, source_target_pairs={{0,8},{4,12},{8,0},{12,4},{1,9},{5,13},{9,1},{13,5},{2,10},{6,14},... | collective-permute-start | bytes 147464 | tf_op jit(solution)/shard_map/ppermute | solution.py:769
  17.0 6.8 %collective-permute-start.7 = (f32[3,4,8,128]{3,2,1,0:T(8,128)S(1)}, f32[3,4,8,128]{3,2,1,0:T(8,128)S(1)}, u32[]{:S(2)}, u32[]{:S(2)}) collective-permute-start(f32[3,4,8,128]{3,2,1,0:T(8,128)S(1)} %get-tuple-element.30), channel_id=1, source_target_pairs={{0,4},{4,0},{8,12},{12,8},{1,5},{5,1},{9,13},{13,9},{2,6},{6,2},{1... | collective-permute-start | bytes 147464 | tf_op jit(solution)/shard_map/ppermute | solution.py:769
  18.2 5.6 %collective-permute-start.6 = (f32[3,4,8,128]{3,2,1,0:T(8,128)S(1)}, f32[3,4,8,128]{3,2,1,0:T(8,128)S(1)}, u32[]{:S(2)}, u32[]{:S(2)}) collective-permute-start(f32[3,4,8,128]{3,2,1,0:T(8,128)S(1)} %get-tuple-element.30), channel_id=1, source_target_pairs={{0,2},{1,3},{2,0},{3,1},{4,6},{5,7},{6,4},{7,5},{8,10},{9,11},{10,... | collective-permute-start | bytes 147464 | tf_op jit(solution)/shard_map/ppermute | solution.py:769
  19.7 5.2 %collective-permute-start.11 = (f32[3,4,8,128]{3,2,1,0:T(8,128)S(1)}, f32[3,4,8,128]{3,2,1,0:T(8,128)S(1)}, u32[]{:S(2)}, u32[]{:S(2)}) collective-permute-start(f32[3,4,8,128]{3,2,1,0:T(8,128)S(1)} %get-tuple-element.30), channel_id=1, source_target_pairs={{0,6},{1,7},{2,4},{3,5},{4,2},{5,3},{6,0},{7,1},{8,14},{9,15},{10,... | collective-permute-start | bytes 147464 | tf_op jit(solution)/shard_map/ppermute | solution.py:791
  22.2 5.0 %collective-permute-start.10 = (f32[2,3,4,8,128]{4,3,2,1,0:T(8,128)S(1)}, f32[2,3,4,8,128]{4,3,2,1,0:T(8,128)S(1)}, u32[]{:S(2)}, u32[]{:S(2)}) collective-permute-start(f32[2,3,4,8,128]{4,3,2,1,0:T(8,128)S(1)} %pad_maximum_fusion.2), channel_id=1, source_target_pairs={{0,2},{1,3},{2,0},{3,1},{4,6},{5,7},{6,4},{7,5},{8,10},{9,11},{10,... | collective-permute-start | bytes 294920 | tf_op jit(solution)/shard_map/ppermute | solution.py:769
  23.8 4.8 %collective-permute-start.12 = (f32[5,3,4,8,128]{4,3,2,1,0:T(8,128)S(1)}, f32[5,3,4,8,128]{4,3,2,1,0:T(8,128)S(1)}, u32[]{:S(2)}, u32[]{:S(2)}) collective-permute-start(f32[5,3,4,8,128]{4,3,2,1,0:T(8,128)S(1)} %constant_dynamic-update-slice_fusion.first), channel_id=1, source_target_pairs={{0,1},{1,0},{2,3},{3,2},{4,5},{5,4},{6,7},{7,6},{8,9},{9,8},{10,11... | collective-permute-start | bytes 737288 | tf_op jit(solution)/shard_map/ppermute | solution.py:769
  27.2 1.4 %collective-permute-start.13 = (f32[3,3,4,8,128]{4,3,2,1,0:T(8,128)S(1)}, f32[3,3,4,8,128]{4,3,2,1,0:T(8,128)S(1)}, u32[]{:S(2)}, u32[]{:S(2)}) collective-permute-start(f32[3,3,4,8,128]{4,3,2,1,0:T(8,128)S(1)} %pad_maximum_fusion.1.second), channel_id=1, source_target_pairs={{0,1},{1,0},{2,3},{3,2},{4,5},{5,4},{6,7},{7,6},{8,9},{9,8},{10,11... | collective-permute-start | bytes 442376 | tf_op jit(solution)/shard_map/ppermute | solution.py:769

commit v8 on v7

--- a/solution.py
+++ b/solution.py
@@ -323,16 +323,18 @@
             r = key if listed is None else listed[key]
             c_here, u_here = c[key], u[key]
             here = weight(coupling, r)
+            conc_right, chem_right_here = right_at(r)
             flux = across[key] * u[key + 1] + across[key - 1] * u[key - 1]
-            flux = flux + weight(up_y, r) * at(chem, r, 1) + weight(down_y, r) * at(chem, r, -1)
-            flux = flux + weight(up_z, r) * lane_roll(u_here, -self.dup)
-            flux = flux + weight(down_z, r) * lane_roll(u_here, self.dup)
+            flux = flux + (weight(up_y, r) * at(chem, r, 1) + weight(down_y, r) * at(chem, r, -1))
+            flux = flux + (conc_right - c_here - here * u_here)
+            flux_z = weight(up_z, r) * lane_roll(u_here, -self.dup)
+            flux_z = flux_z + weight(down_z, r) * lane_roll(u_here, self.dup)
+            conc_left = flux + flux_z
             near = (c[key - 1] + c[key + 1]) + (at(conc, r, 1) + at(conc, r, -1))
-            near = near + (lane_roll(c_here, self.dup) + lane_roll(c_here, -self.dup))
-            conc_right, chem_right_here = right_at(r)
-            conc_left = conc_right - c_here + (flux - here * u_here)
-            chem_left = chem_right_here - u_here + self.diagonal * c_here
-            chem_left = chem_left - (GRADIENT_ENERGY * self.scale) * near
+            pull = GRADIENT_ENERGY * self.scale
+            chem_left = (chem_right_here - u_here + self.diagonal * c_here) - pull * near
+            near_z = lane_roll(c_here, self.dup) + lane_roll(c_here, -self.dup)
+            chem_left = chem_left - pull * near_z
             yield r, c_here, u_here, conc_left, chem_left, here, weight(gain, r)
 
     def steps(self, conc_left, chem_left, coupling, gain):
@@ -676,10 +678,15 @@
             half = pair_rows(sums.at[2], index, columns)
             put_padded((out_mobility,))(index, 0.125 * pair_lanes(half, dup))
 
-    stage(one.set_weights, mob1, rows1)
+    half1 = rows1 // 2
+    for start in (0, half1):
+        stage(one.set_weights, mob1, half1, start)
     stage(one.first_sweep, right1, rows1, put_padded(a1))
-    stage(one.sweep, a1, right1, 0, rows1, rows1, window1, put_padded(b1))
-    stage(one.coarse_right, b1, right1, 0, rows1, rows1, window1, put_sums(sums1))
+    for start in (0, half1):
+        stage(one.sweep, a1, right1, start, half1, half1, window1, put_padded(b1))
+    for start in (0, half1):
+        put = put_sums(sums1, start // 2)
+        stage(one.coarse_right, b1, right1, start, half1, half1, window1, put)
     stage(coarsen, mob1, sums1, right2, mob2, 2)
 
     stage(two.set_weights, mob2, rows2)
@@ -713,8 +720,10 @@
     stage(two.sweep, b2, right2, 0, rows2, rows2, window2, put_padded(a2))
     for row in range(rows2):
         correct(a2, row, b1, a1, spread2, row)
-    stage(one.sweep, a1, right1, -2, own_rows + 4, own_rows + 4, window1, put_padded(b1))
-    stage(one.sweep, b1, right1, -1, own_rows + 2, own_rows + 2, window1, put_padded(a1))
+    for start, count in ((-2, 6), (4, own_rows - 2)):
+        stage(one.sweep, a1, right1, start, count, count, window1, put_padded(b1))
+    for start, count in ((-1, 5), (4, own_rows - 3)):
+        stage(one.sweep, b1, right1, start, count, count, window1, put_padded(a1))
 
     rows, columns = conc_new.shape[:2]
     wide = (PAD - HALO, columns + 2 * HALO)
@@ -797,10 +806,9 @@
     beside = [swapped(values, "gy", mask) for mask in along_y]
     later, _ = lax.optimization_barrier((values, across[2]))
     corner = [swapped_both(later, along_x[0], mask) for mask in along_y]
-    last = jnp.stack(across[1:])
     first = jnp.stack([values] + beside + across)
-    second = [swapped(last, "gy", mask) for mask in along_y]
-    second = jnp.concatenate(second + [jnp.stack(corner)], axis=0)
+    second = [swapped(block, "gy", mask) for mask in along_y for block in across[1:]]
+    second = jnp.stack(second + corner)
     return first, second, swapped(first, "gy", 1), swapped(second, "gy", 1)
 
 

time: 33.5 us -> 33.1 us (0.988)
  waiting for transfers between devices: 8.16 us -> 6.37 us
  starting transfers between devices: 17.2 us -> 18.8 us
    ppermute x7 -> x8, waiting for transfers between devices: 5.25 us -> 3.26 us  [swapped(): return lax.ppermute(values, axis, [(i, i ^ mask) for i in range(count)])]
    ppermute x7 -> x8, starting transfers between devices: 7.66 us -> 9.2 us  [swapped(): return lax.ppermute(values, axis, [(i, i ^ mask) for i in range(count)])]
  transfers between devices with their start and end apart: 14 -> 15, of which waited for: 7 -> 7; matrix products, arithmetic and copies ran while one was open for 0% -> 0% of each run, Pallas kernels for 3% -> 3%
where the time goes in v8:
time: 33.1 us; the launch traced here: 33 us
  starting transfers between devices  18.8 us (57%)
  waiting for transfers between devices  6.37 us (19%)
  Pallas kernels  6.09 us (18%)
  other arithmetic  1 us (3%)
  between operations  0.72 us (2%)
    ppermute x8, starting transfers between devices, swapped(): return lax.ppermute(values, axis, [(i, i ^ mask) for i in range(count)])  9.2 us
    ppermute x6, starting transfers between devices, shifted(): lax.ppermute(values, axis, [(i, (i + by) % count) for i in range(count)])  8.7 us
    pallas_call x5, Pallas kernels, call_kernel(): pl.pallas_call(kernel, out_shape=shapes, in_specs=[whole_block()] * len(a...  6.09 us
    ppermute x8, waiting for transfers between devices, swapped(): return lax.ppermute(values, axis, [(i, i ^ mask) for i in range(count)])  3.26 us
    ppermute x6, waiting for transfers between devices, shifted(): lax.ppermute(values, axis, [(i, (i + by) % count) for i in range(count)])  1.89 us
    ppermute x1, waiting for transfers between devices, swapped_both(): return lax.ppermute(values, ('gx', 'gy'), pairs)  1.22 us
    concatenate x1, other arithmetic, two_phase_solve(): fields = jnp.concatenate([conc, chem], axis=0).reshape((2,) + block)  0.99 us
    ppermute x1, starting transfers between devices, swapped_both(): return lax.ppermute(values, ('gx', 'gy'), pairs)  0.85 us
  transfers between devices with their start and end apart: 15, of which 7 were waited for; matrix products, arithmetic and copies ran while one was open for 0% of the time, Pallas kernels for 3%

profile of v8, /device:TPU:0, one launch (start us, length us, event | category | flops | bytes accessed | tf_op | source)
XLA Modules:
  0.0 33.0 jit_solution(1061380670061083914)
XLA Ops:
  0.6 1.0 %pad_maximum_fusion = f32[32,16,128]{2,1,0:T(8,128)S(1)} fusion(f32[16,16,128]{2,1,0:T(8,128)} %param.3, f32[16,16,128]{2,1,0:T(8,128)} %param.2), kind=kLoop, calls=%fused_computation | loop fusion | flops 65536 | bytes 524288 | tf_op jit(solution)/shard_map/concatenate | solution.py:820
  1.6 3.1 %collective-permute-start = (f32[2,4,16,128]{3,2,1,0:T(8,128)S(1)}, f32[2,4,16,128]{3,2,1,0:T(8,128)S(1)}, u32[]{:S(2)}, u32[]{:S(2)}) collective-permute-start(f32[2,4,16,128]{3,2,1,0:T(8,128)S(1)} %get-tuple-element.18), channel_id=1, source_target_pairs={{0,4},{4,8},{8,12},{12,0},{1,5},{5,9},{9,13},{13,1},{2,6},{6,10},{... | collective-permute-start | bytes 196616 | tf_op jit(solution)/shard_map/ppermute | solution.py:773
  4.7 2.1 %collective-permute-start.1 = (f32[2,4,16,128]{3,2,1,0:T(8,128)S(1)}, f32[2,4,16,128]{3,2,1,0:T(8,128)S(1)}, u32[]{:S(2)}, u32[]{:S(2)}) collective-permute-start(f32[2,4,16,128]{3,2,1,0:T(8,128)S(1)} %get-tuple-element.19), channel_id=1, source_target_pairs={{0,12},{4,0},{8,4},{12,8},{1,13},{5,1},{9,5},{13,9},{2,14},{6,2},{... | collective-permute-start | bytes 196616 | tf_op jit(solution)/shard_map/ppermute | solution.py:773
  6.8 0.0 collective-permute-start.2
  6.8 1.7 %collective-permute-start.3 = (f32[16,8,128]{2,1,0:T(8,128)S(1)}, f32[16,8,128]{2,1,0:T(8,128)S(1)}, u32[]{:S(2)}, u32[]{:S(2)}) collective-permute-start(f32[16,8,128]{2,1,0:T(8,128)S(1)} %get-tuple-element.21), channel_id=1, source_target_pairs={{0,3},{1,0},{2,1},{3,2},{4,7},{5,4},{6,5},{7,6},{8,11},{9,8},{10,9... | collective-permute-start | bytes 196616 | tf_op jit(solution)/shard_map/ppermute | solution.py:773
  8.6 0.6 %collective-permute-done.before = f32[2,4,16,128]{3,2,1,0:T(8,128)S(1)} collective-permute-done((f32[2,4,16,128]{3,2,1,0:T(8,128)S(1)}, f32[2,4,16,128]{3,2,1,0:T(8,128)S(1)}, u32[]{:S(2)}, u32[]{:S(2)}) %collective-permute-start) | collective-permute-done | bytes 65568 | tf_op jit(solution)/shard_map/ppermute | solution.py:773
  9.1 0.5 %collective-permute-done.1.after = f32[2,4,16,128]{3,2,1,0:T(8,128)S(1)} collective-permute-done((f32[2,4,16,128]{3,2,1,0:T(8,128)S(1)}, f32[2,4,16,128]{3,2,1,0:T(8,128)S(1)}, u32[]{:S(2)}, u32[]{:S(2)}) %collective-permute-start.1) | collective-permute-done | bytes 65568 | tf_op jit(solution)/shard_map/ppermute | solution.py:773
  9.7 0.1 collective-permute-start.4
  9.8 1.7 %collective-permute-start.5 = (f32[8,8,128]{2,1,0:T(8,128)S(1)}, f32[8,8,128]{2,1,0:T(8,128)S(1)}, u32[]{:S(2)}, u32[]{:S(2)}) collective-permute-start(f32[8,8,128]{2,1,0:T(8,128)S(1)} %get-tuple-element.23), channel_id=1, source_target_pairs={{0,3},{1,0},{2,1},{3,2},{4,7},{5,4},{6,5},{7,6},{8,11},{9,8},{10,9... | collective-permute-start | bytes 98312 | tf_op jit(solution)/shard_map/ppermute | solution.py:773
  11.5 0.0 collective-permute-done.2.own_left
  11.5 0.0 collective-permute-done.3.own_right
  11.5 0.8 %shard_map.43 = (f32[3,4,8,128]{3,2,1,0:T(8,128)S(1)}, f32[2,12,24,128]{3,2,1,0:T(8,128)S(1)}, f32[16,32,128]{2,1,0:T(8,128)S(1)}, f32[7,14,24,128]{3,2,1,0:T(8,128)S(1)}, f32[2,4,32,128]{3,2,1,0:T(8,128)S(1)}) custom-call(f32[2,16,16,128]{3,2,1,0:T(8,128)S(1)} %bitcast.15, f32[16,8,128]{2,1,0:T(8,128)S(1)} %collective-permute-done.2.own_left, ...), custom_call_target="tpu_custom_call" | custom-call | tf_op jit(solution)/shard_map/pallas_call | solution.py:761
  12.3 0.7 %collective-permute-done.4.corner_left = f32[8,8,128]{2,1,0:T(8,128)S(1)} collective-permute-done((f32[8,8,128]{2,1,0:T(8,128)S(1)}, f32[8,8,128]{2,1,0:T(8,128)S(1)}, u32[]{:S(2)}, u32[]{:S(2)}) %collective-permute-start.4) | collective-permute-done | bytes 32800 | tf_op jit(solution)/shard_map/ppermute | solution.py:773
  13.1 0.0 collective-permute-done.5.corner_right
  13.1 0.6 %shard_map.44 = (f32[3,4,8,128]{3,2,1,0:T(8,128)S(1)}, f32[2,8,24,128]{3,2,1,0:T(8,128)S(1)}, f32[2,32,128]{2,1,0:T(8,128)S(1)}, f32[7,5,24,128]{3,2,1,0:T(8,128)S(1)}) custom-call(f32[2,16,16,128]{3,2,1,0:T(8,128)S(1)} %bitcast.16, f32[2,4,16,128]{3,2,1,0:T(8,128)S(1)} %collective-permute-done.before, f32[2,4,16,128]{3,2,1,0:T(8,128)S(1)} %collective-permute-done.1.after, ...), custom_call_target="tpu_custom_call" | custom-call | tf_op jit(solution)/shard_map/pallas_call | solution.py:761
  13.7 3.2 %collective-permute-start.9 = (f32[3,4,8,128]{3,2,1,0:T(8,128)S(1)}, f32[3,4,8,128]{3,2,1,0:T(8,128)S(1)}, u32[]{:S(2)}, u32[]{:S(2)}) collective-permute-start(f32[3,4,8,128]{3,2,1,0:T(8,128)S(1)} %get-tuple-element.30), channel_id=1, source_target_pairs={{0,12},{4,8},{8,4},{12,0},{1,13},{5,9},{9,5},{13,1},{2,14},{6,10},... | collective-permute-start | bytes 147464 | tf_op jit(solution)/shard_map/ppermute | solution.py:778
  17.0 0.0 collective-permute-start.8
  17.0 1.2 %collective-permute-start.7 = (f32[3,4,8,128]{3,2,1,0:T(8,128)S(1)}, f32[3,4,8,128]{3,2,1,0:T(8,128)S(1)}, u32[]{:S(2)}, u32[]{:S(2)}) collective-permute-start(f32[3,4,8,128]{3,2,1,0:T(8,128)S(1)} %get-tuple-element.30), channel_id=1, source_target_pairs={{0,4},{4,0},{8,12},{12,8},{1,5},{5,1},{9,13},{13,9},{2,6},{6,2},{1... | collective-permute-start | bytes 147464 | tf_op jit(solution)/shard_map/ppermute | solution.py:778
  18.2 1.5 %collective-permute-start.6 = (f32[3,4,8,128]{3,2,1,0:T(8,128)S(1)}, f32[3,4,8,128]{3,2,1,0:T(8,128)S(1)}, u32[]{:S(2)}, u32[]{:S(2)}) collective-permute-start(f32[3,4,8,128]{3,2,1,0:T(8,128)S(1)} %get-tuple-element.30), channel_id=1, source_target_pairs={{0,2},{1,3},{2,0},{3,1},{4,6},{5,7},{6,4},{7,5},{8,10},{9,11},{10,... | collective-permute-start | bytes 147464 | tf_op jit(solution)/shard_map/ppermute | solution.py:778
  19.7 0.0 collective-permute-done.9
  19.7 0.8 %collective-permute-start.12 = (f32[3,4,8,128]{3,2,1,0:T(8,128)S(1)}, f32[3,4,8,128]{3,2,1,0:T(8,128)S(1)}, u32[]{:S(2)}, u32[]{:S(2)}) collective-permute-start(f32[3,4,8,128]{3,2,1,0:T(8,128)S(1)} %get-tuple-element.30), channel_id=1, source_target_pairs={{0,6},{1,7},{2,4},{3,5},{4,2},{5,3},{6,0},{7,1},{8,14},{9,15},{10,... | collective-permute-start | bytes 147464 | tf_op jit(solution)/shard_map/ppermute | solution.py:800
  20.5 1.6 %collective-permute-start.11 = (f32[3,4,8,128]{3,2,1,0:T(8,128)S(1)}, f32[3,4,8,128]{3,2,1,0:T(8,128)S(1)}, u32[]{:S(2)}, u32[]{:S(2)}) collective-permute-start(f32[3,4,8,128]{3,2,1,0:T(8,128)S(1)} %collective-permute-done.9), channel_id=1, source_target_pairs={{0,2},{1,3},{2,0},{3,1},{4,6},{5,7},{6,4},{7,5},{8,10},{9,11},{10,... | collective-permute-start | bytes 147464 | tf_op jit(solution)/shard_map/ppermute | solution.py:778
  22.2 0.0 collective-permute-done.8
  22.2 1.5 %collective-permute-start.10 = (f32[3,4,8,128]{3,2,1,0:T(8,128)S(1)}, f32[3,4,8,128]{3,2,1,0:T(8,128)S(1)}, u32[]{:S(2)}, u32[]{:S(2)}) collective-permute-start(f32[3,4,8,128]{3,2,1,0:T(8,128)S(1)} %collective-permute-done.8), channel_id=1, source_target_pairs={{0,2},{1,3},{2,0},{3,1},{4,6},{5,7},{6,4},{7,5},{8,10},{9,11},{10,... | collective-permute-start | bytes 147464 | tf_op jit(solution)/shard_map/ppermute | solution.py:778
  23.7 0.0 collective-permute-done.6
  23.7 0.0 collective-permute-done.7
  23.7 0.1 collective-permute-start.13
  23.8 1.2 %collective-permute-done.12 = f32[3,4,8,128]{3,2,1,0:T(8,128)S(1)} collective-permute-done((f32[3,4,8,128]{3,2,1,0:T(8,128)S(1)}, f32[3,4,8,128]{3,2,1,0:T(8,128)S(1)}, u32[]{:S(2)}, u32[]{:S(2)}) %collective-permute-start.12) | collective-permute-done | bytes 49184 | tf_op jit(solution)/shard_map/ppermute | solution.py:800
  25.0 1.0 %collective-permute-done.11 = f32[3,4,8,128]{3,2,1,0:T(8,128)S(1)} collective-permute-done((f32[3,4,8,128]{3,2,1,0:T(8,128)S(1)}, f32[3,4,8,128]{3,2,1,0:T(8,128)S(1)}, u32[]{:S(2)}, u32[]{:S(2)}) %collective-permute-start.11) | collective-permute-done | bytes 49184 | tf_op jit(solution)/shard_map/ppermute | solution.py:778
  26.1 0.8 %collective-permute-done.10 = f32[3,4,8,128]{3,2,1,0:T(8,128)S(1)} collective-permute-done((f32[3,4,8,128]{3,2,1,0:T(8,128)S(1)}, f32[3,4,8,128]{3,2,1,0:T(8,128)S(1)}, u32[]{:S(2)}, u32[]{:S(2)}) %collective-permute-start.10) | collective-permute-done | bytes 49184 | tf_op jit(solution)/shard_map/ppermute | solution.py:778
  26.9 0.1 collective-permute-start.14
  27.0 1.4 %collective-permute-done.14.second_far = f32[3,3,4,8,128]{4,3,2,1,0:T(8,128)S(1)} collective-permute-done((f32[3,3,4,8,128]{4,3,2,1,0:T(8,128)S(1)}, f32[3,3,4,8,128]{4,3,2,1,0:T(8,128)S(1)}, u32[]{:S(2)}, u32[]{:S(2)}) %collective-permute-start.14) | collective-permute-done | bytes 147488 | tf_op jit(solution)/shard_map/ppermute | solution.py:778
  28.4 0.0 collective-permute-done.13.first_far
  28.4 4.6 %shard_map.45 = (f32[16,16,128]{2,1,0:T(8,128)}, f32[16,16,128]{2,1,0:T(8,128)}) custom-call(f32[5,3,4,8,128]{4,3,2,1,0:T(8,128)S(1)} %bitcast_dynamic-update-slice_fusion.first, f32[3,3,4,8,128]{4,3,2,1,0:T(8,128)S(1)} %pad_maximum_fusion.1.second, f32[5,3,4,8,128]{4,3,2,1,0:T(8,128)S(1)} %collective-permute-done.13.first_far, ...), custom_call_target="tpu_custom_call" | custom-call | tf_op jit(solution)/shard_map/pallas_call | solution.py:761
  (8 shorter events, 0.1 us)
Async XLA Ops:
  1.6 7.5 %collective-permute-start = (f32[2,4,16,128]{3,2,1,0:T(8,128)S(1)}, f32[2,4,16,128]{3,2,1,0:T(8,128)S(1)}, u32[]{:S(2)}, u32[]{:S(2)}) collective-permute-start(f32[2,4,16,128]{3,2,1,0:T(8,128)S(1)} %get-tuple-element.18), channel_id=1, source_target_pairs={{0,4},{4,8},{8,12},{12,0},{1,5},{5,9},{9,13},{13,1},{2,6},{6,10},{... | collective-permute-start | bytes 196616 | tf_op jit(solution)/shard_map/ppermute | solution.py:773
  4.7 5.0 %collective-permute-start.1 = (f32[2,4,16,128]{3,2,1,0:T(8,128)S(1)}, f32[2,4,16,128]{3,2,1,0:T(8,128)S(1)}, u32[]{:S(2)}, u32[]{:S(2)}) collective-permute-start(f32[2,4,16,128]{3,2,1,0:T(8,128)S(1)} %get-tuple-element.19), channel_id=1, source_target_pairs={{0,12},{4,0},{8,4},{12,8},{1,13},{5,1},{9,5},{13,9},{2,14},{6,2},{... | collective-permute-start | bytes 196616 | tf_op jit(solution)/shard_map/ppermute | solution.py:773
  6.8 4.7 %collective-permute-start.2 = (f32[16,8,128]{2,1,0:T(8,128)S(1)}, f32[16,8,128]{2,1,0:T(8,128)S(1)}, u32[]{:S(2)}, u32[]{:S(2)}) collective-permute-start(f32[16,8,128]{2,1,0:T(8,128)S(1)} %get-tuple-element.20), channel_id=1, source_target_pairs={{0,1},{1,2},{2,3},{3,0},{4,5},{5,6},{6,7},{7,4},{8,9},{9,10},{10,1... | collective-permute-start | bytes 196616 | tf_op jit(solution)/shard_map/ppermute | solution.py:773
  6.8 4.7 %collective-permute-start.3 = (f32[16,8,128]{2,1,0:T(8,128)S(1)}, f32[16,8,128]{2,1,0:T(8,128)S(1)}, u32[]{:S(2)}, u32[]{:S(2)}) collective-permute-start(f32[16,8,128]{2,1,0:T(8,128)S(1)} %get-tuple-element.21), channel_id=1, source_target_pairs={{0,3},{1,0},{2,1},{3,2},{4,7},{5,4},{6,5},{7,6},{8,11},{9,8},{10,9... | collective-permute-start | bytes 196616 | tf_op jit(solution)/shard_map/ppermute | solution.py:773
  9.7 3.4 %collective-permute-start.4 = (f32[8,8,128]{2,1,0:T(8,128)S(1)}, f32[8,8,128]{2,1,0:T(8,128)S(1)}, u32[]{:S(2)}, u32[]{:S(2)}) collective-permute-start(f32[8,8,128]{2,1,0:T(8,128)S(1)} %get-tuple-element.22), channel_id=1, source_target_pairs={{0,1},{1,2},{2,3},{3,0},{4,5},{5,6},{6,7},{7,4},{8,9},{9,10},{10,1... | collective-permute-start | bytes 98312 | tf_op jit(solution)/shard_map/ppermute | solution.py:773
  9.8 3.3 %collective-permute-start.5 = (f32[8,8,128]{2,1,0:T(8,128)S(1)}, f32[8,8,128]{2,1,0:T(8,128)S(1)}, u32[]{:S(2)}, u32[]{:S(2)}) collective-permute-start(f32[8,8,128]{2,1,0:T(8,128)S(1)} %get-tuple-element.23), channel_id=1, source_target_pairs={{0,3},{1,0},{2,1},{3,2},{4,7},{5,4},{6,5},{7,6},{8,11},{9,8},{10,9... | collective-permute-start | bytes 98312 | tf_op jit(solution)/shard_map/ppermute | solution.py:773
  13.7 5.9 %collective-permute-start.9 = (f32[3,4,8,128]{3,2,1,0:T(8,128)S(1)}, f32[3,4,8,128]{3,2,1,0:T(8,128)S(1)}, u32[]{:S(2)}, u32[]{:S(2)}) collective-permute-start(f32[3,4,8,128]{3,2,1,0:T(8,128)S(1)} %get-tuple-element.30), channel_id=1, source_target_pairs={{0,12},{4,8},{8,4},{12,0},{1,13},{5,9},{9,5},{13,1},{2,14},{6,10},... | collective-permute-start | bytes 147464 | tf_op jit(solution)/shard_map/ppermute | solution.py:778
  17.0 5.2 %collective-permute-start.8 = (f32[3,4,8,128]{3,2,1,0:T(8,128)S(1)}, f32[3,4,8,128]{3,2,1,0:T(8,128)S(1)}, u32[]{:S(2)}, u32[]{:S(2)}) collective-permute-start(f32[3,4,8,128]{3,2,1,0:T(8,128)S(1)} %get-tuple-element.30), channel_id=1, source_target_pairs={{0,8},{4,12},{8,0},{12,4},{1,9},{5,13},{9,1},{13,5},{2,10},{6,14},... | collective-permute-start | bytes 147464 | tf_op jit(solution)/shard_map/ppermute | solution.py:778
  17.0 6.7 %collective-permute-start.7 = (f32[3,4,8,128]{3,2,1,0:T(8,128)S(1)}, f32[3,4,8,128]{3,2,1,0:T(8,128)S(1)}, u32[]{:S(2)}, u32[]{:S(2)}) collective-permute-start(f32[3,4,8,128]{3,2,1,0:T(8,128)S(1)} %get-tuple-element.30), channel_id=1, source_target_pairs={{0,4},{4,0},{8,12},{12,8},{1,5},{5,1},{9,13},{13,9},{2,6},{6,2},{1... | collective-permute-start | bytes 147464 | tf_op jit(solution)/shard_map/ppermute | solution.py:778
  18.2 5.5 %collective-permute-start.6 = (f32[3,4,8,128]{3,2,1,0:T(8,128)S(1)}, f32[3,4,8,128]{3,2,1,0:T(8,128)S(1)}, u32[]{:S(2)}, u32[]{:S(2)}) collective-permute-start(f32[3,4,8,128]{3,2,1,0:T(8,128)S(1)} %get-tuple-element.30), channel_id=1, source_target_pairs={{0,2},{1,3},{2,0},{3,1},{4,6},{5,7},{6,4},{7,5},{8,10},{9,11},{10,... | collective-permute-start | bytes 147464 | tf_op jit(solution)/shard_map/ppermute | solution.py:778
  19.7 5.3 %collective-permute-start.12 = (f32[3,4,8,128]{3,2,1,0:T(8,128)S(1)}, f32[3,4,8,128]{3,2,1,0:T(8,128)S(1)}, u32[]{:S(2)}, u32[]{:S(2)}) collective-permute-start(f32[3,4,8,128]{3,2,1,0:T(8,128)S(1)} %get-tuple-element.30), channel_id=1, source_target_pairs={{0,6},{1,7},{2,4},{3,5},{4,2},{5,3},{6,0},{7,1},{8,14},{9,15},{10,... | collective-permute-start | bytes 147464 | tf_op jit(solution)/shard_map/ppermute | solution.py:800
  20.5 5.5 %collective-permute-start.11 = (f32[3,4,8,128]{3,2,1,0:T(8,128)S(1)}, f32[3,4,8,128]{3,2,1,0:T(8,128)S(1)}, u32[]{:S(2)}, u32[]{:S(2)}) collective-permute-start(f32[3,4,8,128]{3,2,1,0:T(8,128)S(1)} %collective-permute-done.9), channel_id=1, source_target_pairs={{0,2},{1,3},{2,0},{3,1},{4,6},{5,7},{6,4},{7,5},{8,10},{9,11},{10,... | collective-permute-start | bytes 147464 | tf_op jit(solution)/shard_map/ppermute | solution.py:778
  22.2 4.7 %collective-permute-start.10 = (f32[3,4,8,128]{3,2,1,0:T(8,128)S(1)}, f32[3,4,8,128]{3,2,1,0:T(8,128)S(1)}, u32[]{:S(2)}, u32[]{:S(2)}) collective-permute-start(f32[3,4,8,128]{3,2,1,0:T(8,128)S(1)} %collective-permute-done.8), channel_id=1, source_target_pairs={{0,2},{1,3},{2,0},{3,1},{4,6},{5,7},{6,4},{7,5},{8,10},{9,11},{10,... | collective-permute-start | bytes 147464 | tf_op jit(solution)/shard_map/ppermute | solution.py:778
  23.7 4.6 %collective-permute-start.13 = (f32[5,3,4,8,128]{4,3,2,1,0:T(8,128)S(1)}, f32[5,3,4,8,128]{4,3,2,1,0:T(8,128)S(1)}, u32[]{:S(2)}, u32[]{:S(2)}) collective-permute-start(f32[5,3,4,8,128]{4,3,2,1,0:T(8,128)S(1)} %bitcast_dynamic-update-slice_fusion.first), channel_id=1, source_target_pairs={{0,1},{1,0},{2,3},{3,2},{4,5},{5,4},{6,7},{7,6},{8,9},{9,8},{10,11... | collective-permute-start | bytes 737288 | tf_op jit(solution)/shard_map/ppermute | solution.py:778
  26.9 1.4 %collective-permute-start.14 = (f32[3,3,4,8,128]{4,3,2,1,0:T(8,128)S(1)}, f32[3,3,4,8,128]{4,3,2,1,0:T(8,128)S(1)}, u32[]{:S(2)}, u32[]{:S(2)}) collective-permute-start(f32[3,3,4,8,128]{4,3,2,1,0:T(8,128)S(1)} %pad_maximum_fusion.1.second), channel_id=1, source_target_pairs={{0,1},{1,0},{2,3},{3,2},{4,5},{5,4},{6,7},{7,6},{8,9},{9,8},{10,11... | collective-permute-start | bytes 442376 | tf_op jit(solution)/shard_map/ppermute | solution.py:778

commit v9 on v8

--- a/solution.py
+++ b/solution.py
@@ -612,7 +612,7 @@
 
 
 def coarse_kernel(
-    slots, grid, first, second, first_far, second_far,
+    slots, grid, first, second, third, first_far, second_far, third_far,
     kept_early, right_early, weights_early, kept_late, right_late, weights_late,
     conc_new, chem_new, *scratch,
 ):
@@ -639,7 +639,7 @@
     own_rows, own_columns = 2 * rows1 // grid[0], columns1 // grid[1]
     even = lane_even((own_columns, lanes), 1)
     blocks = {}
-    for last, sources in enumerate(((first, second), (first_far, second_far))):
+    for last, sources in enumerate(((first, second, third), (first_far, second_far, third_far))):
         for source, masks in zip(sources, slots):
             for slot, (mask_x, mask_y) in enumerate(masks):
                 blocks[mask_x, mask_y ^ last] = source.at[slot]
@@ -786,8 +786,9 @@
 def slot_masks():
     along_x, along_y = far_masks()
     first = [(0, 0)] + [(0, y) for y in along_y] + [(x, 0) for x in along_x]
-    second = [(x, y) for y in along_y for x in along_x[1:]]
-    return first, second + [(along_x[0], y) for y in along_y]
+    second = [(x, y) for y in along_y for x in along_x[2:]]
+    second += [(along_x[0], y) for y in along_y]
+    return first, second, [(along_x[1], y) for y in along_y]
 
 
 def swapped_both(values, mask_x, mask_y):
@@ -807,9 +808,11 @@
     later, _ = lax.optimization_barrier((values, across[2]))
     corner = [swapped_both(later, along_x[0], mask) for mask in along_y]
     first = jnp.stack([values] + beside + across)
-    second = [swapped(block, "gy", mask) for mask in along_y for block in across[1:]]
+    second = [swapped(block, "gy", mask) for mask in along_y for block in across[2:]]
     second = jnp.stack(second + corner)
-    return first, second, swapped(first, "gy", 1), swapped(second, "gy", 1)
+    third = jnp.stack([swapped(across[1], "gy", mask) for mask in along_y])
+    far = tuple(swapped(group, "gy", 1) for group in (first, second, third))
+    return (first, second, third) + far
 
 
 def two_phase_solve(conc, chem):

time: 33.1 us -> 32.9 us (level)
    ppermute x8 -> x9, starting transfers between devices: 9.2 us -> 8.98 us  [swapped(): return lax.ppermute(values, axis, [(i, i ^ mask) for i in range(count)])]
    ppermute x8 -> x9, waiting for transfers between devices: 3.26 us -> 3.44 us  [swapped(): return lax.ppermute(values, axis, [(i, i ^ mask) for i in range(count)])]
  transfers between devices with their start and end apart: 15 -> 16, of which waited for: 7 -> 8; matrix products, arithmetic and copies ran while one was open for 0% -> 0% of each run, Pallas kernels for 3% -> 3%
where the time goes in v9:
time: 32.9 us; the launch traced here: 32.8 us
  starting transfers between devices  18.5 us (56%)
  waiting for transfers between devices  6.39 us (19%)
  Pallas kernels  6.11 us (19%)
  other arithmetic  0.99 us (3%)
  between operations  0.71 us (2%)
    ppermute x9, starting transfers between devices, swapped(): return lax.ppermute(values, axis, [(i, i ^ mask) for i in range(count)])  8.98 us
    ppermute x6, starting transfers between devices, shifted(): lax.ppermute(values, axis, [(i, (i + by) % count) for i in range(count)])  8.7 us
    pallas_call x5, Pallas kernels, call_kernel(): pl.pallas_call(kernel, out_shape=shapes, in_specs=[whole_block()] * len(a...  6.11 us
    ppermute x9, waiting for transfers between devices, swapped(): return lax.ppermute(values, axis, [(i, i ^ mask) for i in range(count)])  3.44 us
    ppermute x6, waiting for transfers between devices, shifted(): lax.ppermute(values, axis, [(i, (i + by) % count) for i in range(count)])  1.89 us
    ppermute x1, waiting for transfers between devices, swapped_both(): return lax.ppermute(values, ('gx', 'gy'), pairs)  1.06 us
    concatenate x1, other arithmetic, two_phase_solve(): fields = jnp.concatenate([conc, chem], axis=0).reshape((2,) + block)  0.99 us
    ppermute x1, starting transfers between devices, swapped_both(): return lax.ppermute(values, ('gx', 'gy'), pairs)  0.85 us
  transfers between devices with their start and end apart: 16, of which 8 were waited for; matrix products, arithmetic and copies ran while one was open for 0% of the time, Pallas kernels for 3%

profile of v9, /device:TPU:0, one launch (start us, length us, event | category | flops | bytes accessed | tf_op | source)
XLA Modules:
  0.0 32.8 jit_solution(6996965288790298659)
XLA Ops:
  0.6 1.0 %pad_maximum_fusion = f32[32,16,128]{2,1,0:T(8,128)S(1)} fusion(f32[16,16,128]{2,1,0:T(8,128)} %param.3, f32[16,16,128]{2,1,0:T(8,128)} %param.2), kind=kLoop, calls=%fused_computation | loop fusion | flops 65536 | bytes 524288 | tf_op jit(solution)/shard_map/concatenate | solution.py:823
  1.6 3.1 %collective-permute-start = (f32[2,4,16,128]{3,2,1,0:T(8,128)S(1)}, f32[2,4,16,128]{3,2,1,0:T(8,128)S(1)}, u32[]{:S(2)}, u32[]{:S(2)}) collective-permute-start(f32[2,4,16,128]{3,2,1,0:T(8,128)S(1)} %get-tuple-element.18), channel_id=1, source_target_pairs={{0,4},{4,8},{8,12},{12,0},{1,5},{5,9},{9,13},{13,1},{2,6},{6,10},{... | collective-permute-start | bytes 196616 | tf_op jit(solution)/shard_map/ppermute | solution.py:773
  4.7 2.1 %collective-permute-start.1 = (f32[2,4,16,128]{3,2,1,0:T(8,128)S(1)}, f32[2,4,16,128]{3,2,1,0:T(8,128)S(1)}, u32[]{:S(2)}, u32[]{:S(2)}) collective-permute-start(f32[2,4,16,128]{3,2,1,0:T(8,128)S(1)} %get-tuple-element.19), channel_id=1, source_target_pairs={{0,12},{4,0},{8,4},{12,8},{1,13},{5,1},{9,5},{13,9},{2,14},{6,2},{... | collective-permute-start | bytes 196616 | tf_op jit(solution)/shard_map/ppermute | solution.py:773
  6.8 0.0 collective-permute-start.2
  6.8 1.7 %collective-permute-start.3 = (f32[16,8,128]{2,1,0:T(8,128)S(1)}, f32[16,8,128]{2,1,0:T(8,128)S(1)}, u32[]{:S(2)}, u32[]{:S(2)}) collective-permute-start(f32[16,8,128]{2,1,0:T(8,128)S(1)} %get-tuple-element.21), channel_id=1, source_target_pairs={{0,3},{1,0},{2,1},{3,2},{4,7},{5,4},{6,5},{7,6},{8,11},{9,8},{10,9... | collective-permute-start | bytes 196616 | tf_op jit(solution)/shard_map/ppermute | solution.py:773
  8.6 0.6 %collective-permute-done.before = f32[2,4,16,128]{3,2,1,0:T(8,128)S(1)} collective-permute-done((f32[2,4,16,128]{3,2,1,0:T(8,128)S(1)}, f32[2,4,16,128]{3,2,1,0:T(8,128)S(1)}, u32[]{:S(2)}, u32[]{:S(2)}) %collective-permute-start) | collective-permute-done | bytes 65568 | tf_op jit(solution)/shard_map/ppermute | solution.py:773
  9.1 0.5 %collective-permute-done.1.after = f32[2,4,16,128]{3,2,1,0:T(8,128)S(1)} collective-permute-done((f32[2,4,16,128]{3,2,1,0:T(8,128)S(1)}, f32[2,4,16,128]{3,2,1,0:T(8,128)S(1)}, u32[]{:S(2)}, u32[]{:S(2)}) %collective-permute-start.1) | collective-permute-done | bytes 65568 | tf_op jit(solution)/shard_map/ppermute | solution.py:773
  9.7 0.1 collective-permute-start.4
  9.8 1.7 %collective-permute-start.5 = (f32[8,8,128]{2,1,0:T(8,128)S(1)}, f32[8,8,128]{2,1,0:T(8,128)S(1)}, u32[]{:S(2)}, u32[]{:S(2)}) collective-permute-start(f32[8,8,128]{2,1,0:T(8,128)S(1)} %get-tuple-element.23), channel_id=1, source_target_pairs={{0,3},{1,0},{2,1},{3,2},{4,7},{5,4},{6,5},{7,6},{8,11},{9,8},{10,9... | collective-permute-start | bytes 98312 | tf_op jit(solution)/shard_map/ppermute | solution.py:773
  11.5 0.0 collective-permute-done.2.own_left
  11.5 0.0 collective-permute-done.3.own_right
  11.5 0.8 %shard_map.43 = (f32[3,4,8,128]{3,2,1,0:T(8,128)S(1)}, f32[2,12,24,128]{3,2,1,0:T(8,128)S(1)}, f32[16,32,128]{2,1,0:T(8,128)S(1)}, f32[7,14,24,128]{3,2,1,0:T(8,128)S(1)}, f32[2,4,32,128]{3,2,1,0:T(8,128)S(1)}) custom-call(f32[2,16,16,128]{3,2,1,0:T(8,128)S(1)} %bitcast.15, f32[16,8,128]{2,1,0:T(8,128)S(1)} %collective-permute-done.2.own_left, ...), custom_call_target="tpu_custom_call" | custom-call | tf_op jit(solution)/shard_map/pallas_call | solution.py:761
  12.3 0.7 %collective-permute-done.4.corner_left = f32[8,8,128]{2,1,0:T(8,128)S(1)} collective-permute-done((f32[8,8,128]{2,1,0:T(8,128)S(1)}, f32[8,8,128]{2,1,0:T(8,128)S(1)}, u32[]{:S(2)}, u32[]{:S(2)}) %collective-permute-start.4) | collective-permute-done | bytes 32800 | tf_op jit(solution)/shard_map/ppermute | solution.py:773
  13.1 0.0 collective-permute-done.5.corner_right
  13.1 0.7 %shard_map.44 = (f32[3,4,8,128]{3,2,1,0:T(8,128)S(1)}, f32[2,8,24,128]{3,2,1,0:T(8,128)S(1)}, f32[2,32,128]{2,1,0:T(8,128)S(1)}, f32[7,5,24,128]{3,2,1,0:T(8,128)S(1)}) custom-call(f32[2,16,16,128]{3,2,1,0:T(8,128)S(1)} %bitcast.16, f32[2,4,16,128]{3,2,1,0:T(8,128)S(1)} %collective-permute-done.before, f32[2,4,16,128]{3,2,1,0:T(8,128)S(1)} %collective-permute-done.1.after, ...), custom_call_target="tpu_custom_call" | custom-call | tf_op jit(solution)/shard_map/pallas_call | solution.py:761
  13.8 3.2 %collective-permute-start.9 = (f32[3,4,8,128]{3,2,1,0:T(8,128)S(1)}, f32[3,4,8,128]{3,2,1,0:T(8,128)S(1)}, u32[]{:S(2)}, u32[]{:S(2)}) collective-permute-start(f32[3,4,8,128]{3,2,1,0:T(8,128)S(1)} %get-tuple-element.30), channel_id=1, source_target_pairs={{0,12},{4,8},{8,4},{12,0},{1,13},{5,9},{9,5},{13,1},{2,14},{6,10},... | collective-permute-start | bytes 147464 | tf_op jit(solution)/shard_map/ppermute | solution.py:778
  17.0 0.0 collective-permute-start.8
  17.0 1.2 %collective-permute-start.7 = (f32[3,4,8,128]{3,2,1,0:T(8,128)S(1)}, f32[3,4,8,128]{3,2,1,0:T(8,128)S(1)}, u32[]{:S(2)}, u32[]{:S(2)}) collective-permute-start(f32[3,4,8,128]{3,2,1,0:T(8,128)S(1)} %get-tuple-element.30), channel_id=1, source_target_pairs={{0,4},{4,0},{8,12},{12,8},{1,5},{5,1},{9,13},{13,9},{2,6},{6,2},{1... | collective-permute-start | bytes 147464 | tf_op jit(solution)/shard_map/ppermute | solution.py:778
  18.2 1.5 %collective-permute-start.6 = (f32[3,4,8,128]{3,2,1,0:T(8,128)S(1)}, f32[3,4,8,128]{3,2,1,0:T(8,128)S(1)}, u32[]{:S(2)}, u32[]{:S(2)}) collective-permute-start(f32[3,4,8,128]{3,2,1,0:T(8,128)S(1)} %get-tuple-element.30), channel_id=1, source_target_pairs={{0,2},{1,3},{2,0},{3,1},{4,6},{5,7},{6,4},{7,5},{8,10},{9,11},{10,... | collective-permute-start | bytes 147464 | tf_op jit(solution)/shard_map/ppermute | solution.py:778
  19.7 0.0 collective-permute-done.9
  19.7 0.8 %collective-permute-start.11 = (f32[3,4,8,128]{3,2,1,0:T(8,128)S(1)}, f32[3,4,8,128]{3,2,1,0:T(8,128)S(1)}, u32[]{:S(2)}, u32[]{:S(2)}) collective-permute-start(f32[3,4,8,128]{3,2,1,0:T(8,128)S(1)} %get-tuple-element.30), channel_id=1, source_target_pairs={{0,6},{1,7},{2,4},{3,5},{4,2},{5,3},{6,0},{7,1},{8,14},{9,15},{10,... | collective-permute-start | bytes 147464 | tf_op jit(solution)/shard_map/ppermute | solution.py:801
  20.5 1.6 %collective-permute-start.10 = (f32[3,4,8,128]{3,2,1,0:T(8,128)S(1)}, f32[3,4,8,128]{3,2,1,0:T(8,128)S(1)}, u32[]{:S(2)}, u32[]{:S(2)}) collective-permute-start(f32[3,4,8,128]{3,2,1,0:T(8,128)S(1)} %collective-permute-done.9), channel_id=1, source_target_pairs={{0,2},{1,3},{2,0},{3,1},{4,6},{5,7},{6,4},{7,5},{8,10},{9,11},{10,... | collective-permute-start | bytes 147464 | tf_op jit(solution)/shard_map/ppermute | solution.py:778
  22.2 0.4 %collective-permute-done.6 = f32[3,4,8,128]{3,2,1,0:T(8,128)S(1)} collective-permute-done((f32[3,4,8,128]{3,2,1,0:T(8,128)S(1)}, f32[3,4,8,128]{3,2,1,0:T(8,128)S(1)}, u32[]{:S(2)}, u32[]{:S(2)}) %collective-permute-start.6) | collective-permute-done | bytes 49184 | tf_op jit(solution)/shard_map/ppermute | solution.py:778
  22.6 0.0 collective-permute-done.7
  22.6 0.0 collective-permute-done.8
  22.7 0.2 collective-permute-start.13
  22.8 1.2 %collective-permute-start.12 = (f32[3,4,8,128]{3,2,1,0:T(8,128)S(1)}, f32[3,4,8,128]{3,2,1,0:T(8,128)S(1)}, u32[]{:S(2)}, u32[]{:S(2)}) collective-permute-start(f32[3,4,8,128]{3,2,1,0:T(8,128)S(1)} %collective-permute-done.8), channel_id=1, source_target_pairs={{0,2},{1,3},{2,0},{3,1},{4,6},{5,7},{6,4},{7,5},{8,10},{9,11},{10,... | collective-permute-start | bytes 147464 | tf_op jit(solution)/shard_map/ppermute | solution.py:778
  24.0 1.1 %collective-permute-done.11 = f32[3,4,8,128]{3,2,1,0:T(8,128)S(1)} collective-permute-done((f32[3,4,8,128]{3,2,1,0:T(8,128)S(1)}, f32[3,4,8,128]{3,2,1,0:T(8,128)S(1)}, u32[]{:S(2)}, u32[]{:S(2)}) %collective-permute-start.11) | collective-permute-done | bytes 49184 | tf_op jit(solution)/shard_map/ppermute | solution.py:801
  25.0 0.8 %collective-permute-done.10 = f32[3,4,8,128]{3,2,1,0:T(8,128)S(1)} collective-permute-done((f32[3,4,8,128]{3,2,1,0:T(8,128)S(1)}, f32[3,4,8,128]{3,2,1,0:T(8,128)S(1)}, u32[]{:S(2)}, u32[]{:S(2)}) %collective-permute-start.10) | collective-permute-done | bytes 49184 | tf_op jit(solution)/shard_map/ppermute | solution.py:778
  25.9 0.1 collective-permute-start.14
  26.0 1.0 %collective-permute-done.12 = f32[3,4,8,128]{3,2,1,0:T(8,128)S(1)} collective-permute-done((f32[3,4,8,128]{3,2,1,0:T(8,128)S(1)}, f32[3,4,8,128]{3,2,1,0:T(8,128)S(1)}, u32[]{:S(2)}, u32[]{:S(2)}) %collective-permute-start.12) | collective-permute-done | bytes 49184 | tf_op jit(solution)/shard_map/ppermute | solution.py:778
  26.9 0.0 collective-permute-start.15
  26.9 1.2 %collective-permute-done.15.third_far = f32[1,3,4,8,128]{4,3,2,1,0:T(8,128)S(1)} collective-permute-done((f32[1,3,4,8,128]{4,3,2,1,0:T(8,128)S(1)}, f32[1,3,4,8,128]{4,3,2,1,0:T(8,128)S(1)}, u32[]{:S(2)}, u32[]{:S(2)}) %collective-permute-start.15) | collective-permute-done | bytes 49184 | tf_op jit(solution)/shard_map/ppermute | solution.py:778
  28.2 0.0 collective-permute-done.14.second_far
  28.2 0.0 collective-permute-done.13.first_far
  28.2 4.6 %shard_map.45 = (f32[16,16,128]{2,1,0:T(8,128)}, f32[16,16,128]{2,1,0:T(8,128)}) custom-call(f32[5,3,4,8,128]{4,3,2,1,0:T(8,128)S(1)} %bitcast_dynamic-update-slice_fusion.first, f32[2,3,4,8,128]{4,3,2,1,0:T(8,128)S(1)} %pad_maximum_fusion.1.second, f32[1,3,4,8,128]{4,3,2,1,0:T(8,128)S(1)} %bitcast.18, ...), custom_call_target="tpu_custom_call" | custom-call | tf_op jit(solution)/shard_map/pallas_call | solution.py:761
  (8 shorter events, 0.1 us)
Async XLA Ops:
  1.6 7.5 %collective-permute-start = (f32[2,4,16,128]{3,2,1,0:T(8,128)S(1)}, f32[2,4,16,128]{3,2,1,0:T(8,128)S(1)}, u32[]{:S(2)}, u32[]{:S(2)}) collective-permute-start(f32[2,4,16,128]{3,2,1,0:T(8,128)S(1)} %get-tuple-element.18), channel_id=1, source_target_pairs={{0,4},{4,8},{8,12},{12,0},{1,5},{5,9},{9,13},{13,1},{2,6},{6,10},{... | collective-permute-start | bytes 196616 | tf_op jit(solution)/shard_map/ppermute | solution.py:773
  4.7 5.0 %collective-permute-start.1 = (f32[2,4,16,128]{3,2,1,0:T(8,128)S(1)}, f32[2,4,16,128]{3,2,1,0:T(8,128)S(1)}, u32[]{:S(2)}, u32[]{:S(2)}) collective-permute-start(f32[2,4,16,128]{3,2,1,0:T(8,128)S(1)} %get-tuple-element.19), channel_id=1, source_target_pairs={{0,12},{4,0},{8,4},{12,8},{1,13},{5,1},{9,5},{13,9},{2,14},{6,2},{... | collective-permute-start | bytes 196616 | tf_op jit(solution)/shard_map/ppermute | solution.py:773
  6.8 4.7 %collective-permute-start.2 = (f32[16,8,128]{2,1,0:T(8,128)S(1)}, f32[16,8,128]{2,1,0:T(8,128)S(1)}, u32[]{:S(2)}, u32[]{:S(2)}) collective-permute-start(f32[16,8,128]{2,1,0:T(8,128)S(1)} %get-tuple-element.20), channel_id=1, source_target_pairs={{0,1},{1,2},{2,3},{3,0},{4,5},{5,6},{6,7},{7,4},{8,9},{9,10},{10,1... | collective-permute-start | bytes 196616 | tf_op jit(solution)/shard_map/ppermute | solution.py:773
  6.8 4.7 %collective-permute-start.3 = (f32[16,8,128]{2,1,0:T(8,128)S(1)}, f32[16,8,128]{2,1,0:T(8,128)S(1)}, u32[]{:S(2)}, u32[]{:S(2)}) collective-permute-start(f32[16,8,128]{2,1,0:T(8,128)S(1)} %get-tuple-element.21), channel_id=1, source_target_pairs={{0,3},{1,0},{2,1},{3,2},{4,7},{5,4},{6,5},{7,6},{8,11},{9,8},{10,9... | collective-permute-start | bytes 196616 | tf_op jit(solution)/shard_map/ppermute | solution.py:773
  9.7 3.4 %collective-permute-start.4 = (f32[8,8,128]{2,1,0:T(8,128)S(1)}, f32[8,8,128]{2,1,0:T(8,128)S(1)}, u32[]{:S(2)}, u32[]{:S(2)}) collective-permute-start(f32[8,8,128]{2,1,0:T(8,128)S(1)} %get-tuple-element.22), channel_id=1, source_target_pairs={{0,1},{1,2},{2,3},{3,0},{4,5},{5,6},{6,7},{7,4},{8,9},{9,10},{10,1... | collective-permute-start | bytes 98312 | tf_op jit(solution)/shard_map/ppermute | solution.py:773
  9.8 3.3 %collective-permute-start.5 = (f32[8,8,128]{2,1,0:T(8,128)S(1)}, f32[8,8,128]{2,1,0:T(8,128)S(1)}, u32[]{:S(2)}, u32[]{:S(2)}) collective-permute-start(f32[8,8,128]{2,1,0:T(8,128)S(1)} %get-tuple-element.23), channel_id=1, source_target_pairs={{0,3},{1,0},{2,1},{3,2},{4,7},{5,4},{6,5},{7,6},{8,11},{9,8},{10,9... | collective-permute-start | bytes 98312 | tf_op jit(solution)/shard_map/ppermute | solution.py:773
  13.8 5.9 %collective-permute-start.9 = (f32[3,4,8,128]{3,2,1,0:T(8,128)S(1)}, f32[3,4,8,128]{3,2,1,0:T(8,128)S(1)}, u32[]{:S(2)}, u32[]{:S(2)}) collective-permute-start(f32[3,4,8,128]{3,2,1,0:T(8,128)S(1)} %get-tuple-element.30), channel_id=1, source_target_pairs={{0,12},{4,8},{8,4},{12,0},{1,13},{5,9},{9,5},{13,1},{2,14},{6,10},... | collective-permute-start | bytes 147464 | tf_op jit(solution)/shard_map/ppermute | solution.py:778
  17.0 5.6 %collective-permute-start.8 = (f32[3,4,8,128]{3,2,1,0:T(8,128)S(1)}, f32[3,4,8,128]{3,2,1,0:T(8,128)S(1)}, u32[]{:S(2)}, u32[]{:S(2)}) collective-permute-start(f32[3,4,8,128]{3,2,1,0:T(8,128)S(1)} %get-tuple-element.30), channel_id=1, source_target_pairs={{0,8},{4,12},{8,0},{12,4},{1,9},{5,13},{9,1},{13,5},{2,10},{6,14},... | collective-permute-start | bytes 147464 | tf_op jit(solution)/shard_map/ppermute | solution.py:778
  17.0 5.6 %collective-permute-start.7 = (f32[3,4,8,128]{3,2,1,0:T(8,128)S(1)}, f32[3,4,8,128]{3,2,1,0:T(8,128)S(1)}, u32[]{:S(2)}, u32[]{:S(2)}) collective-permute-start(f32[3,4,8,128]{3,2,1,0:T(8,128)S(1)} %get-tuple-element.30), channel_id=1, source_target_pairs={{0,4},{4,0},{8,12},{12,8},{1,5},{5,1},{9,13},{13,9},{2,6},{6,2},{1... | collective-permute-start | bytes 147464 | tf_op jit(solution)/shard_map/ppermute | solution.py:778
  18.2 4.4 %collective-permute-start.6 = (f32[3,4,8,128]{3,2,1,0:T(8,128)S(1)}, f32[3,4,8,128]{3,2,1,0:T(8,128)S(1)}, u32[]{:S(2)}, u32[]{:S(2)}) collective-permute-start(f32[3,4,8,128]{3,2,1,0:T(8,128)S(1)} %get-tuple-element.30), channel_id=1, source_target_pairs={{0,2},{1,3},{2,0},{3,1},{4,6},{5,7},{6,4},{7,5},{8,10},{9,11},{10,... | collective-permute-start | bytes 147464 | tf_op jit(solution)/shard_map/ppermute | solution.py:778
  19.7 5.3 %collective-permute-start.11 = (f32[3,4,8,128]{3,2,1,0:T(8,128)S(1)}, f32[3,4,8,128]{3,2,1,0:T(8,128)S(1)}, u32[]{:S(2)}, u32[]{:S(2)}) collective-permute-start(f32[3,4,8,128]{3,2,1,0:T(8,128)S(1)} %get-tuple-element.30), channel_id=1, source_target_pairs={{0,6},{1,7},{2,4},{3,5},{4,2},{5,3},{6,0},{7,1},{8,14},{9,15},{10,... | collective-permute-start | bytes 147464 | tf_op jit(solution)/shard_map/ppermute | solution.py:801
  20.5 5.3 %collective-permute-start.10 = (f32[3,4,8,128]{3,2,1,0:T(8,128)S(1)}, f32[3,4,8,128]{3,2,1,0:T(8,128)S(1)}, u32[]{:S(2)}, u32[]{:S(2)}) collective-permute-start(f32[3,4,8,128]{3,2,1,0:T(8,128)S(1)} %collective-permute-done.9), channel_id=1, source_target_pairs={{0,2},{1,3},{2,0},{3,1},{4,6},{5,7},{6,4},{7,5},{8,10},{9,11},{10,... | collective-permute-start | bytes 147464 | tf_op jit(solution)/shard_map/ppermute | solution.py:778
  22.7 5.5 %collective-permute-start.13 = (f32[5,3,4,8,128]{4,3,2,1,0:T(8,128)S(1)}, f32[5,3,4,8,128]{4,3,2,1,0:T(8,128)S(1)}, u32[]{:S(2)}, u32[]{:S(2)}) collective-permute-start(f32[5,3,4,8,128]{4,3,2,1,0:T(8,128)S(1)} %bitcast_dynamic-update-slice_fusion.first), channel_id=1, source_target_pairs={{0,1},{1,0},{2,3},{3,2},{4,5},{5,4},{6,7},{7,6},{8,9},{9,8},{10,11... | collective-permute-start | bytes 737288 | tf_op jit(solution)/shard_map/ppermute | solution.py:778
  22.8 4.1 %collective-permute-start.12 = (f32[3,4,8,128]{3,2,1,0:T(8,128)S(1)}, f32[3,4,8,128]{3,2,1,0:T(8,128)S(1)}, u32[]{:S(2)}, u32[]{:S(2)}) collective-permute-start(f32[3,4,8,128]{3,2,1,0:T(8,128)S(1)} %collective-permute-done.8), channel_id=1, source_target_pairs={{0,2},{1,3},{2,0},{3,1},{4,6},{5,7},{6,4},{7,5},{8,10},{9,11},{10,... | collective-permute-start | bytes 147464 | tf_op jit(solution)/shard_map/ppermute | solution.py:778
  25.9 2.3 %collective-permute-start.14 = (f32[2,3,4,8,128]{4,3,2,1,0:T(8,128)S(1)}, f32[2,3,4,8,128]{4,3,2,1,0:T(8,128)S(1)}, u32[]{:S(2)}, u32[]{:S(2)}) collective-permute-start(f32[2,3,4,8,128]{4,3,2,1,0:T(8,128)S(1)} %pad_maximum_fusion.1.second), channel_id=1, source_target_pairs={{0,1},{1,0},{2,3},{3,2},{4,5},{5,4},{6,7},{7,6},{8,9},{9,8},{10,11... | collective-permute-start | bytes 294920 | tf_op jit(solution)/shard_map/ppermute | solution.py:778
  26.9 1.2 %collective-permute-start.15 = (f32[1,3,4,8,128]{4,3,2,1,0:T(8,128)S(1)}, f32[1,3,4,8,128]{4,3,2,1,0:T(8,128)S(1)}, u32[]{:S(2)}, u32[]{:S(2)}) collective-permute-start(f32[1,3,4,8,128]{4,3,2,1,0:T(8,128)S(1)} %bitcast.17), channel_id=1, source_target_pairs={{0,1},{1,0},{2,3},{3,2},{4,5},{5,4},{6,7},{7,6},{8,9},{9,8},{10,11... | collective-permute-start | bytes 147464 | tf_op jit(solution)/shard_map/ppermute | solution.py:778

commit v10 on v9

--- a/solution.py
+++ b/solution.py
@@ -744,16 +744,21 @@
                 put_window((target,), wide)(fine, source[fine] + both)
     fine = fine_level(weights)
     right_side = (right_conc,)
-    fine.sweep(
-        (fine_a0, fine_a1), right_side, HALO - 1, rows + 2, rows + 2, wide,
-        put_window((fine_b0, fine_b1), wide),
-    )
+    half = rows // 2
+    for start in (HALO - 1, HALO + half):
+        stage(
+            fine.sweep, (fine_a0, fine_a1), right_side, start, half + 1, half + 1, wide,
+            put_window((fine_b0, fine_b1), wide),
+        )
 
     def put_new(row, conc_value, chem_value):
         conc_new[row - HALO] = conc_value
         chem_new[row - HALO] = chem_value
 
-    fine.sweep((fine_b0, fine_b1), right_side, HALO, rows, rows, (PAD, columns), put_new)
+    for start in (HALO, HALO + half):
+        stage(
+            fine.sweep, (fine_b0, fine_b1), right_side, start, half, half, (PAD, columns), put_new
+        )
 
 
 def call_kernel(kernel, outs, scratch, *args, vmem_mib=8):

time: 32.9 us -> 32.9 us (level)
  no operation moved by 1% of the time
where the time goes in v10:
time: 32.9 us; the launch traced here: 32.8 us
  starting transfers between devices  18.5 us (56%)
  waiting for transfers between devices  6.39 us (19%)
  Pallas kernels  6.15 us (19%)
  other arithmetic  0.99 us (3%)
  between operations  0.71 us (2%)
    ppermute x9, starting transfers between devices, swapped(): return lax.ppermute(values, axis, [(i, i ^ mask) for i in range(count)])  8.98 us
    ppermute x6, starting transfers between devices, shifted(): lax.ppermute(values, axis, [(i, (i + by) % count) for i in range(count)])  8.7 us
    pallas_call x5, Pallas kernels, call_kernel(): pl.pallas_call(kernel, out_shape=shapes, in_specs=[whole_block()] * len(a...  6.15 us
    ppermute x9, waiting for transfers between devices, swapped(): return lax.ppermute(values, axis, [(i, i ^ mask) for i in range(count)])  3.44 us
    ppermute x6, waiting for transfers between devices, shifted(): lax.ppermute(values, axis, [(i, (i + by) % count) for i in range(count)])  1.89 us
    ppermute x1, waiting for transfers between devices, swapped_both(): return lax.ppermute(values, ('gx', 'gy'), pairs)  1.06 us
    concatenate x1, other arithmetic, two_phase_solve(): fields = jnp.concatenate([conc, chem], axis=0).reshape((2,) + block)  0.99 us
    ppermute x1, starting transfers between devices, swapped_both(): return lax.ppermute(values, ('gx', 'gy'), pairs)  0.85 us
  transfers between devices with their start and end apart: 16, of which 8 were waited for; matrix products, arithmetic and copies ran while one was open for 0% of the time, Pallas kernels for 3%

profile of v10, /device:TPU:0, one launch (start us, length us, event | category | flops | bytes accessed | tf_op | source)
XLA Modules:
  0.0 32.8 jit_solution(8218056008643317033)
XLA Ops:
  0.6 1.0 %pad_maximum_fusion = f32[32,16,128]{2,1,0:T(8,128)S(1)} fusion(f32[16,16,128]{2,1,0:T(8,128)} %param.3, f32[16,16,128]{2,1,0:T(8,128)} %param.2), kind=kLoop, calls=%fused_computation | loop fusion | flops 65536 | bytes 524288 | tf_op jit(solution)/shard_map/concatenate | solution.py:828
  1.6 3.1 %collective-permute-start = (f32[2,4,16,128]{3,2,1,0:T(8,128)S(1)}, f32[2,4,16,128]{3,2,1,0:T(8,128)S(1)}, u32[]{:S(2)}, u32[]{:S(2)}) collective-permute-start(f32[2,4,16,128]{3,2,1,0:T(8,128)S(1)} %get-tuple-element.18), channel_id=1, source_target_pairs={{0,4},{4,8},{8,12},{12,0},{1,5},{5,9},{9,13},{13,1},{2,6},{6,10},{... | collective-permute-start | bytes 196616 | tf_op jit(solution)/shard_map/ppermute | solution.py:778
  4.7 2.1 %collective-permute-start.1 = (f32[2,4,16,128]{3,2,1,0:T(8,128)S(1)}, f32[2,4,16,128]{3,2,1,0:T(8,128)S(1)}, u32[]{:S(2)}, u32[]{:S(2)}) collective-permute-start(f32[2,4,16,128]{3,2,1,0:T(8,128)S(1)} %get-tuple-element.19), channel_id=1, source_target_pairs={{0,12},{4,0},{8,4},{12,8},{1,13},{5,1},{9,5},{13,9},{2,14},{6,2},{... | collective-permute-start | bytes 196616 | tf_op jit(solution)/shard_map/ppermute | solution.py:778
  6.8 0.0 collective-permute-start.2
  6.8 1.7 %collective-permute-start.3 = (f32[16,8,128]{2,1,0:T(8,128)S(1)}, f32[16,8,128]{2,1,0:T(8,128)S(1)}, u32[]{:S(2)}, u32[]{:S(2)}) collective-permute-start(f32[16,8,128]{2,1,0:T(8,128)S(1)} %get-tuple-element.21), channel_id=1, source_target_pairs={{0,3},{1,0},{2,1},{3,2},{4,7},{5,4},{6,5},{7,6},{8,11},{9,8},{10,9... | collective-permute-start | bytes 196616 | tf_op jit(solution)/shard_map/ppermute | solution.py:778
  8.6 0.6 %collective-permute-done.before = f32[2,4,16,128]{3,2,1,0:T(8,128)S(1)} collective-permute-done((f32[2,4,16,128]{3,2,1,0:T(8,128)S(1)}, f32[2,4,16,128]{3,2,1,0:T(8,128)S(1)}, u32[]{:S(2)}, u32[]{:S(2)}) %collective-permute-start) | collective-permute-done | bytes 65568 | tf_op jit(solution)/shard_map/ppermute | solution.py:778
  9.1 0.5 %collective-permute-done.1.after = f32[2,4,16,128]{3,2,1,0:T(8,128)S(1)} collective-permute-done((f32[2,4,16,128]{3,2,1,0:T(8,128)S(1)}, f32[2,4,16,128]{3,2,1,0:T(8,128)S(1)}, u32[]{:S(2)}, u32[]{:S(2)}) %collective-permute-start.1) | collective-permute-done | bytes 65568 | tf_op jit(solution)/shard_map/ppermute | solution.py:778
  9.7 0.1 collective-permute-start.4
  9.8 1.7 %collective-permute-start.5 = (f32[8,8,128]{2,1,0:T(8,128)S(1)}, f32[8,8,128]{2,1,0:T(8,128)S(1)}, u32[]{:S(2)}, u32[]{:S(2)}) collective-permute-start(f32[8,8,128]{2,1,0:T(8,128)S(1)} %get-tuple-element.23), channel_id=1, source_target_pairs={{0,3},{1,0},{2,1},{3,2},{4,7},{5,4},{6,5},{7,6},{8,11},{9,8},{10,9... | collective-permute-start | bytes 98312 | tf_op jit(solution)/shard_map/ppermute | solution.py:778
  11.5 0.0 collective-permute-done.2.own_left
  11.5 0.0 collective-permute-done.3.own_right
  11.5 0.8 %shard_map.43 = (f32[3,4,8,128]{3,2,1,0:T(8,128)S(1)}, f32[2,12,24,128]{3,2,1,0:T(8,128)S(1)}, f32[16,32,128]{2,1,0:T(8,128)S(1)}, f32[7,14,24,128]{3,2,1,0:T(8,128)S(1)}, f32[2,4,32,128]{3,2,1,0:T(8,128)S(1)}) custom-call(f32[2,16,16,128]{3,2,1,0:T(8,128)S(1)} %bitcast.15, f32[16,8,128]{2,1,0:T(8,128)S(1)} %collective-permute-done.2.own_left, ...), custom_call_target="tpu_custom_call" | custom-call | tf_op jit(solution)/shard_map/pallas_call | solution.py:766
  12.3 0.7 %collective-permute-done.4.corner_left = f32[8,8,128]{2,1,0:T(8,128)S(1)} collective-permute-done((f32[8,8,128]{2,1,0:T(8,128)S(1)}, f32[8,8,128]{2,1,0:T(8,128)S(1)}, u32[]{:S(2)}, u32[]{:S(2)}) %collective-permute-start.4) | collective-permute-done | bytes 32800 | tf_op jit(solution)/shard_map/ppermute | solution.py:778
  13.1 0.0 collective-permute-done.5.corner_right
  13.1 0.7 %shard_map.44 = (f32[3,4,8,128]{3,2,1,0:T(8,128)S(1)}, f32[2,8,24,128]{3,2,1,0:T(8,128)S(1)}, f32[2,32,128]{2,1,0:T(8,128)S(1)}, f32[7,5,24,128]{3,2,1,0:T(8,128)S(1)}) custom-call(f32[2,16,16,128]{3,2,1,0:T(8,128)S(1)} %bitcast.16, f32[2,4,16,128]{3,2,1,0:T(8,128)S(1)} %collective-permute-done.before, f32[2,4,16,128]{3,2,1,0:T(8,128)S(1)} %collective-permute-done.1.after, ...), custom_call_target="tpu_custom_call" | custom-call | tf_op jit(solution)/shard_map/pallas_call | solution.py:766
  13.8 3.2 %collective-permute-start.9 = (f32[3,4,8,128]{3,2,1,0:T(8,128)S(1)}, f32[3,4,8,128]{3,2,1,0:T(8,128)S(1)}, u32[]{:S(2)}, u32[]{:S(2)}) collective-permute-start(f32[3,4,8,128]{3,2,1,0:T(8,128)S(1)} %get-tuple-element.30), channel_id=1, source_target_pairs={{0,12},{4,8},{8,4},{12,0},{1,13},{5,9},{9,5},{13,1},{2,14},{6,10},... | collective-permute-start | bytes 147464 | tf_op jit(solution)/shard_map/ppermute | solution.py:783
  17.0 0.0 collective-permute-start.8
  17.0 1.2 %collective-permute-start.7 = (f32[3,4,8,128]{3,2,1,0:T(8,128)S(1)}, f32[3,4,8,128]{3,2,1,0:T(8,128)S(1)}, u32[]{:S(2)}, u32[]{:S(2)}) collective-permute-start(f32[3,4,8,128]{3,2,1,0:T(8,128)S(1)} %get-tuple-element.30), channel_id=1, source_target_pairs={{0,4},{4,0},{8,12},{12,8},{1,5},{5,1},{9,13},{13,9},{2,6},{6,2},{1... | collective-permute-start | bytes 147464 | tf_op jit(solution)/shard_map/ppermute | solution.py:783
  18.2 1.5 %collective-permute-start.6 = (f32[3,4,8,128]{3,2,1,0:T(8,128)S(1)}, f32[3,4,8,128]{3,2,1,0:T(8,128)S(1)}, u32[]{:S(2)}, u32[]{:S(2)}) collective-permute-start(f32[3,4,8,128]{3,2,1,0:T(8,128)S(1)} %get-tuple-element.30), channel_id=1, source_target_pairs={{0,2},{1,3},{2,0},{3,1},{4,6},{5,7},{6,4},{7,5},{8,10},{9,11},{10,... | collective-permute-start | bytes 147464 | tf_op jit(solution)/shard_map/ppermute | solution.py:783
  19.7 0.0 collective-permute-done.9
  19.7 0.8 %collective-permute-start.11 = (f32[3,4,8,128]{3,2,1,0:T(8,128)S(1)}, f32[3,4,8,128]{3,2,1,0:T(8,128)S(1)}, u32[]{:S(2)}, u32[]{:S(2)}) collective-permute-start(f32[3,4,8,128]{3,2,1,0:T(8,128)S(1)} %get-tuple-element.30), channel_id=1, source_target_pairs={{0,6},{1,7},{2,4},{3,5},{4,2},{5,3},{6,0},{7,1},{8,14},{9,15},{10,... | collective-permute-start | bytes 147464 | tf_op jit(solution)/shard_map/ppermute | solution.py:806
  20.5 1.6 %collective-permute-start.10 = (f32[3,4,8,128]{3,2,1,0:T(8,128)S(1)}, f32[3,4,8,128]{3,2,1,0:T(8,128)S(1)}, u32[]{:S(2)}, u32[]{:S(2)}) collective-permute-start(f32[3,4,8,128]{3,2,1,0:T(8,128)S(1)} %collective-permute-done.9), channel_id=1, source_target_pairs={{0,2},{1,3},{2,0},{3,1},{4,6},{5,7},{6,4},{7,5},{8,10},{9,11},{10,... | collective-permute-start | bytes 147464 | tf_op jit(solution)/shard_map/ppermute | solution.py:783
  22.2 0.4 %collective-permute-done.6 = f32[3,4,8,128]{3,2,1,0:T(8,128)S(1)} collective-permute-done((f32[3,4,8,128]{3,2,1,0:T(8,128)S(1)}, f32[3,4,8,128]{3,2,1,0:T(8,128)S(1)}, u32[]{:S(2)}, u32[]{:S(2)}) %collective-permute-start.6) | collective-permute-done | bytes 49184 | tf_op jit(solution)/shard_map/ppermute | solution.py:783
  22.6 0.0 collective-permute-done.7
  22.6 0.0 collective-permute-done.8
  22.7 0.2 collective-permute-start.13
  22.8 1.2 %collective-permute-start.12 = (f32[3,4,8,128]{3,2,1,0:T(8,128)S(1)}, f32[3,4,8,128]{3,2,1,0:T(8,128)S(1)}, u32[]{:S(2)}, u32[]{:S(2)}) collective-permute-start(f32[3,4,8,128]{3,2,1,0:T(8,128)S(1)} %collective-permute-done.8), channel_id=1, source_target_pairs={{0,2},{1,3},{2,0},{3,1},{4,6},{5,7},{6,4},{7,5},{8,10},{9,11},{10,... | collective-permute-start | bytes 147464 | tf_op jit(solution)/shard_map/ppermute | solution.py:783
  24.0 1.1 %collective-permute-done.11 = f32[3,4,8,128]{3,2,1,0:T(8,128)S(1)} collective-permute-done((f32[3,4,8,128]{3,2,1,0:T(8,128)S(1)}, f32[3,4,8,128]{3,2,1,0:T(8,128)S(1)}, u32[]{:S(2)}, u32[]{:S(2)}) %collective-permute-start.11) | collective-permute-done | bytes 49184 | tf_op jit(solution)/shard_map/ppermute | solution.py:806
  25.0 0.8 %collective-permute-done.10 = f32[3,4,8,128]{3,2,1,0:T(8,128)S(1)} collective-permute-done((f32[3,4,8,128]{3,2,1,0:T(8,128)S(1)}, f32[3,4,8,128]{3,2,1,0:T(8,128)S(1)}, u32[]{:S(2)}, u32[]{:S(2)}) %collective-permute-start.10) | collective-permute-done | bytes 49184 | tf_op jit(solution)/shard_map/ppermute | solution.py:783
  25.9 0.1 collective-permute-start.14
  26.0 1.0 %collective-permute-done.12 = f32[3,4,8,128]{3,2,1,0:T(8,128)S(1)} collective-permute-done((f32[3,4,8,128]{3,2,1,0:T(8,128)S(1)}, f32[3,4,8,128]{3,2,1,0:T(8,128)S(1)}, u32[]{:S(2)}, u32[]{:S(2)}) %collective-permute-start.12) | collective-permute-done | bytes 49184 | tf_op jit(solution)/shard_map/ppermute | solution.py:783
  26.9 0.0 collective-permute-start.15
  26.9 1.2 %collective-permute-done.15.third_far = f32[1,3,4,8,128]{4,3,2,1,0:T(8,128)S(1)} collective-permute-done((f32[1,3,4,8,128]{4,3,2,1,0:T(8,128)S(1)}, f32[1,3,4,8,128]{4,3,2,1,0:T(8,128)S(1)}, u32[]{:S(2)}, u32[]{:S(2)}) %collective-permute-start.15) | collective-permute-done | bytes 49184 | tf_op jit(solution)/shard_map/ppermute | solution.py:783
  28.2 0.0 collective-permute-done.14.second_far
  28.2 0.0 collective-permute-done.13.first_far
  28.2 4.6 %shard_map.45 = (f32[16,16,128]{2,1,0:T(8,128)}, f32[16,16,128]{2,1,0:T(8,128)}) custom-call(f32[5,3,4,8,128]{4,3,2,1,0:T(8,128)S(1)} %bitcast_dynamic-update-slice_fusion.first, f32[2,3,4,8,128]{4,3,2,1,0:T(8,128)S(1)} %pad_maximum_fusion.1.second, f32[1,3,4,8,128]{4,3,2,1,0:T(8,128)S(1)} %bitcast.18, ...), custom_call_target="tpu_custom_call" | custom-call | tf_op jit(solution)/shard_map/pallas_call | solution.py:766
  (8 shorter events, 0.1 us)
Async XLA Ops:
  1.6 7.5 %collective-permute-start = (f32[2,4,16,128]{3,2,1,0:T(8,128)S(1)}, f32[2,4,16,128]{3,2,1,0:T(8,128)S(1)}, u32[]{:S(2)}, u32[]{:S(2)}) collective-permute-start(f32[2,4,16,128]{3,2,1,0:T(8,128)S(1)} %get-tuple-element.18), channel_id=1, source_target_pairs={{0,4},{4,8},{8,12},{12,0},{1,5},{5,9},{9,13},{13,1},{2,6},{6,10},{... | collective-permute-start | bytes 196616 | tf_op jit(solution)/shard_map/ppermute | solution.py:778
  4.7 5.0 %collective-permute-start.1 = (f32[2,4,16,128]{3,2,1,0:T(8,128)S(1)}, f32[2,4,16,128]{3,2,1,0:T(8,128)S(1)}, u32[]{:S(2)}, u32[]{:S(2)}) collective-permute-start(f32[2,4,16,128]{3,2,1,0:T(8,128)S(1)} %get-tuple-element.19), channel_id=1, source_target_pairs={{0,12},{4,0},{8,4},{12,8},{1,13},{5,1},{9,5},{13,9},{2,14},{6,2},{... | collective-permute-start | bytes 196616 | tf_op jit(solution)/shard_map/ppermute | solution.py:778
  6.8 4.7 %collective-permute-start.2 = (f32[16,8,128]{2,1,0:T(8,128)S(1)}, f32[16,8,128]{2,1,0:T(8,128)S(1)}, u32[]{:S(2)}, u32[]{:S(2)}) collective-permute-start(f32[16,8,128]{2,1,0:T(8,128)S(1)} %get-tuple-element.20), channel_id=1, source_target_pairs={{0,1},{1,2},{2,3},{3,0},{4,5},{5,6},{6,7},{7,4},{8,9},{9,10},{10,1... | collective-permute-start | bytes 196616 | tf_op jit(solution)/shard_map/ppermute | solution.py:778
  6.8 4.7 %collective-permute-start.3 = (f32[16,8,128]{2,1,0:T(8,128)S(1)}, f32[16,8,128]{2,1,0:T(8,128)S(1)}, u32[]{:S(2)}, u32[]{:S(2)}) collective-permute-start(f32[16,8,128]{2,1,0:T(8,128)S(1)} %get-tuple-element.21), channel_id=1, source_target_pairs={{0,3},{1,0},{2,1},{3,2},{4,7},{5,4},{6,5},{7,6},{8,11},{9,8},{10,9... | collective-permute-start | bytes 196616 | tf_op jit(solution)/shard_map/ppermute | solution.py:778
  9.7 3.4 %collective-permute-start.4 = (f32[8,8,128]{2,1,0:T(8,128)S(1)}, f32[8,8,128]{2,1,0:T(8,128)S(1)}, u32[]{:S(2)}, u32[]{:S(2)}) collective-permute-start(f32[8,8,128]{2,1,0:T(8,128)S(1)} %get-tuple-element.22), channel_id=1, source_target_pairs={{0,1},{1,2},{2,3},{3,0},{4,5},{5,6},{6,7},{7,4},{8,9},{9,10},{10,1... | collective-permute-start | bytes 98312 | tf_op jit(solution)/shard_map/ppermute | solution.py:778
  9.8 3.3 %collective-permute-start.5 = (f32[8,8,128]{2,1,0:T(8,128)S(1)}, f32[8,8,128]{2,1,0:T(8,128)S(1)}, u32[]{:S(2)}, u32[]{:S(2)}) collective-permute-start(f32[8,8,128]{2,1,0:T(8,128)S(1)} %get-tuple-element.23), channel_id=1, source_target_pairs={{0,3},{1,0},{2,1},{3,2},{4,7},{5,4},{6,5},{7,6},{8,11},{9,8},{10,9... | collective-permute-start | bytes 98312 | tf_op jit(solution)/shard_map/ppermute | solution.py:778
  13.8 5.9 %collective-permute-start.9 = (f32[3,4,8,128]{3,2,1,0:T(8,128)S(1)}, f32[3,4,8,128]{3,2,1,0:T(8,128)S(1)}, u32[]{:S(2)}, u32[]{:S(2)}) collective-permute-start(f32[3,4,8,128]{3,2,1,0:T(8,128)S(1)} %get-tuple-element.30), channel_id=1, source_target_pairs={{0,12},{4,8},{8,4},{12,0},{1,13},{5,9},{9,5},{13,1},{2,14},{6,10},... | collective-permute-start | bytes 147464 | tf_op jit(solution)/shard_map/ppermute | solution.py:783
  17.0 5.6 %collective-permute-start.8 = (f32[3,4,8,128]{3,2,1,0:T(8,128)S(1)}, f32[3,4,8,128]{3,2,1,0:T(8,128)S(1)}, u32[]{:S(2)}, u32[]{:S(2)}) collective-permute-start(f32[3,4,8,128]{3,2,1,0:T(8,128)S(1)} %get-tuple-element.30), channel_id=1, source_target_pairs={{0,8},{4,12},{8,0},{12,4},{1,9},{5,13},{9,1},{13,5},{2,10},{6,14},... | collective-permute-start | bytes 147464 | tf_op jit(solution)/shard_map/ppermute | solution.py:783
  17.0 5.6 %collective-permute-start.7 = (f32[3,4,8,128]{3,2,1,0:T(8,128)S(1)}, f32[3,4,8,128]{3,2,1,0:T(8,128)S(1)}, u32[]{:S(2)}, u32[]{:S(2)}) collective-permute-start(f32[3,4,8,128]{3,2,1,0:T(8,128)S(1)} %get-tuple-element.30), channel_id=1, source_target_pairs={{0,4},{4,0},{8,12},{12,8},{1,5},{5,1},{9,13},{13,9},{2,6},{6,2},{1... | collective-permute-start | bytes 147464 | tf_op jit(solution)/shard_map/ppermute | solution.py:783
  18.2 4.4 %collective-permute-start.6 = (f32[3,4,8,128]{3,2,1,0:T(8,128)S(1)}, f32[3,4,8,128]{3,2,1,0:T(8,128)S(1)}, u32[]{:S(2)}, u32[]{:S(2)}) collective-permute-start(f32[3,4,8,128]{3,2,1,0:T(8,128)S(1)} %get-tuple-element.30), channel_id=1, source_target_pairs={{0,2},{1,3},{2,0},{3,1},{4,6},{5,7},{6,4},{7,5},{8,10},{9,11},{10,... | collective-permute-start | bytes 147464 | tf_op jit(solution)/shard_map/ppermute | solution.py:783
  19.7 5.3 %collective-permute-start.11 = (f32[3,4,8,128]{3,2,1,0:T(8,128)S(1)}, f32[3,4,8,128]{3,2,1,0:T(8,128)S(1)}, u32[]{:S(2)}, u32[]{:S(2)}) collective-permute-start(f32[3,4,8,128]{3,2,1,0:T(8,128)S(1)} %get-tuple-element.30), channel_id=1, source_target_pairs={{0,6},{1,7},{2,4},{3,5},{4,2},{5,3},{6,0},{7,1},{8,14},{9,15},{10,... | collective-permute-start | bytes 147464 | tf_op jit(solution)/shard_map/ppermute | solution.py:806
  20.5 5.3 %collective-permute-start.10 = (f32[3,4,8,128]{3,2,1,0:T(8,128)S(1)}, f32[3,4,8,128]{3,2,1,0:T(8,128)S(1)}, u32[]{:S(2)}, u32[]{:S(2)}) collective-permute-start(f32[3,4,8,128]{3,2,1,0:T(8,128)S(1)} %collective-permute-done.9), channel_id=1, source_target_pairs={{0,2},{1,3},{2,0},{3,1},{4,6},{5,7},{6,4},{7,5},{8,10},{9,11},{10,... | collective-permute-start | bytes 147464 | tf_op jit(solution)/shard_map/ppermute | solution.py:783
  22.7 5.5 %collective-permute-start.13 = (f32[5,3,4,8,128]{4,3,2,1,0:T(8,128)S(1)}, f32[5,3,4,8,128]{4,3,2,1,0:T(8,128)S(1)}, u32[]{:S(2)}, u32[]{:S(2)}) collective-permute-start(f32[5,3,4,8,128]{4,3,2,1,0:T(8,128)S(1)} %bitcast_dynamic-update-slice_fusion.first), channel_id=1, source_target_pairs={{0,1},{1,0},{2,3},{3,2},{4,5},{5,4},{6,7},{7,6},{8,9},{9,8},{10,11... | collective-permute-start | bytes 737288 | tf_op jit(solution)/shard_map/ppermute | solution.py:783
  22.8 4.1 %collective-permute-start.12 = (f32[3,4,8,128]{3,2,1,0:T(8,128)S(1)}, f32[3,4,8,128]{3,2,1,0:T(8,128)S(1)}, u32[]{:S(2)}, u32[]{:S(2)}) collective-permute-start(f32[3,4,8,128]{3,2,1,0:T(8,128)S(1)} %collective-permute-done.8), channel_id=1, source_target_pairs={{0,2},{1,3},{2,0},{3,1},{4,6},{5,7},{6,4},{7,5},{8,10},{9,11},{10,... | collective-permute-start | bytes 147464 | tf_op jit(solution)/shard_map/ppermute | solution.py:783
  25.9 2.3 %collective-permute-start.14 = (f32[2,3,4,8,128]{4,3,2,1,0:T(8,128)S(1)}, f32[2,3,4,8,128]{4,3,2,1,0:T(8,128)S(1)}, u32[]{:S(2)}, u32[]{:S(2)}) collective-permute-start(f32[2,3,4,8,128]{4,3,2,1,0:T(8,128)S(1)} %pad_maximum_fusion.1.second), channel_id=1, source_target_pairs={{0,1},{1,0},{2,3},{3,2},{4,5},{5,4},{6,7},{7,6},{8,9},{9,8},{10,11... | collective-permute-start | bytes 294920 | tf_op jit(solution)/shard_map/ppermute | solution.py:783
  26.9 1.2 %collective-permute-start.15 = (f32[1,3,4,8,128]{4,3,2,1,0:T(8,128)S(1)}, f32[1,3,4,8,128]{4,3,2,1,0:T(8,128)S(1)}, u32[]{:S(2)}, u32[]{:S(2)}) collective-permute-start(f32[1,3,4,8,128]{4,3,2,1,0:T(8,128)S(1)} %bitcast.17), channel_id=1, source_target_pairs={{0,1},{1,0},{2,3},{3,2},{4,5},{5,4},{6,7},{7,6},{8,9},{9,8},{10,11... | collective-permute-start | bytes 147464 | tf_op jit(solution)/shard_map/ppermute | solution.py:783
